TPU v7x, 128 devices: a whole 4x4x4 slice. The times are simulated.
128 devices in a mesh: frame: 32 (over x, y, core), head: 4 (over z).
Axes of the slice: x: 4, y: 4, z: 4, core: 2. Of those that a mesh axis runs over, the one named last changes fastest.
Arguments:
- query_raw: bfloat16 [4096, 2560], P('frame', 'head'), may hold values from -20 to 20
- key_raw: bfloat16 [4096, 2560], P('frame', 'head'), may hold values from -20 to 20
- values: bfloat16 [4096, 2560], P('frame', 'head'), may hold values from -6 to 6
- query_gain: float32 [2560], P('head'), may hold values from 0.5 to 2
- key_gain: float32 [2560], P('head'), may hold values from 0.5 to 2
- out_grad: bfloat16 [4096, 2560], P('frame', 'head'), may hold values from -128 to 128
- window_offset: int32 [7], replicated, may hold values from 0 to 3
Outputs:
- query_raw_grad: bfloat16 [4096, 2560], P('frame', 'head')
- key_raw_grad: bfloat16 [4096, 2560], P('frame', 'head')
- value_grad: bfloat16 [4096, 2560], P('frame', 'head')
All inputs are finite; a program needn't handle non-finite values.
Results may differ from a plain program's by a relative error of at most 0.0065.
The roundings to bfloat16 on the way count: a program that leaves them out, or rounds other values in their place, can miss the bound.
Values may be sent and summed in bfloat16 or wider, within the bound.
A program may use at most 64 MiB of HBM per device.

v0:
```python
import jax
import jax.numpy as jnp
from jax import lax
from jax.sharding import PartitionSpec as P

HEADS = 20
HD = 128
NB = 4
BANDS = 7
TOK_FRAME = 128
BLK = 32


EPSILON = 1e-06
MASKED_SCORE = -1e30
BLOCK_LIMIT = 512


def window_mask(query_rows, key_rows, window_offset):
    query_frame = query_rows // TOK_FRAME
    key_frame = key_rows // TOK_FRAME
    query_block = query_rows % TOK_FRAME // BLK
    key_block = key_rows % TOK_FRAME // BLK
    distance = jnp.abs(query_frame[:, None] - key_frame[None, :])
    band_level = jnp.zeros(distance.shape, jnp.int32)
    for exponent in range(1, BANDS + 1):
        band_level = band_level + (distance >= 2**exponent).astype(jnp.int32)
    offset = jnp.zeros(distance.shape, jnp.int32)
    for band_index in range(BANDS):
        offset = offset + jnp.where(band_level == band_index + 1, window_offset[band_index], 0)
    window_width = jnp.maximum(1, jnp.right_shift(jnp.int32(NB), band_level))
    relative = (key_block[None, :] - query_block[:, None] - offset) % NB
    return (band_level == 0) | (relative < window_width)


def blockwise(block_fn):

    def run_blocks(running, incoming, first_row):
        count_rows = incoming[0].shape[0]
        stride = count_rows
        while stride > BLOCK_LIMIT and stride % 2 == 0:
            stride = stride // 2

        def one_block(block_index, partial_state):
            sliced = tuple(
                (
                    lax.dynamic_slice_in_dim(member, block_index * stride, stride, 0)
                    for member in incoming
                )
            )
            return block_fn(partial_state, sliced, block_index * stride)

        return lax.fori_loop(0, count_rows // stride, one_block, running)

    return run_blocks


def fold_keys(keys, values, block_fn, start_state):
    return block_fn(
        start_state,
        (
            lax.all_gather(keys, "frame", axis=0, tiled=True),
            lax.all_gather(values, "frame", axis=0, tiled=True),
        ),
        jnp.int32(0),
    )


def local(query_raw, key_raw, values, query_gain, key_gain, out_grad, window_offset):
    local_rows, features = query_raw.shape
    head_count = features // HD
    score_scale = HD ** (-0.5)
    channels = HEADS * HD
    query_float = query_raw.astype(jnp.float32)
    key_float = key_raw.astype(jnp.float32)
    query_square, key_square = lax.psum(
        (jnp.sum(query_float * query_float, axis=-1), jnp.sum(key_float * key_float, axis=-1)),
        "head",
    )
    query_rms = lax.rsqrt(query_square / channels + EPSILON)[:, None]
    key_rms = lax.rsqrt(key_square / channels + EPSILON)[:, None]
    queries = (query_float * query_rms * query_gain).astype(jnp.bfloat16)
    keys = (key_float * key_rms * key_gain).astype(jnp.bfloat16)
    query_heads = queries.reshape(local_rows, head_count, HD)
    key_heads = keys.reshape(local_rows, head_count, HD)
    value_heads = values.reshape(local_rows, head_count, HD)
    grad_heads = out_grad.reshape(local_rows, head_count, HD)
    own_rows = lax.axis_index("frame") * local_rows + jnp.arange(local_rows, dtype=jnp.int32)

    def block_scores(other_keys, other_values, first_row):
        count_rows = other_keys.shape[0]
        key_part = other_keys.reshape(count_rows, head_count, HD)
        value_part = other_values.reshape(count_rows, head_count, HD)
        scores = (
            jnp.einsum("qhd,khd->hqk", query_heads, key_part, preferred_element_type=jnp.float32)
            * score_scale
        )
        grad_probs = jnp.einsum(
            "qhd,khd->hqk", grad_heads, value_part, preferred_element_type=jnp.float32
        )
        allowed = window_mask(
            own_rows, first_row + jnp.arange(count_rows, dtype=jnp.int32), window_offset
        )[None]
        return (key_part, scores, grad_probs, allowed)

    def first_block(partial_state, sliced, first_row):
        row_peak, row_total, weighted = partial_state[:3]
        key_part, scores, grad_probs, allowed = block_scores(sliced[0], sliced[1], first_row)
        new_peak = jnp.maximum(row_peak, jnp.max(jnp.where(allowed, scores, MASKED_SCORE), axis=-1))
        rescale = jnp.exp(row_peak - new_peak)
        weights = jnp.where(allowed, jnp.exp(scores - new_peak[..., None]), 0.0)
        row_total = row_total * rescale + jnp.sum(weights, axis=-1)
        weighted = weighted * rescale + jnp.sum(weights * grad_probs, axis=-1)
        return (new_peak, row_total, weighted)

    stats_shape = (head_count, local_rows)
    zero_heads = jnp.zeros((local_rows, head_count, HD), jnp.float32)
    start_state = (
        jnp.full(stats_shape, MASKED_SCORE, jnp.float32),
        jnp.zeros(stats_shape, jnp.float32),
        jnp.zeros(stats_shape, jnp.float32),
    )
    first_state = fold_keys(keys, values, blockwise(first_block), start_state)
    row_peak, row_total, weighted = first_state[:3]
    log_total = row_peak + jnp.log(row_total)
    delta = weighted / row_total
    all_log, all_delta = (
        lax.all_gather(log_total, "frame", axis=1, tiled=True),
        lax.all_gather(delta, "frame", axis=1, tiled=True),
    )

    def second_block(partial_state, sliced, first_row):
        key_acc, value_acc = partial_state
        count_rows = sliced[0].shape[0]
        query_part = sliced[0].reshape(count_rows, head_count, HD)
        grad_part = sliced[1].reshape(count_rows, head_count, HD)
        scores = (
            jnp.einsum("qhd,khd->hqk", query_part, key_heads, preferred_element_type=jnp.float32)
            * score_scale
        )
        grad_probs = jnp.einsum(
            "qhd,khd->hqk", grad_part, value_heads, preferred_element_type=jnp.float32
        )
        allowed = window_mask(
            first_row + jnp.arange(count_rows, dtype=jnp.int32), own_rows, window_offset
        )[None]
        log_part = lax.dynamic_slice_in_dim(all_log, first_row, count_rows, 1)
        delta_part = lax.dynamic_slice_in_dim(all_delta, first_row, count_rows, 1)
        probs = jnp.where(allowed, jnp.exp(scores - log_part[..., None]), 0.0)
        grad_scores = probs * (grad_probs - delta_part[..., None])
        value_acc = value_acc + jnp.einsum(
            "hqk,qhd->khd",
            probs.astype(jnp.bfloat16),
            grad_part,
            preferred_element_type=jnp.float32,
        )
        key_acc = key_acc + jnp.einsum(
            "hqk,qhd->khd",
            grad_scores.astype(jnp.bfloat16),
            query_part,
            preferred_element_type=jnp.float32,
        )
        return (key_acc, value_acc)

    key_acc, value_acc = blockwise(second_block)(
        (zero_heads, zero_heads),
        (
            lax.all_gather(queries, "frame", axis=0, tiled=True),
            lax.all_gather(out_grad, "frame", axis=0, tiled=True),
        ),
        jnp.int32(0),
    )

    def third_block(partial_state, sliced, first_row):
        key_part, scores, grad_probs, allowed = block_scores(sliced[0], sliced[1], first_row)
        probs = jnp.where(allowed, jnp.exp(scores - log_total[..., None]), 0.0)
        grad_scores = probs * (grad_probs - delta[..., None])
        return partial_state + jnp.einsum(
            "hqk,khd->qhd",
            grad_scores,
            key_part.astype(jnp.float32),
            precision=lax.Precision.HIGHEST,
        )

    query_grad = fold_keys(keys, values, blockwise(third_block), zero_heads) * score_scale
    query_grad_rows = query_grad.reshape(local_rows, features)
    key_grad_rows = key_acc.reshape(local_rows, features) * score_scale
    query_gained = query_gain * query_grad_rows
    key_gained = key_gain * key_grad_rows
    query_inner, key_inner = lax.psum(
        (jnp.sum(query_gained * query_float, axis=-1), jnp.sum(key_gained * key_float, axis=-1)),
        "head",
    )
    query_cubed = query_rms * query_rms * query_rms
    key_cubed = key_rms * key_rms * key_rms
    query_raw_grad = (
        query_rms * query_gained - query_cubed / channels * query_float * query_inner[:, None]
    ).astype(jnp.bfloat16)
    key_raw_grad = (
        key_rms * key_gained - key_cubed / channels * key_float * key_inner[:, None]
    ).astype(jnp.bfloat16)
    value_grad = value_acc.reshape(local_rows, features).astype(jnp.bfloat16)
    return (query_raw_grad, key_raw_grad, value_grad)


def solution(mesh):
    placed = (
        P("frame", "head"),
        P("frame", "head"),
        P("frame", "head"),
        P("head"),
        P("head"),
        P("frame", "head"),
        P(),
    )
    return jax.shard_map(
        local,
        mesh=mesh,
        in_specs=placed,
        out_specs=(P("frame", "head"), P("frame", "head"), P("frame", "head")),
        check_vma=False,
    )
```

profile of v0, /device:TPU:0, one launch (start us, length us, event | category | flops | bytes accessed | tf_op | source)
XLA Modules:
  0.0 435.7 jit_solution(14875314555634357682)
XLA Ops:
  9.7 11.9 %all-reduce.1 = (f32[128]{0:T(128)S(1)}, f32[128]{0:T(128)S(1)}) all-reduce(f32[128]{0:T(128)S(1)} %get-tuple-element.1622, f32[128]{0:T(128)S(1)} %get-tuple-element.1621), channel_id=1, replica_groups=mesh['frame'=32,'head'=4] {'head'}, use_global_device_ids=true, to_apply=%region_3.0 | all-reduce | flops 256 | bytes 2048 | tf_op jit(solution)/shard_map/psum | solution.py:76
  33.6 40.3 %all-gather.5.cloned.1.call-done = bf16[4096,640]{0,1:T(8,128)(2,1)} async-done(((bf16[128,640]{0,1:T(8,128)(2,1)}), bf16[4096,640]{0,1:T(8,128)(2,1)}) %all-gather.5.cloned.1.call-update) | async-done | bytes 5242896 | tf_op jit(solution)/shard_map/all_gather | solution.py:62
  73.9 52.7 %all-gather.7.cloned.1.call-done = bf16[4096,640]{0,1:T(8,128)(2,1)} async-done(((bf16[128,640]{0,1:T(8,128)(2,1)}), bf16[4096,640]{0,1:T(8,128)(2,1)}) %all-gather.7.cloned.1.call-update) | async-done | bytes 5242896 | tf_op jit(solution)/shard_map/all_gather | solution.py:63
  126.6 73.7 %while.66 = (s32[]{:T(128)}, f32[5,128]{1,0:T(8,128)S(1)}, f32[5,128]{1,0:T(8,128)S(1)}, f32[5,128]{1,0:T(8,128)S(1)}, s32[7]{0:T(128)S(1)}, /*index=5*/bf16[409...) while((s32[]{:T(128)}, f32[5,128]{1,0:T(8,128)S(1)}, ...), condition=%wide.region_8.9_spmd.clone.clone.clone, body=%wide.region_4.8_spmd.clone.clone.clone.sunk | while | flops 175008896 | bytes 8510758 | solution.py:53
  128.7 4.9 %fusion.180 = pred[128,512]{0,1:T(8,128)(4,1)S(1)} fusion(s32[]{:T(128)} %bitcast.168, s32[]{:T(128)} %bitcast.169, s32[]{:T(128)} %bitcast.170, s32[]{:T(128)} %bitcast.171, s32[]{:T(128)} %bitcast.172, s32[]{:T(128)} %bitcast.173, s32[]{:T(128)} %bitcast.174, s32[128]{0:T(128)S(1)} %get-tuple-element.1843, s32[512]{0:T(512)S(1)} %get-tuple-element.1844, ...), kind=kLoop, calls=%fused_computation.34.clone.1 | loop fusion | flops 3932160 | bytes 70684 | tf_op jit(solution)/shard_map/while/body/eval_jaxpr/or | solution.py:33
  137.9 5.0 %fusion.180 = pred[128,512]{0,1:T(8,128)(4,1)S(1)} fusion(s32[]{:T(128)} %bitcast.168, s32[]{:T(128)} %bitcast.169, s32[]{:T(128)} %bitcast.170, s32[]{:T(128)} %bitcast.171, s32[]{:T(128)} %bitcast.172, s32[]{:T(128)} %bitcast.173, s32[]{:T(128)} %bitcast.174, s32[128]{0:T(128)S(1)} %get-tuple-element.1843, s32[512]{0:T(512)S(1)} %get-tuple-element.1844, ...), kind=kLoop, calls=%fused_computation.34.clone.1 | loop fusion | flops 3932160 | bytes 70684 | tf_op jit(solution)/shard_map/while/body/eval_jaxpr/or | solution.py:33
  147.2 4.9 %fusion.180 = pred[128,512]{0,1:T(8,128)(4,1)S(1)} fusion(s32[]{:T(128)} %bitcast.168, s32[]{:T(128)} %bitcast.169, s32[]{:T(128)} %bitcast.170, s32[]{:T(128)} %bitcast.171, s32[]{:T(128)} %bitcast.172, s32[]{:T(128)} %bitcast.173, s32[]{:T(128)} %bitcast.174, s32[128]{0:T(128)S(1)} %get-tuple-element.1843, s32[512]{0:T(512)S(1)} %get-tuple-element.1844, ...), kind=kLoop, calls=%fused_computation.34.clone.1 | loop fusion | flops 3932160 | bytes 70684 | tf_op jit(solution)/shard_map/while/body/eval_jaxpr/or | solution.py:33
  156.4 4.9 %fusion.180 = pred[128,512]{0,1:T(8,128)(4,1)S(1)} fusion(s32[]{:T(128)} %bitcast.168, s32[]{:T(128)} %bitcast.169, s32[]{:T(128)} %bitcast.170, s32[]{:T(128)} %bitcast.171, s32[]{:T(128)} %bitcast.172, s32[]{:T(128)} %bitcast.173, s32[]{:T(128)} %bitcast.174, s32[128]{0:T(128)S(1)} %get-tuple-element.1843, s32[512]{0:T(512)S(1)} %get-tuple-element.1844, ...), kind=kLoop, calls=%fused_computation.34.clone.1 | loop fusion | flops 3932160 | bytes 70684 | tf_op jit(solution)/shard_map/while/body/eval_jaxpr/or | solution.py:33
  165.6 4.9 %fusion.180 = pred[128,512]{0,1:T(8,128)(4,1)S(1)} fusion(s32[]{:T(128)} %bitcast.168, s32[]{:T(128)} %bitcast.169, s32[]{:T(128)} %bitcast.170, s32[]{:T(128)} %bitcast.171, s32[]{:T(128)} %bitcast.172, s32[]{:T(128)} %bitcast.173, s32[]{:T(128)} %bitcast.174, s32[128]{0:T(128)S(1)} %get-tuple-element.1843, s32[512]{0:T(512)S(1)} %get-tuple-element.1844, ...), kind=kLoop, calls=%fused_computation.34.clone.1 | loop fusion | flops 3932160 | bytes 70684 | tf_op jit(solution)/shard_map/while/body/eval_jaxpr/or | solution.py:33
  174.8 5.0 %fusion.180 = pred[128,512]{0,1:T(8,128)(4,1)S(1)} fusion(s32[]{:T(128)} %bitcast.168, s32[]{:T(128)} %bitcast.169, s32[]{:T(128)} %bitcast.170, s32[]{:T(128)} %bitcast.171, s32[]{:T(128)} %bitcast.172, s32[]{:T(128)} %bitcast.173, s32[]{:T(128)} %bitcast.174, s32[128]{0:T(128)S(1)} %get-tuple-element.1843, s32[512]{0:T(512)S(1)} %get-tuple-element.1844, ...), kind=kLoop, calls=%fused_computation.34.clone.1 | loop fusion | flops 3932160 | bytes 70684 | tf_op jit(solution)/shard_map/while/body/eval_jaxpr/or | solution.py:33
  184.0 4.9 %fusion.180 = pred[128,512]{0,1:T(8,128)(4,1)S(1)} fusion(s32[]{:T(128)} %bitcast.168, s32[]{:T(128)} %bitcast.169, s32[]{:T(128)} %bitcast.170, s32[]{:T(128)} %bitcast.171, s32[]{:T(128)} %bitcast.172, s32[]{:T(128)} %bitcast.173, s32[]{:T(128)} %bitcast.174, s32[128]{0:T(128)S(1)} %get-tuple-element.1843, s32[512]{0:T(512)S(1)} %get-tuple-element.1844, ...), kind=kLoop, calls=%fused_computation.34.clone.1 | loop fusion | flops 3932160 | bytes 70684 | tf_op jit(solution)/shard_map/while/body/eval_jaxpr/or | solution.py:33
  193.3 4.9 %fusion.180 = pred[128,512]{0,1:T(8,128)(4,1)S(1)} fusion(s32[]{:T(128)} %bitcast.168, s32[]{:T(128)} %bitcast.169, s32[]{:T(128)} %bitcast.170, s32[]{:T(128)} %bitcast.171, s32[]{:T(128)} %bitcast.172, s32[]{:T(128)} %bitcast.173, s32[]{:T(128)} %bitcast.174, s32[128]{0:T(128)S(1)} %get-tuple-element.1843, s32[512]{0:T(512)S(1)} %get-tuple-element.1844, ...), kind=kLoop, calls=%fused_computation.34.clone.1 | loop fusion | flops 3932160 | bytes 70684 | tf_op jit(solution)/shard_map/while/body/eval_jaxpr/or | solution.py:33
  200.4 26.1 %all_gather.23 = f32[5,4096]{1,0:T(8,128)} all-gather(f32[5,128]{1,0:T(8,128)S(1)} %get-tuple-element.1949), channel_id=1, replica_groups=mesh['frame'=32,'head'=4] {'frame'}, dimensions={1}, use_global_device_ids=true | all-gather | bytes 84480 | tf_op jit(solution)/shard_map/all_gather | solution.py:128
  226.5 24.7 %all_gather.25 = f32[5,4096]{1,0:T(8,128)} all-gather(f32[5,128]{1,0:T(8,128)S(1)} %get-tuple-element.1952), channel_id=1, replica_groups=mesh['frame'=32,'head'=4] {'frame'}, dimensions={1}, use_global_device_ids=true | all-gather | bytes 84480 | tf_op jit(solution)/shard_map/all_gather | solution.py:129
  251.2 70.5 %while.67 = (s32[]{:T(128)}, f32[128,5,128]{0,2,1:T(8,128)S(1)}, bf16[4096,640]{0,1:T(8,128)(2,1)}, s32[7]{0:T(128)S(1)}, bf16[128,5,128]{2,1,0:T(8,128)(2,1)}, ...) while((s32[]{:T(128)}, f32[128,5,128]{0,2,1:T(8,128)S(1)}, ...), condition=%wide.region_10.11_spmd.clone.clone.clone, body=%wide.region_9.10_spmd.clone.clone.clone.sunk | while | flops 676846336 | bytes 12270941 | solution.py:53
  253.7 4.9 %fusion.193 = pred[128,512]{1,0:T(8,128)(4,1)S(1)} fusion(s32[]{:T(128)} %bitcast.188, s32[]{:T(128)} %bitcast.189, s32[]{:T(128)} %bitcast.190, s32[]{:T(128)} %bitcast.191, s32[]{:T(128)} %bitcast.192, s32[]{:T(128)} %bitcast.193, s32[]{:T(128)} %bitcast.194, s32[128]{0:T(128)S(1)} %get-tuple-element.1872, s32[512]{0:T(512)S(1)} %get-tuple-element.1873, ...), kind=kLoop, calls=%fused_computation.100.clone.1 | loop fusion | flops 3932160 | bytes 70684 | tf_op jit(solution)/shard_map/while/body/eval_jaxpr/or | solution.py:33
  262.5 4.9 %fusion.193 = pred[128,512]{1,0:T(8,128)(4,1)S(1)} fusion(s32[]{:T(128)} %bitcast.188, s32[]{:T(128)} %bitcast.189, s32[]{:T(128)} %bitcast.190, s32[]{:T(128)} %bitcast.191, s32[]{:T(128)} %bitcast.192, s32[]{:T(128)} %bitcast.193, s32[]{:T(128)} %bitcast.194, s32[128]{0:T(128)S(1)} %get-tuple-element.1872, s32[512]{0:T(512)S(1)} %get-tuple-element.1873, ...), kind=kLoop, calls=%fused_computation.100.clone.1 | loop fusion | flops 3932160 | bytes 70684 | tf_op jit(solution)/shard_map/while/body/eval_jaxpr/or | solution.py:33
  271.3 4.9 %fusion.193 = pred[128,512]{1,0:T(8,128)(4,1)S(1)} fusion(s32[]{:T(128)} %bitcast.188, s32[]{:T(128)} %bitcast.189, s32[]{:T(128)} %bitcast.190, s32[]{:T(128)} %bitcast.191, s32[]{:T(128)} %bitcast.192, s32[]{:T(128)} %bitcast.193, s32[]{:T(128)} %bitcast.194, s32[128]{0:T(128)S(1)} %get-tuple-element.1872, s32[512]{0:T(512)S(1)} %get-tuple-element.1873, ...), kind=kLoop, calls=%fused_computation.100.clone.1 | loop fusion | flops 3932160 | bytes 70684 | tf_op jit(solution)/shard_map/while/body/eval_jaxpr/or | solution.py:33
  280.1 4.9 %fusion.193 = pred[128,512]{1,0:T(8,128)(4,1)S(1)} fusion(s32[]{:T(128)} %bitcast.188, s32[]{:T(128)} %bitcast.189, s32[]{:T(128)} %bitcast.190, s32[]{:T(128)} %bitcast.191, s32[]{:T(128)} %bitcast.192, s32[]{:T(128)} %bitcast.193, s32[]{:T(128)} %bitcast.194, s32[128]{0:T(128)S(1)} %get-tuple-element.1872, s32[512]{0:T(512)S(1)} %get-tuple-element.1873, ...), kind=kLoop, calls=%fused_computation.100.clone.1 | loop fusion | flops 3932160 | bytes 70684 | tf_op jit(solution)/shard_map/while/body/eval_jaxpr/or | solution.py:33
  288.9 4.9 %fusion.193 = pred[128,512]{1,0:T(8,128)(4,1)S(1)} fusion(s32[]{:T(128)} %bitcast.188, s32[]{:T(128)} %bitcast.189, s32[]{:T(128)} %bitcast.190, s32[]{:T(128)} %bitcast.191, s32[]{:T(128)} %bitcast.192, s32[]{:T(128)} %bitcast.193, s32[]{:T(128)} %bitcast.194, s32[128]{0:T(128)S(1)} %get-tuple-element.1872, s32[512]{0:T(512)S(1)} %get-tuple-element.1873, ...), kind=kLoop, calls=%fused_computation.100.clone.1 | loop fusion | flops 3932160 | bytes 70684 | tf_op jit(solution)/shard_map/while/body/eval_jaxpr/or | solution.py:33
  297.8 4.9 %fusion.193 = pred[128,512]{1,0:T(8,128)(4,1)S(1)} fusion(s32[]{:T(128)} %bitcast.188, s32[]{:T(128)} %bitcast.189, s32[]{:T(128)} %bitcast.190, s32[]{:T(128)} %bitcast.191, s32[]{:T(128)} %bitcast.192, s32[]{:T(128)} %bitcast.193, s32[]{:T(128)} %bitcast.194, s32[128]{0:T(128)S(1)} %get-tuple-element.1872, s32[512]{0:T(512)S(1)} %get-tuple-element.1873, ...), kind=kLoop, calls=%fused_computation.100.clone.1 | loop fusion | flops 3932160 | bytes 70684 | tf_op jit(solution)/shard_map/while/body/eval_jaxpr/or | solution.py:33
  306.6 4.9 %fusion.193 = pred[128,512]{1,0:T(8,128)(4,1)S(1)} fusion(s32[]{:T(128)} %bitcast.188, s32[]{:T(128)} %bitcast.189, s32[]{:T(128)} %bitcast.190, s32[]{:T(128)} %bitcast.191, s32[]{:T(128)} %bitcast.192, s32[]{:T(128)} %bitcast.193, s32[]{:T(128)} %bitcast.194, s32[128]{0:T(128)S(1)} %get-tuple-element.1872, s32[512]{0:T(512)S(1)} %get-tuple-element.1873, ...), kind=kLoop, calls=%fused_computation.100.clone.1 | loop fusion | flops 3932160 | bytes 70684 | tf_op jit(solution)/shard_map/while/body/eval_jaxpr/or | solution.py:33
  315.4 4.9 %fusion.193 = pred[128,512]{1,0:T(8,128)(4,1)S(1)} fusion(s32[]{:T(128)} %bitcast.188, s32[]{:T(128)} %bitcast.189, s32[]{:T(128)} %bitcast.190, s32[]{:T(128)} %bitcast.191, s32[]{:T(128)} %bitcast.192, s32[]{:T(128)} %bitcast.193, s32[]{:T(128)} %bitcast.194, s32[128]{0:T(128)S(1)} %get-tuple-element.1872, s32[512]{0:T(512)S(1)} %get-tuple-element.1873, ...), kind=kLoop, calls=%fused_computation.100.clone.1 | loop fusion | flops 3932160 | bytes 70684 | tf_op jit(solution)/shard_map/while/body/eval_jaxpr/or | solution.py:33
  324.2 89.3 %while.68 = (s32[]{:T(128)}, f32[128,5,128]{0,2,1:T(8,128)S(1)}, f32[128,5,128]{0,2,1:T(8,128)S(1)}, bf16[4096,640]{0,1:T(8,128)(2,1)}, s32[7]{0:T(128)S(1)}, /*...) while((s32[]{:T(128)}, f32[128,5,128]{0,2,1:T(8,128)S(1)}, ...), condition=%wide.region_14.15_spmd.clone.clone.clone, body=%wide.region_13.14_spmd.clone.clone.clone.sunk | while | flops 342121216 | bytes 11671886 | solution.py:53
  327.6 4.9 %fusion.205 = pred[512,128]{1,0:T(8,128)(4,1)S(1)} fusion(s32[]{:T(128)} %bitcast.205, s32[]{:T(128)} %bitcast.206, s32[]{:T(128)} %bitcast.207, s32[]{:T(128)} %bitcast.208, s32[]{:T(128)} %bitcast.209, s32[]{:T(128)} %bitcast.210, s32[]{:T(128)} %bitcast.211, s32[512]{0:T(512)S(1)} %get-tuple-element.1896, s32[128]{0:T(128)S(1)} %get-tuple-element.1897, ...), kind=kLoop, calls=%fused_computation.166.clone.1 | loop fusion | flops 3932160 | bytes 70684 | tf_op jit(solution)/shard_map/while/body/eval_jaxpr/or | solution.py:33
  338.8 4.9 %fusion.205 = pred[512,128]{1,0:T(8,128)(4,1)S(1)} fusion(s32[]{:T(128)} %bitcast.205, s32[]{:T(128)} %bitcast.206, s32[]{:T(128)} %bitcast.207, s32[]{:T(128)} %bitcast.208, s32[]{:T(128)} %bitcast.209, s32[]{:T(128)} %bitcast.210, s32[]{:T(128)} %bitcast.211, s32[512]{0:T(512)S(1)} %get-tuple-element.1896, s32[128]{0:T(128)S(1)} %get-tuple-element.1897, ...), kind=kLoop, calls=%fused_computation.166.clone.1 | loop fusion | flops 3932160 | bytes 70684 | tf_op jit(solution)/shard_map/while/body/eval_jaxpr/or | solution.py:33
  350.0 4.9 %fusion.205 = pred[512,128]{1,0:T(8,128)(4,1)S(1)} fusion(s32[]{:T(128)} %bitcast.205, s32[]{:T(128)} %bitcast.206, s32[]{:T(128)} %bitcast.207, s32[]{:T(128)} %bitcast.208, s32[]{:T(128)} %bitcast.209, s32[]{:T(128)} %bitcast.210, s32[]{:T(128)} %bitcast.211, s32[512]{0:T(512)S(1)} %get-tuple-element.1896, s32[128]{0:T(128)S(1)} %get-tuple-element.1897, ...), kind=kLoop, calls=%fused_computation.166.clone.1 | loop fusion | flops 3932160 | bytes 70684 | tf_op jit(solution)/shard_map/while/body/eval_jaxpr/or | solution.py:33
  361.1 4.9 %fusion.205 = pred[512,128]{1,0:T(8,128)(4,1)S(1)} fusion(s32[]{:T(128)} %bitcast.205, s32[]{:T(128)} %bitcast.206, s32[]{:T(128)} %bitcast.207, s32[]{:T(128)} %bitcast.208, s32[]{:T(128)} %bitcast.209, s32[]{:T(128)} %bitcast.210, s32[]{:T(128)} %bitcast.211, s32[512]{0:T(512)S(1)} %get-tuple-element.1896, s32[128]{0:T(128)S(1)} %get-tuple-element.1897, ...), kind=kLoop, calls=%fused_computation.166.clone.1 | loop fusion | flops 3932160 | bytes 70684 | tf_op jit(solution)/shard_map/while/body/eval_jaxpr/or | solution.py:33
  372.3 4.9 %fusion.205 = pred[512,128]{1,0:T(8,128)(4,1)S(1)} fusion(s32[]{:T(128)} %bitcast.205, s32[]{:T(128)} %bitcast.206, s32[]{:T(128)} %bitcast.207, s32[]{:T(128)} %bitcast.208, s32[]{:T(128)} %bitcast.209, s32[]{:T(128)} %bitcast.210, s32[]{:T(128)} %bitcast.211, s32[512]{0:T(512)S(1)} %get-tuple-element.1896, s32[128]{0:T(128)S(1)} %get-tuple-element.1897, ...), kind=kLoop, calls=%fused_computation.166.clone.1 | loop fusion | flops 3932160 | bytes 70684 | tf_op jit(solution)/shard_map/while/body/eval_jaxpr/or | solution.py:33
  394.6 4.9 %fusion.205 = pred[512,128]{1,0:T(8,128)(4,1)S(1)} fusion(s32[]{:T(128)} %bitcast.205, s32[]{:T(128)} %bitcast.206, s32[]{:T(128)} %bitcast.207, s32[]{:T(128)} %bitcast.208, s32[]{:T(128)} %bitcast.209, s32[]{:T(128)} %bitcast.210, s32[]{:T(128)} %bitcast.211, s32[512]{0:T(512)S(1)} %get-tuple-element.1896, s32[128]{0:T(128)S(1)} %get-tuple-element.1897, ...), kind=kLoop, calls=%fused_computation.166.clone.1 | loop fusion | flops 3932160 | bytes 70684 | tf_op jit(solution)/shard_map/while/body/eval_jaxpr/or | solution.py:33
  405.8 4.9 %fusion.205 = pred[512,128]{1,0:T(8,128)(4,1)S(1)} fusion(s32[]{:T(128)} %bitcast.205, s32[]{:T(128)} %bitcast.206, s32[]{:T(128)} %bitcast.207, s32[]{:T(128)} %bitcast.208, s32[]{:T(128)} %bitcast.209, s32[]{:T(128)} %bitcast.210, s32[]{:T(128)} %bitcast.211, s32[512]{0:T(512)S(1)} %get-tuple-element.1896, s32[128]{0:T(128)S(1)} %get-tuple-element.1897, ...), kind=kLoop, calls=%fused_computation.166.clone.1 | loop fusion | flops 3932160 | bytes 70684 | tf_op jit(solution)/shard_map/while/body/eval_jaxpr/or | solution.py:33
  414.6 10.7 %all-reduce = (f32[128]{0:T(128)S(1)}, f32[128]{0:T(128)S(1)}) all-reduce(f32[128]{0:T(128)} %fusion.112, f32[128]{0:T(128)S(1)} %fusion.119), channel_id=1, replica_groups=mesh['frame'=32,'head'=4] {'head'}, use_global_device_ids=true, to_apply=%region_12.13 | all-reduce | flops 256 | bytes 2048 | tf_op jit(solution)/shard_map/psum | solution.py:190
  (319 shorter events, 140.3 us)
Async XLA Ops:
  7.2 16.6 %copy-start.10 = (bf16[128,640]{1,0:T(8,128)(2,1)S(1)}, bf16[128,640]{1,0:T(8,128)(2,1)}, u32[]{:S(2)}) copy-start(bf16[128,640]{1,0:T(8,128)(2,1)} %param.15) | copy-start | bytes 491524
  7.2 18.1 %copy-start.13 = (f32[640]{0:T(1024)S(1)}, f32[640]{0:T(1024)}, u32[]{:S(2)}) copy-start(f32[640]{0:T(1024)} %param.16) | copy-start | bytes 7684
  7.2 19.0 %copy-start.11 = (bf16[128,640]{1,0:T(8,128)(2,1)S(1)}, bf16[128,640]{1,0:T(8,128)(2,1)}, u32[]{:S(2)}) copy-start(bf16[128,640]{1,0:T(8,128)(2,1)} %param.18) | copy-start | bytes 491524
  7.2 66.7 %all-gather.5.cloned.1.call-start = ((), (), s32[]{:S(2)}) async-start(), calls=%async_computation | async-start | bytes 5406720 | tf_op jit(solution)/shard_map/all_gather | solution.py:62
  8.4 18.6 %copy-start.5 = (bf16[128,640]{0,1:T(8,128)(2,1)}, bf16[128,640]{0,1:T(8,128)(2,1)S(1)}, u32[]{:S(2)}) copy-start(bf16[128,640]{0,1:T(8,128)(2,1)S(1)} %copy.22) | copy-start | bytes 491524
  9.6 19.3 %copy-start.3 = (bf16[128,640]{0,1:T(8,128)(2,1)}, bf16[128,640]{0,1:T(8,128)(2,1)S(1)}, u32[]{:S(2)}) copy-start(bf16[128,640]{0,1:T(8,128)(2,1)S(1)} %copy.23) | copy-start | bytes 491524
  23.7 103.0 %all-gather.7.cloned.1.call-start = ((), (), s32[]{:S(2)}) async-start(), calls=%async_computation.1 | async-start | bytes 5406720 | tf_op jit(solution)/shard_map/all_gather | solution.py:63
  24.6 8.0 %copy-start.14 = (f32[640]{0:T(1024)S(1)}, f32[640]{0:T(1024)}, u32[]{:S(2)}) copy-start(f32[640]{0:T(1024)} %param.17) | copy-start | bytes 7684
  24.6 8.0 %copy-start.8 = (bf16[128,640]{0,1:T(8,128)(2,1)S(1)}, bf16[128,640]{0,1:T(8,128)(2,1)}, u32[]{:S(2)}) copy-start(bf16[128,640]{0,1:T(8,128)(2,1)} %fusion.115) | copy-start | bytes 491524
  24.6 299.5 %all-gather.9.cloned.1.call-start = ((), (), s32[]{:S(2)}) async-start(), calls=%async_computation.2 | async-start | bytes 5406720 | tf_op jit(solution)/shard_map/all_gather | solution.py:168
  26.1 7.3 %copy-start.9 = (bf16[128,640]{0,1:T(8,128)(2,1)S(1)}, bf16[128,640]{0,1:T(8,128)(2,1)}, u32[]{:S(2)}) copy-start(bf16[128,640]{0,1:T(8,128)(2,1)} %copy.24) | copy-start | bytes 491524
  26.1 298.1 %all-gather.11.cloned.1.call-start = ((), (), s32[]{:S(2)}) async-start(), calls=%async_computation.3 | async-start | bytes 5406720 | tf_op jit(solution)/shard_map/all_gather | solution.py:169
  27.0 4.7 %copy-start.7 = (bf16[128,640]{0,1:T(8,128)(2,1)S(1)}, bf16[128,640]{0,1:T(8,128)(2,1)}, u32[]{:S(2)}) copy-start(bf16[128,640]{0,1:T(8,128)(2,1)} %copy.25) | copy-start | bytes 491524
  27.0 99.7 %copy-start = (s32[7]{0:T(128)S(1)}, s32[7]{0:T(128)}, u32[]{:S(2)}) copy-start(s32[7]{0:T(128)} %param.19) | copy-start | bytes 88
  252.6 6.0 %copy-start.2 = (bf16[128,5,128]{2,1,0:T(8,128)(2,1)S(1)}, bf16[128,5,128]{2,1,0:T(8,128)(2,1)}, u32[]{:S(2)}) copy-start(bf16[128,5,128]{2,1,0:T(8,128)(2,1)} %get-tuple-element.1976) | copy-start | bytes 491524 | tf_op jit(solution)/shard_map/while
  261.4 6.0 %copy-start.2 = (bf16[128,5,128]{2,1,0:T(8,128)(2,1)S(1)}, bf16[128,5,128]{2,1,0:T(8,128)(2,1)}, u32[]{:S(2)}) copy-start(bf16[128,5,128]{2,1,0:T(8,128)(2,1)} %get-tuple-element.1976) | copy-start | bytes 491524 | tf_op jit(solution)/shard_map/while
  270.3 6.0 %copy-start.2 = (bf16[128,5,128]{2,1,0:T(8,128)(2,1)S(1)}, bf16[128,5,128]{2,1,0:T(8,128)(2,1)}, u32[]{:S(2)}) copy-start(bf16[128,5,128]{2,1,0:T(8,128)(2,1)} %get-tuple-element.1976) | copy-start | bytes 491524 | tf_op jit(solution)/shard_map/while
  279.1 6.0 %copy-start.2 = (bf16[128,5,128]{2,1,0:T(8,128)(2,1)S(1)}, bf16[128,5,128]{2,1,0:T(8,128)(2,1)}, u32[]{:S(2)}) copy-start(bf16[128,5,128]{2,1,0:T(8,128)(2,1)} %get-tuple-element.1976) | copy-start | bytes 491524 | tf_op jit(solution)/shard_map/while
  287.9 6.0 %copy-start.2 = (bf16[128,5,128]{2,1,0:T(8,128)(2,1)S(1)}, bf16[128,5,128]{2,1,0:T(8,128)(2,1)}, u32[]{:S(2)}) copy-start(bf16[128,5,128]{2,1,0:T(8,128)(2,1)} %get-tuple-element.1976) | copy-start | bytes 491524 | tf_op jit(solution)/shard_map/while
  296.7 6.0 %copy-start.2 = (bf16[128,5,128]{2,1,0:T(8,128)(2,1)S(1)}, bf16[128,5,128]{2,1,0:T(8,128)(2,1)}, u32[]{:S(2)}) copy-start(bf16[128,5,128]{2,1,0:T(8,128)(2,1)} %get-tuple-element.1976) | copy-start | bytes 491524 | tf_op jit(solution)/shard_map/while
  305.5 6.0 %copy-start.2 = (bf16[128,5,128]{2,1,0:T(8,128)(2,1)S(1)}, bf16[128,5,128]{2,1,0:T(8,128)(2,1)}, u32[]{:S(2)}) copy-start(bf16[128,5,128]{2,1,0:T(8,128)(2,1)} %get-tuple-element.1976) | copy-start | bytes 491524 | tf_op jit(solution)/shard_map/while
  314.3 6.0 %copy-start.2 = (bf16[128,5,128]{2,1,0:T(8,128)(2,1)S(1)}, bf16[128,5,128]{2,1,0:T(8,128)(2,1)}, u32[]{:S(2)}) copy-start(bf16[128,5,128]{2,1,0:T(8,128)(2,1)} %get-tuple-element.1976) | copy-start | bytes 491524 | tf_op jit(solution)/shard_map/while
  324.2 8.4 %copy-start.12 = (bf16[128,5,128]{2,0,1:T(8,128)(2,1)S(1)}, bf16[128,5,128]{2,0,1:T(8,128)(2,1)}, u32[]{:S(2)}) copy-start(bf16[128,5,128]{2,0,1:T(8,128)(2,1)} %get-tuple-element.2021) | copy-start | bytes 491524 | tf_op jit(solution)/shard_map/while
  335.3 8.4 %copy-start.12 = (bf16[128,5,128]{2,0,1:T(8,128)(2,1)S(1)}, bf16[128,5,128]{2,0,1:T(8,128)(2,1)}, u32[]{:S(2)}) copy-start(bf16[128,5,128]{2,0,1:T(8,128)(2,1)} %get-tuple-element.2021) | copy-start | bytes 491524 | tf_op jit(solution)/shard_map/while
  346.5 8.4 %copy-start.12 = (bf16[128,5,128]{2,0,1:T(8,128)(2,1)S(1)}, bf16[128,5,128]{2,0,1:T(8,128)(2,1)}, u32[]{:S(2)}) copy-start(bf16[128,5,128]{2,0,1:T(8,128)(2,1)} %get-tuple-element.2021) | copy-start | bytes 491524 | tf_op jit(solution)/shard_map/while
  357.6 8.4 %copy-start.12 = (bf16[128,5,128]{2,0,1:T(8,128)(2,1)S(1)}, bf16[128,5,128]{2,0,1:T(8,128)(2,1)}, u32[]{:S(2)}) copy-start(bf16[128,5,128]{2,0,1:T(8,128)(2,1)} %get-tuple-element.2021) | copy-start | bytes 491524 | tf_op jit(solution)/shard_map/while
  368.8 8.4 %copy-start.12 = (bf16[128,5,128]{2,0,1:T(8,128)(2,1)S(1)}, bf16[128,5,128]{2,0,1:T(8,128)(2,1)}, u32[]{:S(2)}) copy-start(bf16[128,5,128]{2,0,1:T(8,128)(2,1)} %get-tuple-element.2021) | copy-start | bytes 491524 | tf_op jit(solution)/shard_map/while
  380.0 8.4 %copy-start.12 = (bf16[128,5,128]{2,0,1:T(8,128)(2,1)S(1)}, bf16[128,5,128]{2,0,1:T(8,128)(2,1)}, u32[]{:S(2)}) copy-start(bf16[128,5,128]{2,0,1:T(8,128)(2,1)} %get-tuple-element.2021) | copy-start | bytes 491524 | tf_op jit(solution)/shard_map/while
  391.1 8.4 %copy-start.12 = (bf16[128,5,128]{2,0,1:T(8,128)(2,1)S(1)}, bf16[128,5,128]{2,0,1:T(8,128)(2,1)}, u32[]{:S(2)}) copy-start(bf16[128,5,128]{2,0,1:T(8,128)(2,1)} %get-tuple-element.2021) | copy-start | bytes 491524 | tf_op jit(solution)/shard_map/while
  402.3 8.4 %copy-start.12 = (bf16[128,5,128]{2,0,1:T(8,128)(2,1)S(1)}, bf16[128,5,128]{2,0,1:T(8,128)(2,1)}, u32[]{:S(2)}) copy-start(bf16[128,5,128]{2,0,1:T(8,128)(2,1)} %get-tuple-element.2021) | copy-start | bytes 491524 | tf_op jit(solution)/shard_map/while
  413.5 13.8 %copy-start.4 = (bf16[128,640]{0,1:T(8,128)(2,1)S(1)}, bf16[128,640]{0,1:T(8,128)(2,1)}, u32[]{:S(2)}) copy-start(bf16[128,640]{0,1:T(8,128)(2,1)} %copy-done.3) | copy-start | bytes 491524
  413.5 13.8 %copy-start.16 = (f32[128]{0:T(128)S(1)}, f32[128]{0:T(128)}, u32[]{:S(2)}) copy-start(f32[128]{0:T(128)} %get-tuple-element.1617) | copy-start | bytes 1540
  (10 other events, 13.2 us)
Sparse Core Ops, SparseCore 0:
  23.8 50.0 all-gather.4
  76.1 50.4 all-gather.6
  129.4 50.4 all-gather.8
  182.0 50.5 all-gather.10
where the time goes:
time: 439 us; the launch traced here: 436 us
  other arithmetic  129 us (29%)
  waiting for transfers between devices  93.1 us (21%)
  local copies, waits for them, and re-layouts  74.3 us (17%)
  blocking collectives  73.4 us (17%)
  matrix products  50 us (11%)
  between operations  14 us (3%)
    or x24, other arithmetic, window_mask(): return (band_level == 0) | (relative < window_width)  118 us
    all_gather x1, waiting for transfers between devices, fold_keys(): lax.all_gather(values, 'frame', axis=0, tiled=True)  52.7 us
    all_gather x1, waiting for transfers between devices, fold_keys(): lax.all_gather(keys, 'frame', axis=0, tiled=True)  40.3 us
    dynamic_slice x24, local copies, waits for them, and re-layouts, one_block(): lax.dynamic_slice_in_dim(member, block_index * stride, stride, 0)  33.8 us
    all_gather x1, blocking collectives, local(): lax.all_gather(log_total, 'frame', axis=1, tiled=True)  26.1 us
    all_gather x1, blocking collectives, local(): lax.all_gather(delta, 'frame', axis=1, tiled=True)  24.7 us
    slice x24, local copies, waits for them, and re-layouts, window_mask(): window_offset[band_index]  15.9 us
    dot_general x16, matrix products, block_scores(): jnp.einsum('qhd,khd->hqk', grad_heads, value_part, preferred_element_type...  14 us
  transfers between devices with their start and end apart: 4, of which 2 were waited for; matrix products, arithmetic and copies ran while one was open for 35% of the time, Pallas kernels for 0%

commit v1 on v0

v1 whole, which is shorter than its diff:
```python
import functools
import math

import jax
import jax.numpy as jnp
import numpy as np
from jax import lax
from jax.experimental import pallas as pl
from jax.experimental.pallas import tpu as pltpu
from jax.sharding import PartitionSpec as P

HEADS = 20
HD = 128
NB = 4
TOK = 128
BLK = 32
FRAMES = 32
FEAT = HEADS * HD
LOCAL_HEADS = 5
LOCAL = LOCAL_HEADS * HD
TILES = 8
EPSILON = 1e-06
NEG = -1e30
SCALE = HD ** (-0.5)
SCALE2 = SCALE * math.log2(math.e)
MESH = pl.DeviceIdType.MESH
VMEM_LIMIT = 60 * 1024 * 1024

UNITS = LOCAL_HEADS * NB


def unit_device(head, block):
    return 2 * ((3 * (2 * head + block // 2)) % 16) + block % 2


def my_unit():
    me = lax.axis_index("frame")
    slot = lax.rem(11 * (me // 2), 16)
    return me, slot < 2 * LOCAL_HEADS, slot // 2, 2 * lax.rem(slot, 2) + lax.rem(me, 2)


def block_table():
    rows, starts = [], [0]
    for tile in range(TILES):
        for frame in range(max(0, 4 * tile - 4), min(FRAMES, 4 * tile + 8)):
            rows.append((frame, frame - 4 * tile + 4))
        for other in range(TILES):
            apart = other - tile
            if abs(apart) < 2:
                continue
            near = {2: (2, 3), 3: (3,), 4: (3, 4)}.get(abs(apart), (4,))
            for level in near:
                if len(near) == 1:
                    kind = 12
                else:
                    kind = 13 + {-4: 0, -2: 1, 2: 2, 4: 3}[apart] * 2 + (level - near[0])
                rows.append((32 + (level - 2) * 8 + other, kind))
        starts.append(len(rows))
    return np.array(rows, np.int32), np.array(starts, np.int32)


KIND_FAR = [(-4, 3), (-4, 4), (-2, 2), (-2, 3), (2, 2), (2, 3), (4, 3), (4, 4)]
KINDS = 13 + len(KIND_FAR)
MOST_BLOCKS = 20


def enter(barrier_head=True):
    barrier = pltpu.get_barrier_semaphore()
    me = lax.axis_index("frame")
    row = lax.axis_index("head")
    for step in range(1, FRAMES):
        pl.semaphore_signal(
            barrier, inc=1, device_id={"frame": lax.rem(me + step, FRAMES)}, device_id_type=MESH
        )
    for step in range(1, 4):
        pl.semaphore_signal(
            barrier, inc=1, device_id={"head": lax.rem(row + step, 4)}, device_id_type=MESH
        )
    pl.semaphore_wait(barrier, FRAMES - 1 + 3)


def pair_rows(first, second):
    lane = lax.broadcasted_iota(jnp.int32, (TOK, TOK), 1)
    both = jnp.where(lane == 0, first, jnp.where(lane == 1, second, 0.0))
    return both.T[:8]


def pair_columns(rows):
    full = jnp.concatenate([rows, jnp.zeros((TOK - 8, TOK), jnp.float32)], axis=0).T
    return full[:, 0:1], full[:, 1:2]


def head_sum(stat, slots, send_sem, recv_sem):
    row = lax.axis_index("head")
    copies = []
    for step in range(1, 4):
        copy = pltpu.make_async_remote_copy(
            src_ref=stat,
            dst_ref=slots.at[step - 1],
            send_sem=send_sem.at[step - 1],
            recv_sem=recv_sem.at[step - 1],
            device_id={"head": lax.rem(row + step, 4)},
            device_id_type=MESH,
        )
        copy.start()
        copies.append(copy)
    return copies


def head_slice(head):
    return pl.ds(head * HD, HD)


def send_kernel(
    q_ref, k_ref, v_ref, g_ref, qgain_ref, kgain_ref,
    k_all, v_all, q_all, g_all, total_ref,
    keys, queries, stat, slots,
    zsend, zrecv, vsend, gsend, ksend, qsend, vrecv, grecv, krecv, qrecv,
):
    me, is_unit, _, _ = my_unit()
    enter()

    def send(src, dst_all, target, send_sem, recv_sem):
        @pl.when(me != target)
        def _():
            pltpu.make_async_remote_copy(
                src_ref=src, dst_ref=dst_all.at[me], send_sem=send_sem, recv_sem=recv_sem.at[me],
                device_id={"frame": target}, device_id_type=MESH,
            ).start()

        @pl.when(me == target)
        def _():
            pltpu.make_async_copy(src, dst_all.at[me], recv_sem.at[me]).start()

    for head in range(LOCAL_HEADS):
        for block in range(NB):
            unit = head * NB + block
            target = unit_device(head, block)
            send(v_ref.at[:, head_slice(head)], v_all, target, vsend.at[unit], vrecv)
            send(g_ref.at[pl.ds(block * BLK, BLK), head_slice(head)], g_all, target, gsend.at[unit], grecv)

    def squares(ref):
        acc = jnp.zeros((TOK, HD), jnp.float32)
        for head in range(LOCAL_HEADS):
            part = ref[:, head_slice(head)].astype(jnp.float32)
            acc = acc + part * part
        return jnp.sum(acc, axis=1, keepdims=True)

    stat[...] = pair_rows(squares(q_ref), squares(k_ref))
    for copy in head_sum(stat, slots, zsend, zrecv):
        copy.wait()
    total = stat[...] + slots[0] + slots[1] + slots[2]
    total_ref[...] = total
    qsum, ksum = pair_columns(total)
    qrms = lax.rsqrt(qsum / FEAT + EPSILON)
    krms = lax.rsqrt(ksum / FEAT + EPSILON)
    for head in range(LOCAL_HEADS):
        part = k_ref[:, head_slice(head)].astype(jnp.float32)
        keys[head] = (part * krms * kgain_ref[:, head_slice(head)]).astype(jnp.bfloat16)
        part = q_ref[:, head_slice(head)].astype(jnp.float32)
        queries[head] = (part * qrms * qgain_ref[:, head_slice(head)]).astype(jnp.bfloat16)
        for block in range(NB):
            unit = head * NB + block
            target = unit_device(head, block)
            send(keys.at[head], k_all, target, ksend.at[unit], krecv)
            send(queries.at[head, pl.ds(block * BLK, BLK)], q_all, target, qsend.at[unit], qrecv)

    @pl.when(is_unit)
    def _():
        @pl.loop(0, FRAMES)
        def _(frame):
            for ref, sem in ((v_all, vrecv), (g_all, grecv), (k_all, krecv), (q_all, qrecv)):
                pltpu.make_async_copy(ref.at[frame], ref.at[frame], sem.at[frame]).wait()

    for head in range(LOCAL_HEADS):
        for block in range(NB):
            unit = head * NB + block
            target = unit_device(head, block)

            @pl.when(me != target)
            def _():
                rows = pl.ds(block * BLK, BLK)
                for src, dst, ssem, rsem in (
                    (v_ref.at[:, head_slice(head)], v_all, vsend, vrecv),
                    (g_ref.at[rows, head_slice(head)], g_all, gsend, grecv),
                    (keys.at[head], k_all, ksend, krecv),
                    (queries.at[head, rows], q_all, qsend, qrecv),
                ):
                    pltpu.make_async_remote_copy(
                        src_ref=src, dst_ref=dst.at[me], send_sem=ssem.at[unit], recv_sem=rsem.at[me],
                        device_id={"frame": target}, device_id_type=MESH,
                    ).wait_send()


def dot(a, b, contract):
    return lax.dot_general(a, b, (contract, ((), ())), preferred_element_type=jnp.float32)


def unit_kernel(
    offset_ref, table_ref, start_ref,
    k_all, v_all, q_all, g_all,
    dkv_all, dq_all,
    kv, kt, w, acc, bias, tbuf, gbuf, dqt,
):
    _, is_unit, _, block = my_unit()

    @pl.when(is_unit)
    def _():
        row_frame = lax.broadcasted_iota(jnp.int32, (TOK, TOK), 0) // BLK
        lane_frame = lax.broadcasted_iota(jnp.int32, (TOK, TOK), 1) // BLK
        zero = jnp.zeros((TOK, TOK), jnp.float32)
        hit1 = jnp.where(((row_frame - block - offset_ref[0]) & 3) < 2, 0.0, NEG)
        hit2 = jnp.where(((row_frame - block - offset_ref[1]) & 3) < 1, 0.0, NEG)

        @pl.loop(0, 12)
        def _(kind):
            d = jnp.abs(kind - 4 - lane_frame)
            bias[kind] = jnp.where(d < 2, 0.0, jnp.where(d < 4, hit1, hit2))

        bias[12] = zero
        for index, (apart, level) in enumerate(KIND_FAR):
            d = jnp.abs(4 * apart + row_frame - lane_frame)
            bias[13 + index] = jnp.where((d >= 2**level) & (d < 2 ** (level + 1)), 0.0, NEG)

        picks = [
            pl.multiple_of(((block + offset_ref[level - 1]) & 3) * BLK, BLK) for level in (2, 3, 4)
        ]

        @pl.loop(0, FRAMES)
        def _(frame):
            kv[pl.ds(pl.multiple_of(frame * TOK, TOK), TOK), 0:HD] = k_all[frame]
            kv[pl.ds(pl.multiple_of(frame * TOK, TOK), TOK), HD : 2 * HD] = v_all[frame]
            for index, pick in enumerate(picks):
                where = pl.multiple_of((FRAMES * NB + index * FRAMES + frame) * BLK, BLK)
                kv[pl.ds(where, BLK), 0:HD] = k_all[frame, pl.ds(pick, BLK)]
                kv[pl.ds(where, BLK), HD : 2 * HD] = v_all[frame, pl.ds(pick, BLK)]

        @pl.loop(0, 56)
        def _(blk):
            at = pl.ds(pl.multiple_of(blk * TOK, TOK), TOK)
            kt[blk] = kv[at, 0:HD].T
            acc[at, :] = jnp.zeros((TOK, 2 * HD), jnp.float32)

        @pl.loop(0, TILES)
        def _(tile):
            w[tile, 0:TOK, HD:] = jnp.zeros((TOK, HD), jnp.bfloat16)
            w[tile, TOK:, 0:HD] = jnp.zeros((TOK, HD), jnp.bfloat16)
            for part in range(4):
                w[tile, part * BLK : (part + 1) * BLK, 0:HD] = q_all[4 * tile + part]
                w[tile, TOK + part * BLK : TOK + (part + 1) * BLK, HD:] = g_all[4 * tile + part]

        @pl.loop(0, TILES)
        def _(tile):
            first = start_ref[tile]
            count = start_ref[tile + 1] - first

            def scores(slot, peak):
                blk, kind = table_ref[first + slot, 0], table_ref[first + slot, 1]
                at = pl.ds(pl.multiple_of(blk * TOK, TOK), TOK)
                both = dot(kv[at, :], w[tile], ((1,), (1,)))
                t = both[:, 0:TOK] * SCALE2 + bias[kind]
                tbuf[slot] = t
                gbuf[slot] = both[:, TOK:]
                return jnp.maximum(peak, jnp.max(t.reshape(16, 8, TOK), axis=0))

            peak = lax.fori_loop(0, count, scores, jnp.full((8, TOK), NEG, jnp.float32))
            peak = jnp.max(peak, axis=0, keepdims=True)

            def weigh(slot, sums):
                weight = jnp.exp2(tbuf[slot] - peak)
                tbuf[slot] = weight
                return (
                    sums[0] + jnp.sum(weight.reshape(16, 8, TOK), axis=0),
                    sums[1] + jnp.sum((weight * gbuf[slot]).reshape(16, 8, TOK), axis=0),
                )

            blank = jnp.zeros((8, TOK), jnp.float32)
            total, weighted = lax.fori_loop(0, count, weigh, (blank, blank))
            total = jnp.sum(total, axis=0, keepdims=True)
            inverse = 1.0 / total
            delta = jnp.sum(weighted, axis=0, keepdims=True) * inverse
            dqt[...] = jnp.zeros((HD, 2 * TOK), jnp.float32)

            @pl.loop(0, count)
            def _(slot):
                blk = table_ref[first + slot, 0]
                at = pl.ds(pl.multiple_of(blk * TOK, TOK), TOK)
                probs = tbuf[slot] * inverse
                grad = probs * (gbuf[slot] - delta)
                high = grad.astype(jnp.bfloat16)
                low = (grad - high.astype(jnp.float32)).astype(jnp.bfloat16)
                left = jnp.concatenate([high, probs.astype(jnp.bfloat16)], axis=1)
                acc[at, :] += dot(left, w[tile], ((1,), (0,)))
                dqt[...] += dot(kt[blk], jnp.concatenate([high, low], axis=1), ((1,), (0,)))

            dq = (dqt[:, 0:TOK] + dqt[:, TOK:]).T
            for part in range(4):
                dq_all[4 * tile + part] = dq[part * BLK : (part + 1) * BLK]

        @pl.loop(0, FRAMES)
        def _(frame):
            for index, pick in enumerate(picks):
                home = pl.ds(pl.multiple_of(frame * TOK + pick, BLK), BLK)
                where = pl.multiple_of((FRAMES * NB + index * FRAMES + frame) * BLK, BLK)
                acc[home, :] += acc[pl.ds(where, BLK), :]
            dkv_all[frame] = acc[pl.ds(pl.multiple_of(frame * TOK, TOK), TOK), :].astype(jnp.bfloat16)


def home_kernel(
    q_ref, k_ref, qgain_ref, kgain_ref, total_ref, dkv_all, dq_all,
    dq_out, dk_out, dv_out,
    dkv_in, dq_in, kgrad, stat, slots,
    zsend, zrecv, kvsend, qsend, kvrecv, qrecv,
):
    me, is_unit, head, block = my_unit()
    enter()
    unit = head * NB + block

    def copies(frame):
        return (
            pltpu.make_async_remote_copy(
                src_ref=dq_all.at[frame], dst_ref=dq_in.at[unit], send_sem=qsend.at[frame],
                recv_sem=qrecv.at[unit], device_id={"frame": frame}, device_id_type=MESH,
            ),
            pltpu.make_async_remote_copy(
                src_ref=dkv_all.at[frame], dst_ref=dkv_in.at[unit], send_sem=kvsend.at[frame],
                recv_sem=kvrecv.at[unit], device_id={"frame": frame}, device_id_type=MESH,
            ),
        )

    @pl.when(is_unit)
    def _():
        pltpu.make_async_copy(dq_all.at[me], dq_in.at[unit], qrecv.at[unit]).start()
        pltpu.make_async_copy(dkv_all.at[me], dkv_in.at[unit], kvrecv.at[unit]).start()

        @pl.loop(1, FRAMES)
        def _(step):
            for copy in copies(lax.rem(me + step, FRAMES)):
                copy.start()

    qsum, ksum = pair_columns(total_ref[...])
    qrms = lax.rsqrt(qsum / FEAT + EPSILON)
    krms = lax.rsqrt(ksum / FEAT + EPSILON)
    qinner = jnp.zeros((TOK, HD), jnp.float32)
    kinner = jnp.zeros((TOK, HD), jnp.float32)
    for h in range(LOCAL_HEADS):
        for b in range(NB):
            u = h * NB + b
            pltpu.make_async_copy(dq_in.at[u], dq_in.at[u], qrecv.at[u]).wait()
            pltpu.make_async_copy(dkv_in.at[u], dkv_in.at[u], kvrecv.at[u]).wait()
        gained = qgain_ref[:, head_slice(h)] * (dq_in[pl.ds(h * NB, NB)].reshape(TOK, HD) * SCALE)
        qinner = qinner + gained * q_ref[:, head_slice(h)].astype(jnp.float32)
        both = dkv_in[h * NB].astype(jnp.float32)
        for b in range(1, NB):
            both = both + dkv_in[h * NB + b].astype(jnp.float32)
        dv_out[:, head_slice(h)] = both[:, HD:].astype(jnp.bfloat16)
        gained = kgain_ref[:, head_slice(h)] * (both[:, 0:HD] * SCALE)
        kgrad[:, head_slice(h)] = gained
        kinner = kinner + gained * k_ref[:, head_slice(h)].astype(jnp.float32)
    stat[...] = pair_rows(
        jnp.sum(qinner, axis=1, keepdims=True), jnp.sum(kinner, axis=1, keepdims=True)
    )
    for copy in head_sum(stat, slots, zsend, zrecv):
        copy.wait()
    qdot, kdot = pair_columns(stat[...] + slots[0] + slots[1] + slots[2])
    qfactor = qrms * qrms * qrms / FEAT * qdot
    kfactor = krms * krms * krms / FEAT * kdot
    for h in range(LOCAL_HEADS):
        gained = qgain_ref[:, head_slice(h)] * (dq_in[pl.ds(h * NB, NB)].reshape(TOK, HD) * SCALE)
        raw = q_ref[:, head_slice(h)].astype(jnp.float32)
        dq_out[:, head_slice(h)] = (qrms * gained - qfactor * raw).astype(jnp.bfloat16)
        raw = k_ref[:, head_slice(h)].astype(jnp.float32)
        dk_out[:, head_slice(h)] = (krms * kgrad[:, head_slice(h)] - kfactor * raw).astype(jnp.bfloat16)

    @pl.when(is_unit)
    def _():
        @pl.loop(1, FRAMES)
        def _(step):
            for copy in copies(lax.rem(me + step, FRAMES)):
                copy.wait_send()


def local(query_raw, key_raw, values, query_gain, key_gain, out_grad, window_offset):
    bf16, f32 = jnp.bfloat16, jnp.float32
    vmem = pl.BlockSpec(memory_space=pltpu.VMEM)
    hbm = pl.BlockSpec(memory_space=pl.ANY)
    smem = pl.BlockSpec(memory_space=pltpu.SMEM)
    dma = pltpu.SemaphoreType.DMA
    qgain = query_gain.reshape(1, LOCAL)
    kgain = key_gain.reshape(1, LOCAL)
    shape = jax.ShapeDtypeStruct
    k_all, v_all, q_all, g_all, total = pl.pallas_call(
        send_kernel,
        name="to_units",
        out_shape=(
            shape((FRAMES, TOK, HD), bf16),
            shape((FRAMES, TOK, HD), bf16),
            shape((FRAMES, BLK, HD), bf16),
            shape((FRAMES, BLK, HD), bf16),
            shape((8, TOK), f32),
        ),
        in_specs=[vmem] * 6,
        out_specs=[hbm] * 4 + [vmem],
        scratch_shapes=[
            pltpu.VMEM((LOCAL_HEADS, TOK, HD), bf16),
            pltpu.VMEM((LOCAL_HEADS, TOK, HD), bf16),
            pltpu.VMEM((8, TOK), f32),
            pltpu.VMEM((3, 8, TOK), f32),
            dma((3,)), dma((3,)),
            dma((UNITS,)), dma((UNITS,)), dma((UNITS,)), dma((UNITS,)),
            dma((FRAMES,)), dma((FRAMES,)), dma((FRAMES,)), dma((FRAMES,)),
        ],
        compiler_params=pltpu.CompilerParams(
            collective_id=0, has_side_effects=True, vmem_limit_bytes=VMEM_LIMIT
        ),
    )(query_raw, key_raw, values, out_grad, qgain, kgain)
    table, starts = block_table()
    dkv_all, dq_all = pl.pallas_call(
        unit_kernel,
        name="unit_grads",
        out_shape=(shape((FRAMES, TOK, 2 * HD), bf16), shape((FRAMES, BLK, HD), f32)),
        in_specs=[smem] * 3 + [vmem] * 4,
        out_specs=[vmem] * 2,
        scratch_shapes=[
            pltpu.VMEM((56 * TOK, 2 * HD), bf16),
            pltpu.VMEM((56, HD, TOK), bf16),
            pltpu.VMEM((TILES, 2 * TOK, 2 * HD), bf16),
            pltpu.VMEM((56 * TOK, 2 * HD), f32),
            pltpu.VMEM((KINDS, TOK, TOK), f32),
            pltpu.VMEM((MOST_BLOCKS, TOK, TOK), f32),
            pltpu.VMEM((MOST_BLOCKS, TOK, TOK), f32),
            pltpu.VMEM((HD, 2 * TOK), f32),
        ],
        compiler_params=pltpu.CompilerParams(vmem_limit_bytes=VMEM_LIMIT),
    )(window_offset, jnp.asarray(table), jnp.asarray(starts), k_all, v_all, q_all, g_all)
    return pl.pallas_call(
        home_kernel,
        name="to_homes",
        out_shape=(shape((TOK, LOCAL), bf16),) * 3,
        in_specs=[vmem] * 5 + [hbm] * 2,
        out_specs=[vmem] * 3,
        scratch_shapes=[
            pltpu.VMEM((UNITS, TOK, 2 * HD), bf16),
            pltpu.VMEM((UNITS, BLK, HD), f32),
            pltpu.VMEM((TOK, LOCAL), f32),
            pltpu.VMEM((8, TOK), f32),
            pltpu.VMEM((3, 8, TOK), f32),
            dma((3,)), dma((3,)),
            dma((FRAMES,)), dma((FRAMES,)), dma((UNITS,)), dma((UNITS,)),
        ],
        compiler_params=pltpu.CompilerParams(
            collective_id=1, has_side_effects=True, vmem_limit_bytes=VMEM_LIMIT
        ),
    )(query_raw, key_raw, qgain, kgain, total, dkv_all, dq_all)


def solution(mesh):
    placed = (
        P("frame", "head"),
        P("frame", "head"),
        P("frame", "head"),
        P("head"),
        P("head"),
        P("frame", "head"),
        P(),
    )
    return jax.shard_map(
        local,
        mesh=mesh,
        in_specs=placed,
        out_specs=(P("frame", "head"), P("frame", "head"), P("frame", "head")),
        check_vma=False,
    )
```

time: 439 us -> 188 us (0.43)
  the two profiles are of different devices: /device:TPU:0 before, /device:TPU:29 now
where the time goes in v1:
time: 188 us
  Pallas kernels  180 us (96%)
  local copies, waits for them, and re-layouts  7.32 us (4%)
    pallas_call x1, Pallas kernels, local(): pl.pallas_call(unit_kernel, name='unit_grads', out_shape=(shape((FRAMES,...  75 us
    pallas_call x1, Pallas kernels, local(): pl.pallas_call(home_kernel, name='to_homes', out_shape=(shape((TOK, LOCAL...  64.4 us
    pallas_call x1, Pallas kernels, local(): pl.pallas_call(send_kernel, name='to_units', out_shape=(shape((FRAMES, TO...  40.7 us
    unnamed x3, local copies, waits for them, and re-layouts  4.79 us

profile of v1, /device:TPU:29, one launch (start us, length us, event | category | flops | bytes accessed | tf_op | source)
XLA Modules:
  0.0 188.1 jit_solution(4081983847483352605)
XLA Ops:
  0.6 1.3 reshape.12.qgain_ref
  1.9 1.3 reshape.13.kgain_ref
  3.2 40.7 %to_units.1 = (bf16[32,128,128]{2,1,0:T(8,128)(2,1)}, bf16[32,128,128]{2,1,0:T(8,128)(2,1)}, bf16[32,32,128]{2,1,0:T(8,128)(2,1)}, bf16[32,32,128]{2,1,0:T(8,128)(2,1)}, f32[8,128]{1,0:T(8,128)}) custom-call(bf16[128,640]{1,0:T(8,128)(2,1)} %q_ref.3, bf16[128,640]{1,0:T(8,128)(2,1)} %k_ref.3, bf16[128,640]{1,0:T(8,128)(2,1)} %v_ref.1, ...), custom_call_target="tpu_custom_call" | custom-call | tf_op jit(solution)/shard_map/to_units/pallas_call | solution.py:392
  43.9 75.0 %unit_grads.1 = (bf16[32,128,256]{2,1,0:T(8,128)(2,1)}, f32[32,32,128]{2,1,0:T(8,128)}) custom-call(s32[7]{0:T(128)} %offset_ref.1, s32[150,2]{1,0:T(8,128)} %constant.4.clone.table_ref, s32[9]{0:T(128)} %constant.5.clone.start_ref, bf16[32,128,128]{2,1,0:T(8,128)(2,1)} %get-tuple-element.11.k_all, bf16[32,128,128]{2,1,0:T(8,128)(2,1)} %get-tuple-element.12.v_all, ...), custom_call_target="tpu_custom_call" | custom-call | tf_op jit(solution)/shard_map/unit_grads/pallas_call | solution.py:418
  118.9 64.4 %to_homes.1 = (bf16[128,640]{1,0:T(8,128)(2,1)}, bf16[128,640]{1,0:T(8,128)(2,1)}, bf16[128,640]{1,0:T(8,128)(2,1)}) custom-call(bf16[128,640]{1,0:T(8,128)(2,1)} %q_ref.3, bf16[128,640]{1,0:T(8,128)(2,1)} %k_ref.3, f32[1,640]{1,0:T(1,128)} %reshape.12.qgain_ref, f32[1,640]{1,0:T(1,128)} %reshape.13.kgain_ref, f32[8,128]{1,0:T(8,128)} %get-tuple-element.10.total_ref, ...), custom_call_target="tpu_custom_call" | custom-call | tf_op jit(solution)/shard_map/to_homes/pallas_call | solution.py:436
  183.3 1.6 copy.15
  184.9 1.6 copy.16
  186.5 1.6 copy.17

commit v2 on v1

v2 whole, which is shorter than its diff:
```python
import functools
import math

import jax
import jax.numpy as jnp
import numpy as np
from jax import lax
from jax.experimental import pallas as pl
from jax.experimental.pallas import tpu as pltpu
from jax.sharding import PartitionSpec as P

HEADS = 20
HD = 128
NB = 4
TOK = 128
BLK = 32
FRAMES = 32
FEAT = HEADS * HD
LOCAL_HEADS = 5
LOCAL = LOCAL_HEADS * HD
TILES = 8
EPSILON = 1e-06
NEG = -1e30
SCALE = HD ** (-0.5)
SCALE2 = SCALE * math.log2(math.e)
MESH = pl.DeviceIdType.MESH
VMEM_LIMIT = 60 * 1024 * 1024

UNITS = LOCAL_HEADS * NB


def my_unit():
    me = lax.axis_index("frame")
    slot = lax.rem(11 * (me // 2), 16)
    return me, slot < 2 * LOCAL_HEADS, slot // 2, 2 * lax.rem(slot, 2) + lax.rem(me, 2)


def block_table():
    rows = []
    for tile in range(TILES):
        for frame in range(max(0, 4 * tile - 4), min(FRAMES, 4 * tile + 8)):
            rows.append((frame, frame - 4 * tile + 4))
        for other in range(TILES):
            apart = other - tile
            if abs(apart) < 2:
                continue
            near = {2: (2, 3), 3: (3,), 4: (3, 4)}.get(abs(apart), (4,))
            for level in near:
                if len(near) == 1:
                    kind = 12
                else:
                    kind = 13 + {-4: 0, -2: 1, 2: 2, 4: 3}[apart] * 2 + (level - near[0])
                rows.append((32 + (level - 2) * 8 + other, kind))
        while len(rows) < (tile + 1) * MOST_BLOCKS:
            rows.append((4 * tile, KINDS - 1))
    return np.array(rows, np.int32)


KIND_FAR = [(-4, 3), (-4, 4), (-2, 2), (-2, 3), (2, 2), (2, 3), (4, 3), (4, 4)]
KINDS = 14 + len(KIND_FAR)
MOST_BLOCKS = 20
GROUP = 4


def enter(barrier_head=True):
    barrier = pltpu.get_barrier_semaphore()
    me = lax.axis_index("frame")
    row = lax.axis_index("head")
    for step in range(1, FRAMES):
        pl.semaphore_signal(
            barrier, inc=1, device_id={"frame": lax.rem(me + step, FRAMES)}, device_id_type=MESH
        )
    for step in range(1, 4):
        pl.semaphore_signal(
            barrier, inc=1, device_id={"head": lax.rem(row + step, 4)}, device_id_type=MESH
        )
    pl.semaphore_wait(barrier, FRAMES - 1 + 3)


def pair_rows(first, second):
    lane = lax.broadcasted_iota(jnp.int32, (TOK, TOK), 1)
    both = jnp.where(lane == 0, first, jnp.where(lane == 1, second, 0.0))
    return both.T[:8]


def pair_columns(rows):
    full = jnp.concatenate([rows, jnp.zeros((TOK - 8, TOK), jnp.float32)], axis=0).T
    return full[:, 0:1], full[:, 1:2]


def head_sum(stat, slots, send_sem, recv_sem):
    row = lax.axis_index("head")
    copies = []
    for step in range(1, 4):
        copy = pltpu.make_async_remote_copy(
            src_ref=stat,
            dst_ref=slots.at[step - 1],
            send_sem=send_sem.at[step - 1],
            recv_sem=recv_sem.at[step - 1],
            device_id={"head": lax.rem(row + step, 4)},
            device_id_type=MESH,
        )
        copy.start()
        copies.append(copy)
    return copies


def head_slice(head):
    return pl.ds(head * HD, HD)


def lanes(head):
    return pl.ds(pl.multiple_of(head * HD, HD), HD)


def send_kernel(
    q_ref, k_ref, v_ref, g_ref, qgain_ref, kgain_ref,
    k_all, v_all, q_all, g_all, total_ref,
    keys, queries, stat, slots,
    zsend, zrecv, vsend, gsend, ksend, qsend, vrecv, grecv, krecv, qrecv, vpass, kpass,
):
    me, is_unit, _, _ = my_unit()
    core = lax.rem(me, 2)
    chip = me // 2
    enter()

    def remote(src, dst_all, target, send_sem, recv_sem):
        return pltpu.make_async_remote_copy(
            src_ref=src, dst_ref=dst_all.at[me], send_sem=send_sem, recv_sem=recv_sem.at[me],
            device_id={"frame": target}, device_id_type=MESH,
        )

    def send(src, dst_all, target, send_sem, recv_sem):
        @pl.when(me != target)
        def _():
            remote(src, dst_all, target, send_sem, recv_sem).start()

        @pl.when(me == target)
        def _():
            pltpu.make_async_copy(src, dst_all.at[me], recv_sem.at[me]).start()

    def raw_parts(slot):
        head, half = slot // 2, lax.rem(slot, 2)
        base = 2 * lax.rem(3 * slot, 16)
        yield v_ref.at[:, lanes(head)], v_all, base + core, vsend.at[slot], vrecv
        for side in range(2):
            rows = pl.ds(pl.multiple_of((2 * half + side) * BLK, BLK), BLK)
            yield g_ref.at[rows, lanes(head)], g_all, base + side, gsend.at[2 * slot + side], grecv

    def normal_parts(slot):
        head, half = slot // 2, lax.rem(slot, 2)
        base = 2 * lax.rem(3 * slot, 16)
        yield keys.at[head], k_all, base + core, ksend.at[slot], krecv
        for side in range(2):
            rows = pl.ds(pl.multiple_of((2 * half + side) * BLK, BLK), BLK)
            yield queries.at[head, rows], q_all, base + side, qsend.at[2 * slot + side], qrecv

    @pl.loop(0, 2 * LOCAL_HEADS)
    def _(step):
        for part in raw_parts(lax.rem(step + chip, 2 * LOCAL_HEADS)):
            send(*part)

    def squares(ref):
        acc = jnp.zeros((TOK, HD), jnp.float32)
        for head in range(LOCAL_HEADS):
            part = ref[:, head_slice(head)].astype(jnp.float32)
            acc = acc + part * part
        return jnp.sum(acc, axis=1, keepdims=True)

    stat[...] = pair_rows(squares(q_ref), squares(k_ref))
    for copy in head_sum(stat, slots, zsend, zrecv):
        copy.wait()
    total = stat[...] + slots[0] + slots[1] + slots[2]
    total_ref[...] = total
    qsum, ksum = pair_columns(total)
    qrms = lax.rsqrt(qsum / FEAT + EPSILON)
    krms = lax.rsqrt(ksum / FEAT + EPSILON)
    for head in range(LOCAL_HEADS):
        part = k_ref[:, head_slice(head)].astype(jnp.float32)
        keys[head] = (part * krms * kgain_ref[head_slice(head)].reshape(1, HD)).astype(jnp.bfloat16)
        part = q_ref[:, head_slice(head)].astype(jnp.float32)
        queries[head] = (part * qrms * qgain_ref[head_slice(head)].reshape(1, HD)).astype(jnp.bfloat16)

    @pl.loop(0, 2 * LOCAL_HEADS)
    def _(step):
        for part in normal_parts(lax.rem(step + chip, 2 * LOCAL_HEADS)):
            send(*part)

    def forward(ref, step, send_sem, recv_sem):
        frame = lax.rem(me + 2 * step, FRAMES)
        return pltpu.make_async_remote_copy(
            src_ref=ref.at[frame], dst_ref=ref.at[frame], send_sem=send_sem.at[step],
            recv_sem=recv_sem.at[frame], device_id={"frame": me + 1 - 2 * core}, device_id_type=MESH,
        )

    def arrived(ref, frame, sem):
        pltpu.make_async_copy(ref.at[frame], ref.at[frame], sem.at[frame]).wait()

    @pl.when(is_unit)
    def _():
        for ref, ssem, rsem in ((v_all, vpass, vrecv), (k_all, kpass, krecv)):
            @pl.loop(0, FRAMES // 2)
            def _(step):
                arrived(ref, lax.rem(me + 2 * step, FRAMES), rsem)
                forward(ref, step, ssem, rsem).start()

        @pl.loop(0, FRAMES)
        def _(frame):
            arrived(g_all, frame, grecv)
            arrived(q_all, frame, qrecv)

        @pl.loop(0, FRAMES // 2)
        def _(step):
            frame = 2 * step + 1 - core
            arrived(v_all, frame, vrecv)
            arrived(k_all, frame, krecv)
            forward(v_all, step, vpass, vrecv).wait_send()
            forward(k_all, step, kpass, krecv).wait_send()

    @pl.loop(0, 2 * LOCAL_HEADS)
    def _(slot):
        for parts in (raw_parts(slot), normal_parts(slot)):
            for src, dst, target, ssem, rsem in parts:
                @pl.when(me != target)
                def _():
                    remote(src, dst, target, ssem, rsem).wait_send()


def dot(a, b, contract):
    return lax.dot_general(a, b, (contract, ((), ())), preferred_element_type=jnp.float32)


def unit_kernel(
    offset_ref, table_ref,
    k_all, v_all, q_all, g_all,
    dkv_keep, dkv_give, dq_all,
    kv, kt, w, acc, bias, tbuf, gbuf, dqt,
):
    me, is_unit, _, block = my_unit()
    core = lax.rem(me, 2)

    @pl.when(is_unit)
    def _():
        row_frame = lax.broadcasted_iota(jnp.int32, (TOK, TOK), 0) // BLK
        lane_frame = lax.broadcasted_iota(jnp.int32, (TOK, TOK), 1) // BLK
        zero = jnp.zeros((TOK, TOK), jnp.float32)
        hit1 = jnp.where(((row_frame - block - offset_ref[0]) & 3) < 2, 0.0, NEG)
        hit2 = jnp.where(((row_frame - block - offset_ref[1]) & 3) < 1, 0.0, NEG)

        @pl.loop(0, 12)
        def _(kind):
            d = jnp.abs(kind - 4 - lane_frame)
            bias[kind] = jnp.where(d < 2, 0.0, jnp.where(d < 4, hit1, hit2))

        bias[12] = zero
        bias[KINDS - 1] = zero + NEG
        for index, (apart, level) in enumerate(KIND_FAR):
            d = jnp.abs(4 * apart + row_frame - lane_frame)
            bias[13 + index] = jnp.where((d >= 2**level) & (d < 2 ** (level + 1)), 0.0, NEG)

        picks = [
            pl.multiple_of(((block + offset_ref[level - 1]) & 3) * BLK, BLK) for level in (2, 3, 4)
        ]

        @pl.loop(0, FRAMES)
        def _(frame):
            kv[pl.ds(pl.multiple_of(frame * TOK, TOK), TOK), 0:HD] = k_all[frame]
            kv[pl.ds(pl.multiple_of(frame * TOK, TOK), TOK), HD : 2 * HD] = v_all[frame]
            for index, pick in enumerate(picks):
                where = pl.multiple_of((FRAMES * NB + index * FRAMES + frame) * BLK, BLK)
                kv[pl.ds(where, BLK), 0:HD] = k_all[frame, pl.ds(pick, BLK)]
                kv[pl.ds(where, BLK), HD : 2 * HD] = v_all[frame, pl.ds(pick, BLK)]

        @pl.loop(0, 56)
        def _(blk):
            at = pl.ds(pl.multiple_of(blk * TOK, TOK), TOK)
            kt[blk] = kv[at, 0:HD].T
            acc[at, :] = jnp.zeros((TOK, 2 * HD), jnp.float32)

        @pl.loop(0, TILES)
        def _(tile):
            w[tile, 0:TOK, HD:] = jnp.zeros((TOK, HD), jnp.bfloat16)
            w[tile, TOK:, 0:HD] = jnp.zeros((TOK, HD), jnp.bfloat16)
            for part in range(4):
                w[tile, part * BLK : (part + 1) * BLK, 0:HD] = q_all[4 * tile + part]
                w[tile, TOK + part * BLK : TOK + (part + 1) * BLK, HD:] = g_all[4 * tile + part]

        @pl.loop(0, TILES)
        def _(tile):
            first = tile * MOST_BLOCKS
            blks = [table_ref[first + slot, 0] for slot in range(MOST_BLOCKS)]
            at = [pl.ds(pl.multiple_of(blk * TOK, TOK), TOK) for blk in blks]
            groups = [range(i, i + GROUP) for i in range(0, MOST_BLOCKS, GROUP)]
            peak = jnp.full((8, TOK), NEG, jnp.float32)
            for group in groups:
                rows = jnp.concatenate([kv[at[slot], :] for slot in group], axis=0)
                both = dot(rows, w[tile], ((1,), (1,)))
                for index, slot in enumerate(group):
                    part = both[index * TOK : (index + 1) * TOK]
                    t = part[:, 0:TOK] * SCALE2 + bias[table_ref[first + slot, 1]]
                    tbuf[slot] = t
                    gbuf[slot] = part[:, TOK:]
                    peak = jnp.maximum(peak, jnp.max(t.reshape(16, 8, TOK), axis=0))
            peak = jnp.max(peak, axis=0, keepdims=True)
            total = jnp.zeros((8, TOK), jnp.float32)
            weighted = jnp.zeros((8, TOK), jnp.float32)
            for slot in range(MOST_BLOCKS):
                weight = jnp.exp2(tbuf[slot] - peak)
                tbuf[slot] = weight
                total = total + jnp.sum(weight.reshape(16, 8, TOK), axis=0)
                weighted = weighted + jnp.sum((weight * gbuf[slot]).reshape(16, 8, TOK), axis=0)
            total = jnp.sum(total, axis=0, keepdims=True)
            inverse = 1.0 / total
            delta = jnp.sum(weighted, axis=0, keepdims=True) * inverse
            dqt[...] = jnp.zeros((HD, 2 * TOK), jnp.float32)
            for group in groups:
                lefts, lows, highs = [], [], []
                for slot in group:
                    probs = tbuf[slot] * inverse
                    grad = probs * (gbuf[slot] - delta)
                    high = grad.astype(jnp.bfloat16)
                    low = (grad - high.astype(jnp.float32)).astype(jnp.bfloat16)
                    lefts.append(jnp.concatenate([high, probs.astype(jnp.bfloat16)], axis=1))
                    lows.append(jnp.concatenate([high, low], axis=1))
                both = dot(jnp.concatenate(lefts, axis=0), w[tile], ((1,), (0,)))
                for index, slot in enumerate(group):
                    acc[at[slot], :] += both[index * TOK : (index + 1) * TOK]
                keyt = jnp.concatenate([kt[blks[slot]] for slot in group], axis=1)
                dqt[...] += dot(keyt, jnp.concatenate(lows, axis=0), ((1,), (0,)))

            dq = (dqt[:, 0:TOK] + dqt[:, TOK:]).T
            for part in range(4):
                dq_all[4 * tile + part] = dq[part * BLK : (part + 1) * BLK]

        def gathered(frame):
            for index, pick in enumerate(picks):
                home = pl.ds(pl.multiple_of(frame * TOK + pick, BLK), BLK)
                where = pl.multiple_of((FRAMES * NB + index * FRAMES + frame) * BLK, BLK)
                acc[home, :] += acc[pl.ds(where, BLK), :]
            return acc[pl.ds(pl.multiple_of(frame * TOK, TOK), TOK), :]

        @pl.loop(0, FRAMES // 2)
        def _(step):
            dkv_keep[step] = gathered(2 * step + core)
            dkv_give[step] = gathered(2 * step + 1 - core).astype(jnp.bfloat16)


def home_kernel(
    q_ref, k_ref, qgain_ref, kgain_ref, total_ref, dkv_keep, dkv_give, dq_all,
    dq_out, dk_out, dv_out,
    other, mixed, dkv_in, dq_in, kgrad, stat, slots,
    zsend, zrecv, give_send, give_recv, kvsend, qsend, kvrecv, qrecv,
):
    me, is_unit, head, block = my_unit()
    core = lax.rem(me, 2)
    slot = 2 * head + block // 2
    unit = head * NB + block
    enter()

    def order(step):
        x = lax.rem(me // 8 + step + 1, 4)
        y = lax.rem(me // 2 + step // 4 + step, 4)
        return x * 4 + y

    def give(step):
        return pltpu.make_async_remote_copy(
            src_ref=dkv_give.at[step], dst_ref=other.at[step], send_sem=give_send.at[step],
            recv_sem=give_recv.at[step], device_id={"frame": me + 1 - 2 * core}, device_id_type=MESH,
        )

    def send_dq(frame):
        return pltpu.make_async_remote_copy(
            src_ref=dq_all.at[frame], dst_ref=dq_in.at[unit], send_sem=qsend.at[frame],
            recv_sem=qrecv.at[unit], device_id={"frame": frame}, device_id_type=MESH,
        )

    def send_dkv(pair):
        return pltpu.make_async_remote_copy(
            src_ref=mixed.at[pair], dst_ref=dkv_in.at[slot], send_sem=kvsend.at[pair],
            recv_sem=kvrecv.at[slot], device_id={"frame": 2 * pair + core}, device_id_type=MESH,
        )

    @pl.when(is_unit)
    def _():
        @pl.loop(0, FRAMES // 2)
        def _(step):
            give(order(step)).start()

        @pl.loop(0, FRAMES)
        def _(step):
            frame = 2 * order(lax.rem(step, 16)) + lax.rem(core + step // 16, 2)

            @pl.when(frame != me)
            def _():
                send_dq(frame).start()

            @pl.when(frame == me)
            def _():
                pltpu.make_async_copy(dq_all.at[frame], dq_in.at[unit], qrecv.at[unit]).start()

        @pl.loop(0, FRAMES // 2)
        def _(step):
            pair = order(step)
            give(pair).wait_recv()
            mixed[pair] = (dkv_keep[pair] + other[pair].astype(jnp.float32)).astype(jnp.bfloat16)

            @pl.when(2 * pair + core != me)
            def _():
                send_dkv(pair).start()

            @pl.when(2 * pair + core == me)
            def _():
                pltpu.make_async_copy(mixed.at[pair], dkv_in.at[slot], kvrecv.at[slot]).start()

    qsum, ksum = pair_columns(total_ref[...])
    qrms = lax.rsqrt(qsum / FEAT + EPSILON)
    krms = lax.rsqrt(ksum / FEAT + EPSILON)
    qinner = jnp.zeros((TOK, HD), jnp.float32)
    kinner = jnp.zeros((TOK, HD), jnp.float32)
    for h in range(LOCAL_HEADS):
        for b in range(NB):
            u = h * NB + b
            pltpu.make_async_copy(dq_in.at[u], dq_in.at[u], qrecv.at[u]).wait()
        gained = qgain_ref[head_slice(h)].reshape(1, HD) * (dq_in[pl.ds(h * NB, NB)].reshape(TOK, HD) * SCALE)
        qinner = qinner + gained * q_ref[:, head_slice(h)].astype(jnp.float32)
        for u in (2 * h, 2 * h + 1):
            pltpu.make_async_copy(dkv_in.at[u], dkv_in.at[u], kvrecv.at[u]).wait()
        both = dkv_in[2 * h].astype(jnp.float32) + dkv_in[2 * h + 1].astype(jnp.float32)
        dv_out[:, head_slice(h)] = both[:, HD:].astype(jnp.bfloat16)
        gained = kgain_ref[head_slice(h)].reshape(1, HD) * (both[:, 0:HD] * SCALE)
        kgrad[:, head_slice(h)] = gained
        kinner = kinner + gained * k_ref[:, head_slice(h)].astype(jnp.float32)
    stat[...] = pair_rows(
        jnp.sum(qinner, axis=1, keepdims=True), jnp.sum(kinner, axis=1, keepdims=True)
    )
    for copy in head_sum(stat, slots, zsend, zrecv):
        copy.wait()
    qdot, kdot = pair_columns(stat[...] + slots[0] + slots[1] + slots[2])
    qfactor = qrms * qrms * qrms / FEAT * qdot
    kfactor = krms * krms * krms / FEAT * kdot
    for h in range(LOCAL_HEADS):
        gained = qgain_ref[head_slice(h)].reshape(1, HD) * (dq_in[pl.ds(h * NB, NB)].reshape(TOK, HD) * SCALE)
        raw = q_ref[:, head_slice(h)].astype(jnp.float32)
        dq_out[:, head_slice(h)] = (qrms * gained - qfactor * raw).astype(jnp.bfloat16)
        raw = k_ref[:, head_slice(h)].astype(jnp.float32)
        dk_out[:, head_slice(h)] = (krms * kgrad[:, head_slice(h)] - kfactor * raw).astype(jnp.bfloat16)

    @pl.when(is_unit)
    def _():
        @pl.loop(0, FRAMES)
        def _(frame):
            @pl.when(frame != me)
            def _():
                send_dq(frame).wait_send()

        @pl.loop(0, FRAMES // 2)
        def _(pair):
            give(pair).wait_send()

            @pl.when(2 * pair + core != me)
            def _():
                send_dkv(pair).wait_send()


def unit_call(window_offset, k_all, v_all, q_all, g_all):
    bf16, f32 = jnp.bfloat16, jnp.float32
    vmem = pl.BlockSpec(memory_space=pltpu.VMEM)
    smem = pl.BlockSpec(memory_space=pltpu.SMEM)
    shape = jax.ShapeDtypeStruct
    return pl.pallas_call(
        unit_kernel,
        name="unit_grads",
        out_shape=(
            shape((FRAMES // 2, TOK, 2 * HD), f32),
            shape((FRAMES // 2, TOK, 2 * HD), bf16),
            shape((FRAMES, BLK, HD), f32),
        ),
        in_specs=[smem] * 2 + [vmem] * 4,
        out_specs=[vmem] * 3,
        scratch_shapes=[
            pltpu.VMEM((56 * TOK, 2 * HD), bf16),
            pltpu.VMEM((56, HD, TOK), bf16),
            pltpu.VMEM((TILES, 2 * TOK, 2 * HD), bf16),
            pltpu.VMEM((56 * TOK, 2 * HD), f32),
            pltpu.VMEM((KINDS, TOK, TOK), f32),
            pltpu.VMEM((MOST_BLOCKS, TOK, TOK), f32),
            pltpu.VMEM((MOST_BLOCKS, TOK, TOK), f32),
            pltpu.VMEM((HD, 2 * TOK), f32),
        ],
        compiler_params=pltpu.CompilerParams(vmem_limit_bytes=VMEM_LIMIT),
    )(window_offset, jnp.asarray(block_table()), k_all, v_all, q_all, g_all)


def local(query_raw, key_raw, values, query_gain, key_gain, out_grad, window_offset):
    bf16, f32 = jnp.bfloat16, jnp.float32
    vmem = pl.BlockSpec(memory_space=pltpu.VMEM)
    hbm = pl.BlockSpec(memory_space=pl.ANY)
    dma = pltpu.SemaphoreType.DMA
    shape = jax.ShapeDtypeStruct
    k_all, v_all, q_all, g_all, total = pl.pallas_call(
        send_kernel,
        name="to_units",
        out_shape=(
            shape((FRAMES, TOK, HD), bf16),
            shape((FRAMES, TOK, HD), bf16),
            shape((FRAMES, BLK, HD), bf16),
            shape((FRAMES, BLK, HD), bf16),
            shape((8, TOK), f32),
        ),
        in_specs=[vmem] * 6,
        out_specs=[hbm] * 4 + [vmem],
        scratch_shapes=[
            pltpu.VMEM((LOCAL_HEADS, TOK, HD), bf16),
            pltpu.VMEM((LOCAL_HEADS, TOK, HD), bf16),
            pltpu.VMEM((8, TOK), f32),
            pltpu.VMEM((3, 8, TOK), f32),
            dma((3,)), dma((3,)),
            dma((UNITS // 2,)), dma((UNITS,)), dma((UNITS // 2,)), dma((UNITS,)),
            dma((FRAMES,)), dma((FRAMES,)), dma((FRAMES,)), dma((FRAMES,)),
            dma((FRAMES // 2,)), dma((FRAMES // 2,)),
        ],
        compiler_params=pltpu.CompilerParams(
            collective_id=0, has_side_effects=True, vmem_limit_bytes=VMEM_LIMIT
        ),
    )(query_raw, key_raw, values, out_grad, query_gain, key_gain)
    dkv_keep, dkv_give, dq_all = unit_call(window_offset, k_all, v_all, q_all, g_all)
    return pl.pallas_call(
        home_kernel,
        name="to_homes",
        out_shape=(shape((TOK, LOCAL), bf16),) * 3,
        in_specs=[vmem] * 6 + [hbm] * 2,
        out_specs=[vmem] * 3,
        scratch_shapes=[
            pltpu.VMEM((FRAMES // 2, TOK, 2 * HD), bf16),
            pltpu.VMEM((FRAMES // 2, TOK, 2 * HD), bf16),
            pltpu.VMEM((UNITS // 2, TOK, 2 * HD), bf16),
            pltpu.VMEM((UNITS, BLK, HD), f32),
            pltpu.VMEM((TOK, LOCAL), f32),
            pltpu.VMEM((8, TOK), f32),
            pltpu.VMEM((3, 8, TOK), f32),
            dma((3,)), dma((3,)),
            dma((FRAMES // 2,)), dma((FRAMES // 2,)),
            dma((FRAMES // 2,)), dma((FRAMES,)), dma((UNITS // 2,)), dma((UNITS,)),
        ],
        compiler_params=pltpu.CompilerParams(
            collective_id=1, has_side_effects=True, vmem_limit_bytes=VMEM_LIMIT
        ),
    )(query_raw, key_raw, query_gain, key_gain, total, dkv_keep, dkv_give, dq_all)


def solution(mesh):
    placed = (
        P("frame", "head"),
        P("frame", "head"),
        P("frame", "head"),
        P("head"),
        P("head"),
        P("frame", "head"),
        P(),
    )
    return jax.shard_map(
        local,
        mesh=mesh,
        in_specs=placed,
        out_specs=(P("frame", "head"), P("frame", "head"), P("frame", "head")),
        check_vma=False,
    )
```

time: 188 us -> 94.8 us (0.50)
  the two profiles are of different devices: /device:TPU:29 before, /device:TPU:0 now
where the time goes in v2:
time: 94.8 us; the launch traced here: 94.5 us
  Pallas kernels  89 us (94%)
  local copies, waits for them, and re-layouts  4.79 us (5%)
    pallas_call x1, Pallas kernels, local(): pl.pallas_call(home_kernel, name='to_homes', out_shape=(shape((TOK, LOCAL...  33.1 us
    pallas_call x1, Pallas kernels, local(): pl.pallas_call(send_kernel, name='to_units', out_shape=(shape((FRAMES, TO...  30.6 us
    pallas_call x1, Pallas kernels, unit_call(): pl.pallas_call(unit_kernel, name='unit_grads', out_shape=(shape((FRAMES /...  25.4 us
    unnamed x3, local copies, waits for them, and re-layouts  4.79 us

profile of v2, /device:TPU:0, one launch (start us, length us, event | category | flops | bytes accessed | tf_op | source)
XLA Modules:
  0.0 94.5 jit_solution(251948475792767451)
XLA Ops:
  0.6 30.6 %to_units.1 = (bf16[32,128,128]{2,1,0:T(8,128)(2,1)}, bf16[32,128,128]{2,1,0:T(8,128)(2,1)}, bf16[32,32,128]{2,1,0:T(8,128)(2,1)}, bf16[32,32,128]{2,1,0:T(8,128)(2,1)}, f32[8,128]{1,0:T(8,128)}) custom-call(bf16[128,640]{1,0:T(8,128)(2,1)} %q_ref.3, bf16[128,640]{1,0:T(8,128)(2,1)} %k_ref.3, bf16[128,640]{1,0:T(8,128)(2,1)} %v_ref.1, ...), custom_call_target="tpu_custom_call" | custom-call | tf_op jit(solution)/shard_map/to_units/pallas_call | solution.py:500
  31.2 25.4 %unit_grads.1 = (f32[16,128,256]{2,1,0:T(8,128)}, bf16[16,128,256]{2,1,0:T(8,128)(2,1)}, f32[32,32,128]{2,1,0:T(8,128)}) custom-call(s32[7]{0:T(128)} %offset_ref.1, s32[160,2]{1,0:T(8,128)} %constant.2.clone.table_ref, bf16[32,128,128]{2,1,0:T(8,128)(2,1)} %get-tuple-element.12.k_all, bf16[32,128,128]{2,1,0:T(8,128)(2,1)} %get-tuple-element.13.v_all, ...), custom_call_target="tpu_custom_call" | custom-call | tf_op jit(solution)/shard_map/unit_grads/pallas_call | solution.py:470
  56.6 33.1 %to_homes.1 = (bf16[128,640]{1,0:T(8,128)(2,1)}, bf16[128,640]{1,0:T(8,128)(2,1)}, bf16[128,640]{1,0:T(8,128)(2,1)}) custom-call(bf16[128,640]{1,0:T(8,128)(2,1)} %q_ref.3, bf16[128,640]{1,0:T(8,128)(2,1)} %k_ref.3, f32[640]{0:T(1024)} %qgain_ref.3, f32[640]{0:T(1024)} %kgain_ref.3, f32[8,128]{1,0:T(8,128)} %get-tuple-element.11.total_ref, ...), custom_call_target="tpu_custom_call" | custom-call | tf_op jit(solution)/shard_map/to_homes/pallas_call | solution.py:527
  89.7 1.6 %copy.14 = bf16[128,640]{1,0:T(8,128)(2,1)} copy(bf16[128,640]{1,0:T(8,128)(2,1)} %get-tuple-element.22) | data formatting | bytes 327680
  91.3 1.6 %copy.15 = bf16[128,640]{1,0:T(8,128)(2,1)} copy(bf16[128,640]{1,0:T(8,128)(2,1)} %get-tuple-element.23) | data formatting | bytes 327680
  92.9 1.6 %copy.16 = bf16[128,640]{1,0:T(8,128)(2,1)} copy(bf16[128,640]{1,0:T(8,128)(2,1)} %get-tuple-element.24) | data formatting | bytes 327680

commit v3 on v2

v3 whole, which is shorter than its diff:
```python
import functools
import math

import jax
import jax.numpy as jnp
from jax import lax
from jax.experimental import pallas as pl
from jax.experimental.pallas import tpu as pltpu
from jax.sharding import PartitionSpec as P

HEADS = 20
HD = 128
NB = 4
TOK = 128
BLK = 32
FRAMES = 32
FEAT = HEADS * HD
LOCAL_HEADS = 5
LOCAL = LOCAL_HEADS * HD
TILES = 8
EPSILON = 1e-06
NEG = -1e30
SCALE = HD ** (-0.5)
SCALE2 = SCALE * math.log2(math.e)
MESH = pl.DeviceIdType.MESH
VMEM_LIMIT = 60 * 1024 * 1024

UNITS = LOCAL_HEADS * NB


def my_unit():
    me = lax.axis_index("frame")
    slot = lax.rem(11 * (me // 2), 16)
    return me, slot < 2 * LOCAL_HEADS, slot // 2, 2 * lax.rem(slot, 2) + lax.rem(me, 2)


KIND_FAR = [(-4, 3), (-4, 4), (-2, 2), (-2, 3), (2, 2), (2, 3), (4, 3), (4, 4)]
OPEN = 12
SHUT = 13 + len(KIND_FAR)
KINDS = SHUT + 1
MOST_BLOCKS = 20
GROUP = 4


def far_kind(apart, level):
    return 13 + KIND_FAR.index((apart, level))


def far_block(level, other):
    return FRAMES + 8 * (level - 2) + other


def tile_blocks(tile):
    def pick(over, plain, wrapped):
        return plain + over * (wrapped - plain)

    found = [(4 * tile + part, 4 + part) for part in range(4)]
    for apart, first in ((1, 8), (7, 0)):
        other = (tile + apart) % TILES
        over = (tile + apart) // TILES
        over = over if apart == 1 else 1 - over
        for part in range(4):
            block = 4 * other + part
            if part == 0:
                block = pick(over, block, far_block(4, other))
            found.append((block, pick(over, first + part, OPEN if part == 0 else SHUT)))
    for apart in (2, 3, 4, 5, 6):
        other = (tile + apart) % TILES
        over = (tile + apart) // TILES
        if apart == 2:
            found.append((far_block(2 + 2 * over, other), pick(over, far_kind(2, 2), OPEN)))
            found.append((far_block(3, other), pick(over, far_kind(2, 3), SHUT)))
        elif apart == 3:
            found.append((far_block(3 + over, other), OPEN + 0 * over))
        elif apart == 4:
            for level in (3, 4):
                found.append((far_block(level, other), pick(over, far_kind(4, level), far_kind(-4, level))))
        elif apart == 5:
            found.append((far_block(4 - over, other), OPEN + 0 * over))
        else:
            found.append((far_block(4 - 2 * over, other), pick(over, OPEN, far_kind(-2, 2))))
            found.append((far_block(3, other), pick(over, SHUT, far_kind(-2, 3))))
    return found


def greet():
    barrier = pltpu.get_barrier_semaphore()
    me = lax.axis_index("frame")
    row = lax.axis_index("head")
    for step in range(1, FRAMES):
        pl.semaphore_signal(
            barrier, inc=1, device_id={"frame": lax.rem(me + step, FRAMES)}, device_id_type=MESH
        )
    for step in range(1, 4):
        pl.semaphore_signal(
            barrier, inc=1, device_id={"head": lax.rem(row + step, 4)}, device_id_type=MESH
        )


def all_here():
    pl.semaphore_wait(pltpu.get_barrier_semaphore(), FRAMES - 1 + 3)


def pair_rows(first, second):
    lane = lax.broadcasted_iota(jnp.int32, (TOK, TOK), 1)
    both = jnp.where(lane == 0, first, jnp.where(lane == 1, second, 0.0))
    return both.T[:8]


def pair_columns(rows):
    full = jnp.concatenate([rows, jnp.zeros((TOK - 8, TOK), jnp.float32)], axis=0).T
    return full[:, 0:1], full[:, 1:2]


def head_sum(stat, slots, send_sem, recv_sem):
    row = lax.axis_index("head")
    copies = []
    for step in range(1, 4):
        copy = pltpu.make_async_remote_copy(
            src_ref=stat,
            dst_ref=slots.at[step - 1],
            send_sem=send_sem.at[step - 1],
            recv_sem=recv_sem.at[step - 1],
            device_id={"head": lax.rem(row + step, 4)},
            device_id_type=MESH,
        )
        copy.start()
        copies.append(copy)
    return copies


def head_slice(head):
    return pl.ds(head * HD, HD)


def lanes(head):
    return pl.ds(pl.multiple_of(head * HD, HD), HD)


def dot(a, b, contract):
    return lax.dot_general(a, b, (contract, ((), ())), preferred_element_type=jnp.float32)


def frame_rows(frame, width=TOK):
    return pl.ds(pl.multiple_of(frame * width, width), width)


def main_kernel(
    offset_ref, q_ref, k_ref, v_ref, g_ref, qgain_ref, kgain_ref,
    qgrad, kgrad, vgrad, total_ref, inner_ref,
    keys, queries, stat, slots, stat2, slots2,
    kv, kt, w, acc, bias, tbuf, gbuf, dqt,
    dq_done, given, other, mixed, dkv_in, dq_in,
    zsend, zrecv, zsend2, zrecv2, vsend, gsend, ksend, qsend, vrecv, grecv, krecv, qrecv, vpass, kpass,
    give_send, give_recv, kvsend, dqsend, kvrecv, dqrecv,
):
    me, is_unit, my_head, block = my_unit()
    core = lax.rem(me, 2)
    chip = me // 2
    partner = me + 1 - 2 * core
    slot_id = 2 * my_head + block // 2
    unit = my_head * NB + block

    def squares(ref):
        sums = jnp.zeros((TOK, HD), jnp.float32)
        for head in range(LOCAL_HEADS):
            part = ref[:, head_slice(head)].astype(jnp.float32)
            sums = sums + part * part
        return jnp.sum(sums, axis=1, keepdims=True)

    greet()
    stat[...] = pair_rows(squares(q_ref), squares(k_ref))
    all_here()
    sums = head_sum(stat, slots, zsend, zrecv)

    def k_at(frame):
        return kv.at[frame_rows(frame), pl.ds(0, HD)]

    def v_at(frame):
        return kv.at[frame_rows(frame), pl.ds(HD, HD)]

    def q_at(frame):
        return w.at[frame // 4, frame_rows(lax.rem(frame, 4), BLK), pl.ds(0, HD)]

    def g_at(frame):
        return w.at[frame // 4, frame_rows(4 + lax.rem(frame, 4), BLK), pl.ds(HD, HD)]

    def remote(src, place, target, send_sem, recv_sem):
        return pltpu.make_async_remote_copy(
            src_ref=src, dst_ref=place(me), send_sem=send_sem, recv_sem=recv_sem.at[me],
            device_id={"frame": target}, device_id_type=MESH,
        )

    def send(src, place, target, send_sem, recv_sem):
        @pl.when(me != target)
        def _():
            remote(src, place, target, send_sem, recv_sem).start()

        @pl.when(me == target)
        def _():
            pltpu.make_async_copy(src, place(me), recv_sem.at[me]).start()

    def parts_of(slot, key_like, query_like, ksem, qsem, krec, qrec, k_place, q_place):
        head, half = slot // 2, lax.rem(slot, 2)
        base = 2 * lax.rem(3 * slot, 16)
        yield key_like(head), k_place, base + core, ksem.at[slot], krec
        for side in range(2):
            rows = frame_rows(2 * half + side, BLK)
            yield query_like(head, rows), q_place, base + side, qsem.at[2 * slot + side], qrec

    def raw_parts(slot):
        return parts_of(
            slot, lambda head: v_ref.at[:, lanes(head)], lambda head, rows: g_ref.at[rows, lanes(head)],
            vsend, gsend, vrecv, grecv, v_at, g_at,
        )

    def normal_parts(slot):
        return parts_of(
            slot, lambda head: keys.at[head], lambda head, rows: queries.at[head, rows],
            ksend, qsend, krecv, qrecv, k_at, q_at,
        )

    @pl.loop(0, 2 * LOCAL_HEADS)
    def _(step):
        for part in raw_parts(lax.rem(step + chip, 2 * LOCAL_HEADS)):
            send(*part)

    for copy in sums:
        copy.wait()
    total = stat[...] + slots[0] + slots[1] + slots[2]
    total_ref[...] = total
    qsum, ksum = pair_columns(total)
    qrms = lax.rsqrt(qsum / FEAT + EPSILON)
    krms = lax.rsqrt(ksum / FEAT + EPSILON)
    for head in range(LOCAL_HEADS):
        part = k_ref[:, head_slice(head)].astype(jnp.float32)
        keys[head] = (part * krms * kgain_ref[head_slice(head)].reshape(1, HD)).astype(jnp.bfloat16)
        part = q_ref[:, head_slice(head)].astype(jnp.float32)
        queries[head] = (part * qrms * qgain_ref[head_slice(head)].reshape(1, HD)).astype(jnp.bfloat16)

    @pl.loop(0, 2 * LOCAL_HEADS)
    def _(step):
        for part in normal_parts(lax.rem(step + chip, 2 * LOCAL_HEADS)):
            send(*part)

    def order(step):
        x = lax.rem(me // 8 + step + 1, 4)
        y = lax.rem(me // 2 + step // 4 + step, 4)
        return x * 4 + y

    def forward(place, step, send_sem, recv_sem):
        frame = lax.rem(me + 2 * step, FRAMES)
        return pltpu.make_async_remote_copy(
            src_ref=place(frame), dst_ref=place(frame), send_sem=send_sem.at[step],
            recv_sem=recv_sem.at[frame], device_id={"frame": partner}, device_id_type=MESH,
        )

    def arrived(place, frame, sem):
        pltpu.make_async_copy(place(frame), place(frame), sem.at[frame]).wait()

    def give(pair):
        return pltpu.make_async_remote_copy(
            src_ref=given.at[pair], dst_ref=other.at[pair], send_sem=give_send.at[pair],
            recv_sem=give_recv.at[pair], device_id={"frame": partner}, device_id_type=MESH,
        )

    def send_dq(frame):
        return pltpu.make_async_remote_copy(
            src_ref=dq_done.at[frame], dst_ref=dq_in.at[unit], send_sem=dqsend.at[frame],
            recv_sem=dqrecv.at[unit], device_id={"frame": frame}, device_id_type=MESH,
        )

    def send_dkv(pair):
        return pltpu.make_async_remote_copy(
            src_ref=mixed.at[pair], dst_ref=dkv_in.at[slot_id], send_sem=kvsend.at[pair],
            recv_sem=kvrecv.at[slot_id], device_id={"frame": 2 * pair + core}, device_id_type=MESH,
        )

    @pl.when(is_unit)
    def _():
        @pl.loop(0, FRAMES // 2)
        def _(step):
            arrived(v_at, lax.rem(me + 2 * step, FRAMES), vrecv)
            forward(v_at, step, vpass, vrecv).start()

        row_frame = lax.broadcasted_iota(jnp.int32, (TOK, TOK), 0) // BLK
        lane_frame = lax.broadcasted_iota(jnp.int32, (TOK, TOK), 1) // BLK
        zero = jnp.zeros((TOK, TOK), jnp.float32)
        hit1 = jnp.where(((row_frame - block - offset_ref[0]) & 3) < 2, 0.0, NEG)
        hit2 = jnp.where(((row_frame - block - offset_ref[1]) & 3) < 1, 0.0, NEG)

        @pl.loop(0, 12)
        def _(kind):
            d = jnp.abs(kind - 4 - lane_frame)
            bias[kind] = jnp.where(d < 2, 0.0, jnp.where(d < 4, hit1, hit2))

        bias[OPEN] = zero
        bias[SHUT] = zero + NEG
        for apart, level in KIND_FAR:
            d = jnp.abs(4 * apart + row_frame - lane_frame)
            bias[far_kind(apart, level)] = jnp.where((d >= 2**level) & (d < 2 ** (level + 1)), 0.0, NEG)

        @pl.loop(0, 56)
        def _(blk):
            acc[frame_rows(blk), :] = jnp.zeros((TOK, 2 * HD), jnp.float32)

        @pl.loop(0, TILES)
        def _(tile):
            w[tile, 0:TOK, HD:] = jnp.zeros((TOK, HD), jnp.bfloat16)
            w[tile, TOK:, 0:HD] = jnp.zeros((TOK, HD), jnp.bfloat16)

        @pl.loop(0, FRAMES // 2)
        def _(step):
            frame = lax.rem(me + 2 * step, FRAMES)
            arrived(k_at, frame, krecv)
            forward(k_at, step, kpass, krecv).start()
            kt[frame] = kv[frame_rows(frame), 0:HD].T

        @pl.loop(0, FRAMES)
        def _(frame):
            arrived(g_at, frame, grecv)
            arrived(q_at, frame, qrecv)

        @pl.loop(0, FRAMES // 2)
        def _(step):
            frame = lax.rem(me + 2 * step, FRAMES) + 1 - 2 * core
            arrived(v_at, frame, vrecv)
            arrived(k_at, frame, krecv)
            kt[frame] = kv[frame_rows(frame), 0:HD].T

        chosen = [(block + offset_ref[level - 1]) & 3 for level in (2, 3, 4)]
        is_chosen = [
            [(1 - jnp.minimum((pick - which) & 3, 1)).astype(jnp.float32) for which in range(NB)]
            for pick in chosen
        ]

        @pl.loop(0, FRAMES)
        def _(frame):
            blocks = [kv[frame_rows(NB * frame + which, BLK), :] for which in range(NB)]
            for index, weights in enumerate(is_chosen):
                picked = blocks[0] * weights[0].astype(jnp.bfloat16)
                for which in range(1, NB):
                    picked = picked + blocks[which] * weights[which].astype(jnp.bfloat16)
                kv[frame_rows(FRAMES * NB + index * FRAMES + frame, BLK), :] = picked

        @pl.loop(FRAMES, 56)
        def _(blk):
            kt[blk] = kv[frame_rows(blk), 0:HD].T

        @pl.loop(0, TILES)
        def _(tile):
            found = tile_blocks(tile)
            at = [frame_rows(blk) for blk, _ in found]
            groups = [range(i, i + GROUP) for i in range(0, MOST_BLOCKS, GROUP)]
            peak = jnp.full((8, TOK), NEG, jnp.float32)
            for group in groups:
                rows = jnp.concatenate([kv[at[slot], :] for slot in group], axis=0)
                both = dot(rows, w[tile], ((1,), (1,)))
                for index, slot in enumerate(group):
                    part = both[index * TOK : (index + 1) * TOK]
                    t = part[:, 0:TOK] * SCALE2 + bias[found[slot][1]]
                    tbuf[slot] = t
                    gbuf[slot] = part[:, TOK:]
                    peak = jnp.maximum(peak, jnp.max(t.reshape(16, 8, TOK), axis=0))
            peak = jnp.max(peak, axis=0, keepdims=True)
            total = jnp.zeros((8, TOK), jnp.float32)
            weighted = jnp.zeros((8, TOK), jnp.float32)
            for slot in range(MOST_BLOCKS):
                weight = jnp.exp2(tbuf[slot] - peak)
                tbuf[slot] = weight
                total = total + jnp.sum(weight.reshape(16, 8, TOK), axis=0)
                weighted = weighted + jnp.sum((weight * gbuf[slot]).reshape(16, 8, TOK), axis=0)
            total = jnp.sum(total, axis=0, keepdims=True)
            inverse = 1.0 / total
            delta = jnp.sum(weighted, axis=0, keepdims=True) * inverse
            dqt[...] = jnp.zeros((HD, 2 * TOK), jnp.float32)
            for group in groups:
                lefts, lows = [], []
                for slot in group:
                    probs = tbuf[slot] * inverse
                    grad = probs * (gbuf[slot] - delta)
                    high = grad.astype(jnp.bfloat16)
                    low = (grad - high.astype(jnp.float32)).astype(jnp.bfloat16)
                    lefts.append(jnp.concatenate([high, probs.astype(jnp.bfloat16)], axis=1))
                    lows.append(jnp.concatenate([high, low], axis=1))
                both = dot(jnp.concatenate(lefts, axis=0), w[tile], ((1,), (0,)))
                for index, slot in enumerate(group):
                    acc[at[slot], :] += both[index * TOK : (index + 1) * TOK]
                keyt = jnp.concatenate([kt[found[slot][0]] for slot in group], axis=1)
                dqt[...] += dot(keyt, jnp.concatenate(lows, axis=0), ((1,), (0,)))

            dq = (dqt[:, 0:TOK] + dqt[:, TOK:]).T.astype(jnp.bfloat16)
            for part in range(4):
                frame = 4 * tile + part
                dq_done[frame] = dq[part * BLK : (part + 1) * BLK]

                @pl.when(frame != me)
                def _():
                    send_dq(frame).start()

                @pl.when(frame == me)
                def _():
                    pltpu.make_async_copy(dq_done.at[frame], dq_in.at[unit], dqrecv.at[unit]).start()

        def gathered(frame):
            pieces = []
            for which in range(NB):
                piece = acc[frame_rows(NB * frame + which, BLK), :]
                for index, weights in enumerate(is_chosen):
                    far = acc[frame_rows(FRAMES * NB + index * FRAMES + frame, BLK), :]
                    piece = piece + far * weights[which]
                pieces.append(piece)
            return jnp.concatenate(pieces, axis=0)

        @pl.loop(0, FRAMES // 2)
        def _(step):
            pair = order(step)
            given[pair] = gathered(2 * pair + 1 - core).astype(jnp.bfloat16)
            give(pair).start()

        @pl.loop(0, FRAMES // 2)
        def _(step):
            pair = order(step)
            mine = gathered(2 * pair + core)
            give(pair).wait_recv()
            mixed[pair] = (mine + other[pair].astype(jnp.float32)).astype(jnp.bfloat16)

            @pl.when(2 * pair + core != me)
            def _():
                send_dkv(pair).start()

            @pl.when(2 * pair + core == me)
            def _():
                pltpu.make_async_copy(mixed.at[pair], dkv_in.at[slot_id], kvrecv.at[slot_id]).start()

    qinner = jnp.zeros((TOK, HD), jnp.float32)
    kinner = jnp.zeros((TOK, HD), jnp.float32)
    for h in range(LOCAL_HEADS):
        for b in range(NB):
            u = h * NB + b
            pltpu.make_async_copy(dq_in.at[u], dq_in.at[u], dqrecv.at[u]).wait()
        dq = dq_in[pl.ds(h * NB, NB)].astype(jnp.float32).reshape(TOK, HD)
        gained = qgain_ref[head_slice(h)].reshape(1, HD) * (dq * SCALE)
        qgrad[:, head_slice(h)] = gained
        qinner = qinner + gained * q_ref[:, head_slice(h)].astype(jnp.float32)
    for h in range(LOCAL_HEADS):
        for u in (2 * h, 2 * h + 1):
            pltpu.make_async_copy(dkv_in.at[u], dkv_in.at[u], kvrecv.at[u]).wait()
        both = dkv_in[2 * h].astype(jnp.float32) + dkv_in[2 * h + 1].astype(jnp.float32)
        vgrad[:, head_slice(h)] = both[:, HD:].astype(jnp.bfloat16)
        gained = kgain_ref[head_slice(h)].reshape(1, HD) * (both[:, 0:HD] * SCALE)
        kgrad[:, head_slice(h)] = gained
        kinner = kinner + gained * k_ref[:, head_slice(h)].astype(jnp.float32)
    stat2[...] = pair_rows(
        jnp.sum(qinner, axis=1, keepdims=True), jnp.sum(kinner, axis=1, keepdims=True)
    )
    for copy in head_sum(stat2, slots2, zsend2, zrecv2):
        copy.wait()
    inner_ref[...] = stat2[...] + slots2[0] + slots2[1] + slots2[2]

    @pl.loop(0, 2 * LOCAL_HEADS)
    def _(slot):
        for parts in (raw_parts(slot), normal_parts(slot)):
            for src, place, target, ssem, rsem in parts:
                @pl.when(me != target)
                def _():
                    remote(src, place, target, ssem, rsem).wait_send()

    @pl.when(is_unit)
    def _():
        @pl.loop(0, FRAMES)
        def _(frame):
            @pl.when(frame != me)
            def _():
                send_dq(frame).wait_send()

        @pl.loop(0, FRAMES // 2)
        def _(pair):
            forward(v_at, pair, vpass, vrecv).wait_send()
            forward(k_at, pair, kpass, krecv).wait_send()
            give(pair).wait_send()

            @pl.when(2 * pair + core != me)
            def _():
                send_dkv(pair).wait_send()


def finish_kernel(q_ref, k_ref, qgrad, kgrad, vgrad, total_ref, inner_ref, dq_out, dk_out, dv_out):
    qsum, ksum = pair_columns(total_ref[...])
    qdot, kdot = pair_columns(inner_ref[...])
    for raw, grad, square, inner, out in (
        (q_ref, qgrad, qsum, qdot, dq_out),
        (k_ref, kgrad, ksum, kdot, dk_out),
    ):
        rms = lax.rsqrt(square / FEAT + EPSILON)
        factor = rms * rms * rms / FEAT * inner
        for head in range(LOCAL_HEADS):
            at = head_slice(head)
            out[:, at] = (rms * grad[:, at] - factor * raw[:, at].astype(jnp.float32)).astype(jnp.bfloat16)
    dv_out[...] = vgrad[...]


def local(query_raw, key_raw, values, query_gain, key_gain, out_grad, window_offset):
    bf16, f32 = jnp.bfloat16, jnp.float32
    vmem = pl.BlockSpec(memory_space=pltpu.VMEM)
    smem = pl.BlockSpec(memory_space=pltpu.SMEM)
    dma = pltpu.SemaphoreType.DMA
    shape = jax.ShapeDtypeStruct
    half = FRAMES // 2
    qgrad, kgrad, vgrad, total, inner = pl.pallas_call(
        main_kernel,
        name="band_grads",
        out_shape=(
            shape((TOK, LOCAL), f32),
            shape((TOK, LOCAL), f32),
            shape((TOK, LOCAL), bf16),
            shape((8, TOK), f32),
            shape((8, TOK), f32),
        ),
        in_specs=[smem] + [vmem] * 6,
        out_specs=[vmem] * 5,
        scratch_shapes=[
            pltpu.VMEM((LOCAL_HEADS, TOK, HD), bf16),
            pltpu.VMEM((LOCAL_HEADS, TOK, HD), bf16),
            pltpu.VMEM((8, TOK), f32),
            pltpu.VMEM((3, 8, TOK), f32),
            pltpu.VMEM((8, TOK), f32),
            pltpu.VMEM((3, 8, TOK), f32),
            pltpu.VMEM((56 * TOK, 2 * HD), bf16),
            pltpu.VMEM((56, HD, TOK), bf16),
            pltpu.VMEM((TILES, 2 * TOK, 2 * HD), bf16),
            pltpu.VMEM((56 * TOK, 2 * HD), f32),
            pltpu.VMEM((KINDS, TOK, TOK), f32),
            pltpu.VMEM((MOST_BLOCKS, TOK, TOK), f32),
            pltpu.VMEM((MOST_BLOCKS, TOK, TOK), f32),
            pltpu.VMEM((HD, 2 * TOK), f32),
            pltpu.VMEM((FRAMES, BLK, HD), bf16),
            pltpu.VMEM((half, TOK, 2 * HD), bf16),
            pltpu.VMEM((half, TOK, 2 * HD), bf16),
            pltpu.VMEM((half, TOK, 2 * HD), bf16),
            pltpu.VMEM((UNITS // 2, TOK, 2 * HD), bf16),
            pltpu.VMEM((UNITS, BLK, HD), bf16),
            dma((3,)), dma((3,)), dma((3,)), dma((3,)),
            dma((UNITS // 2,)), dma((UNITS,)), dma((UNITS // 2,)), dma((UNITS,)),
            dma((FRAMES,)), dma((FRAMES,)), dma((FRAMES,)), dma((FRAMES,)),
            dma((half,)), dma((half,)), dma((half,)), dma((half,)),
            dma((half,)), dma((FRAMES,)), dma((UNITS // 2,)), dma((UNITS,)),
        ],
        compiler_params=pltpu.CompilerParams(
            collective_id=0, has_side_effects=True, vmem_limit_bytes=VMEM_LIMIT
        ),
    )(window_offset, query_raw, key_raw, values, out_grad, query_gain, key_gain)
    return pl.pallas_call(
        finish_kernel,
        name="norm_grads",
        out_shape=(shape((TOK, LOCAL), bf16),) * 3,
        in_specs=[vmem] * 7,
        out_specs=[vmem] * 3,
    )(query_raw, key_raw, qgrad, kgrad, vgrad, total, inner)


def solution(mesh):
    placed = (
        P("frame", "head"),
        P("frame", "head"),
        P("frame", "head"),
        P("head"),
        P("head"),
        P("frame", "head"),
        P(),
    )
    return jax.shard_map(
        local,
        mesh=mesh,
        in_specs=placed,
        out_specs=(P("frame", "head"), P("frame", "head"), P("frame", "head")),
        check_vma=False,
    )
```

time: 94.8 us -> 75.7 us (0.80)
  Pallas kernels: 89 us -> 74.4 us
  local copies, waits for them, and re-layouts: 4.79 us -> 0 us
    pallas_call x3 -> x2, Pallas kernels: 89 us -> 74.4 us  [the longest x1 72.1 us: local(): pl.pallas_call(main_kernel, name='band_grads', out_shape=(shape((TOK, LOC...]
    unnamed x3 -> x0, local copies, waits for them, and re-layouts: 4.79 us -> none
where the time goes in v3:
time: 75.7 us; the launch traced here: 75 us
  Pallas kernels  74.4 us (98%)
    pallas_call x1, Pallas kernels, local(): pl.pallas_call(main_kernel, name='band_grads', out_shape=(shape((TOK, LOC...  72.1 us
    pallas_call x1, Pallas kernels, local(): pl.pallas_call(finish_kernel, name='norm_grads', out_shape=(shape((TOK, L...  2.35 us

profile of v3, /device:TPU:0, one launch (start us, length us, event | category | flops | bytes accessed | tf_op | source)
XLA Modules:
  0.0 75.0 jit_solution(13606325826145657504)
XLA Ops:
  0.6 72.1 %band_grads.1 = (f32[128,640]{1,0:T(8,128)}, f32[128,640]{1,0:T(8,128)}, bf16[128,640]{1,0:T(8,128)(2,1)}, f32[8,128]{1,0:T(8,128)}, f32[8,128]{1,0:T(8,128)}) custom-call(s32[7]{0:T(128)} %offset_ref.1, bf16[128,640]{1,0:T(8,128)(2,1)} %q_ref.3, bf16[128,640]{1,0:T(8,128)(2,1)} %k_ref.3, bf16[128,640]{1,0:T(8,128)(2,1)} %v_ref.1, bf16[128,640]{1,0:T(8,128)(2,1)} %g_ref.1, ...), custom_call_target="tpu_custom_call" | custom-call | tf_op jit(solution)/shard_map/band_grads/pallas_call | solution.py:510
  72.7 2.4 %norm_grads.1 = (bf16[128,640]{1,0:T(8,128)(2,1)}, bf16[128,640]{1,0:T(8,128)(2,1)}, bf16[128,640]{1,0:T(8,128)(2,1)}) custom-call(bf16[128,640]{1,0:T(8,128)(2,1)} %q_ref.3, bf16[128,640]{1,0:T(8,128)(2,1)} %k_ref.3, f32[128,640]{1,0:T(8,128)} %get-tuple-element.8.qgrad, f32[128,640]{1,0:T(8,128)} %get-tuple-element.9.kgrad, ...), custom_call_target="tpu_custom_call" | custom-call | tf_op jit(solution)/shard_map/norm_grads/pallas_call | solution.py:553

commit v4 on v3

--- a/solution.py
+++ b/solution.py
@@ -39,48 +39,38 @@
 SHUT = 13 + len(KIND_FAR)
 KINDS = SHUT + 1
 MOST_BLOCKS = 20
-GROUP = 4
+TILE_BLOCKS = 7
 
 
 def far_kind(apart, level):
     return 13 + KIND_FAR.index((apart, level))
 
 
-def far_block(level, other):
-    return FRAMES + 8 * (level - 2) + other
-
-
-def tile_blocks(tile):
-    def pick(over, plain, wrapped):
+def blocks_between(apart, over):
+    def pick(plain, wrapped):
         return plain + over * (wrapped - plain)
 
-    found = [(4 * tile + part, 4 + part) for part in range(4)]
-    for apart, first in ((1, 8), (7, 0)):
-        other = (tile + apart) % TILES
-        over = (tile + apart) // TILES
-        over = over if apart == 1 else 1 - over
-        for part in range(4):
-            block = 4 * other + part
-            if part == 0:
-                block = pick(over, block, far_block(4, other))
-            found.append((block, pick(over, first + part, OPEN if part == 0 else SHUT)))
-    for apart in (2, 3, 4, 5, 6):
-        other = (tile + apart) % TILES
-        over = (tile + apart) // TILES
-        if apart == 2:
-            found.append((far_block(2 + 2 * over, other), pick(over, far_kind(2, 2), OPEN)))
-            found.append((far_block(3, other), pick(over, far_kind(2, 3), SHUT)))
-        elif apart == 3:
-            found.append((far_block(3 + over, other), OPEN + 0 * over))
-        elif apart == 4:
-            for level in (3, 4):
-                found.append((far_block(level, other), pick(over, far_kind(4, level), far_kind(-4, level))))
-        elif apart == 5:
-            found.append((far_block(4 - over, other), OPEN + 0 * over))
-        else:
-            found.append((far_block(4 - 2 * over, other), pick(over, OPEN, far_kind(-2, 2))))
-            found.append((far_block(3, other), pick(over, SHUT, far_kind(-2, 3))))
-    return found
+    if apart == 0:
+        return [(part, part, 4 + part) for part in range(4)]
+    if apart in (1, 7):
+        first, slot = (8, 4) if apart == 1 else (0, 8)
+        return [(slot, pick(0, 6), pick(first, OPEN))] + [
+            (slot + part, part, pick(first + part, SHUT)) for part in range(1, 4)
+        ]
+    if apart == 2:
+        return [(12, pick(4, 6), pick(far_kind(2, 2), OPEN)), (13, 5, pick(far_kind(2, 3), SHUT))]
+    if apart == 3:
+        return [(14, pick(5, 6), OPEN)]
+    if apart == 4:
+        return [(13 + level - 1, 2 + level, pick(far_kind(4, level), far_kind(-4, level))) for level in (3, 4)]
+    if apart == 5:
+        return [(17, pick(6, 5), OPEN)]
+    return [(18, pick(6, 4), pick(OPEN, far_kind(-2, 2))), (19, 5, pick(SHUT, far_kind(-2, 3)))]
+
+
+def wrapped(tile, apart):
+    over = (tile + apart) // TILES
+    return 1 - over if apart == 7 else over
 
 
 def greet():
@@ -145,18 +135,21 @@
     return pl.ds(pl.multiple_of(frame * width, width), width)
 
 
+def frame_block(frame):
+    return TILE_BLOCKS * (frame // 4) + lax.rem(frame, 4)
+
+
 def main_kernel(
     offset_ref, q_ref, k_ref, v_ref, g_ref, qgain_ref, kgain_ref,
     qgrad, kgrad, vgrad, total_ref, inner_ref,
     keys, queries, stat, slots, stat2, slots2,
-    kv, kt, w, acc, bias, tbuf, gbuf, dqt,
-    dq_done, given, other, mixed, dkv_in, dq_in,
+    kv, kt, w, acc, bias, tbuf, gbuf, grads, lows, peaks,
+    dq_done, given, other, keep, mixed, dkv_in, dq_in,
     zsend, zrecv, zsend2, zrecv2, vsend, gsend, ksend, qsend, vrecv, grecv, krecv, qrecv, vpass, kpass,
     give_send, give_recv, kvsend, dqsend, kvrecv, dqrecv,
 ):
     me, is_unit, my_head, block = my_unit()
     core = lax.rem(me, 2)
-    chip = me // 2
     partner = me + 1 - 2 * core
     slot_id = 2 * my_head + block // 2
     unit = my_head * NB + block
@@ -174,10 +167,10 @@
     sums = head_sum(stat, slots, zsend, zrecv)
 
     def k_at(frame):
-        return kv.at[frame_rows(frame), pl.ds(0, HD)]
+        return kv.at[frame_rows(frame_block(frame)), pl.ds(0, HD)]
 
     def v_at(frame):
-        return kv.at[frame_rows(frame), pl.ds(HD, HD)]
+        return kv.at[frame_rows(frame_block(frame)), pl.ds(HD, HD)]
 
     def q_at(frame):
         return w.at[frame // 4, frame_rows(lax.rem(frame, 4), BLK), pl.ds(0, HD)]
@@ -200,30 +193,41 @@
         def _():
             pltpu.make_async_copy(src, place(me), recv_sem.at[me]).start()
 
-    def parts_of(slot, key_like, query_like, ksem, qsem, krec, qrec, k_place, q_place):
-        head, half = slot // 2, lax.rem(slot, 2)
-        base = 2 * lax.rem(3 * slot, 16)
-        yield key_like(head), k_place, base + core, ksem.at[slot], krec
-        for side in range(2):
-            rows = frame_rows(2 * half + side, BLK)
-            yield query_like(head, rows), q_place, base + side, qsem.at[2 * slot + side], qrec
-
-    def raw_parts(slot):
-        return parts_of(
-            slot, lambda head: v_ref.at[:, lanes(head)], lambda head, rows: g_ref.at[rows, lanes(head)],
-            vsend, gsend, vrecv, grecv, v_at, g_at,
-        )
-
-    def normal_parts(slot):
-        return parts_of(
-            slot, lambda head: keys.at[head], lambda head, rows: queries.at[head, rows],
-            ksend, qsend, krecv, qrecv, k_at, q_at,
-        )
-
-    @pl.loop(0, 2 * LOCAL_HEADS)
-    def _(step):
-        for part in raw_parts(lax.rem(step + chip, 2 * LOCAL_HEADS)):
-            send(*part)
+    def key_part(slot, source, place, ssem, rsem):
+        return source(slot // 2), place, 2 * lax.rem(3 * slot, 16) + core, ssem.at[slot], rsem
+
+    def query_part(slot, side, source, place, ssem, rsem):
+        rows = frame_rows(2 * lax.rem(slot, 2) + side, BLK)
+        return source(slot // 2, rows), place, 2 * lax.rem(3 * slot, 16) + side, ssem.at[2 * slot + side], rsem
+
+    def parts_v(slot):
+        return (key_part(slot, lambda head: v_ref.at[:, lanes(head)], v_at, vsend, vrecv),)
+
+    def parts_g(slot):
+        return tuple(
+            query_part(slot, side, lambda head, rows: g_ref.at[rows, lanes(head)], g_at, gsend, grecv)
+            for side in range(2)
+        )
+
+    def parts_k(slot):
+        return (key_part(slot, lambda head: keys.at[head], k_at, ksend, krecv),)
+
+    def parts_q(slot):
+        return tuple(
+            query_part(slot, side, lambda head, rows: queries.at[head, rows], q_at, qsend, qrecv)
+            for side in range(2)
+        )
+
+    turn = me // 4 + me // 16
+
+    def send_all(*kinds):
+        @pl.loop(0, 2 * LOCAL_HEADS)
+        def _(step):
+            for kind in kinds:
+                for part in kind(lax.rem(step + turn, 2 * LOCAL_HEADS)):
+                    send(*part)
+
+    send_all(parts_v, parts_g)
 
     for copy in sums:
         copy.wait()
@@ -238,18 +242,11 @@
         part = q_ref[:, head_slice(head)].astype(jnp.float32)
         queries[head] = (part * qrms * qgain_ref[head_slice(head)].reshape(1, HD)).astype(jnp.bfloat16)
 
-    @pl.loop(0, 2 * LOCAL_HEADS)
-    def _(step):
-        for part in normal_parts(lax.rem(step + chip, 2 * LOCAL_HEADS)):
-            send(*part)
-
-    def order(step):
-        x = lax.rem(me // 8 + step + 1, 4)
-        y = lax.rem(me // 2 + step // 4 + step, 4)
-        return x * 4 + y
+    send_all(parts_q)
+    send_all(parts_k)
 
     def forward(place, step, send_sem, recv_sem):
-        frame = lax.rem(me + 2 * step, FRAMES)
+        frame = 2 * step + core
         return pltpu.make_async_remote_copy(
             src_ref=place(frame), dst_ref=place(frame), send_sem=send_sem.at[step],
             recv_sem=recv_sem.at[frame], device_id={"frame": partner}, device_id_type=MESH,
@@ -280,8 +277,9 @@
     def _():
         @pl.loop(0, FRAMES // 2)
         def _(step):
-            arrived(v_at, lax.rem(me + 2 * step, FRAMES), vrecv)
-            forward(v_at, step, vpass, vrecv).start()
+            pair = lax.rem(me // 2 + step, FRAMES // 2)
+            arrived(v_at, 2 * pair + core, vrecv)
+            forward(v_at, pair, vpass, vrecv).start()
 
         row_frame = lax.broadcasted_iota(jnp.int32, (TOK, TOK), 0) // BLK
         lane_frame = lax.broadcasted_iota(jnp.int32, (TOK, TOK), 1) // BLK
@@ -300,96 +298,137 @@
             d = jnp.abs(4 * apart + row_frame - lane_frame)
             bias[far_kind(apart, level)] = jnp.where((d >= 2**level) & (d < 2 ** (level + 1)), 0.0, NEG)
 
-        @pl.loop(0, 56)
-        def _(blk):
-            acc[frame_rows(blk), :] = jnp.zeros((TOK, 2 * HD), jnp.float32)
-
         @pl.loop(0, TILES)
         def _(tile):
             w[tile, 0:TOK, HD:] = jnp.zeros((TOK, HD), jnp.bfloat16)
             w[tile, TOK:, 0:HD] = jnp.zeros((TOK, HD), jnp.bfloat16)
-
-        @pl.loop(0, FRAMES // 2)
-        def _(step):
-            frame = lax.rem(me + 2 * step, FRAMES)
-            arrived(k_at, frame, krecv)
-            forward(k_at, step, kpass, krecv).start()
-            kt[frame] = kv[frame_rows(frame), 0:HD].T
+            peaks[tile] = jnp.full((8, TOK), NEG, jnp.float32)
 
         @pl.loop(0, FRAMES)
         def _(frame):
             arrived(g_at, frame, grecv)
             arrived(q_at, frame, qrecv)
 
-        @pl.loop(0, FRAMES // 2)
+        is_chosen = []
+        for level in (2, 3, 4):
+            pick = (block + offset_ref[level - 1]) & 3
+            is_chosen.append(
+                [(1 - jnp.minimum((pick - which) & 3, 1)).astype(jnp.float32) for which in range(NB)]
+            )
+
+        def at_step(step, body):
+            place = lax.rem(slot_id - step + 20, 10)
+
+            @pl.when(lax.rem(place, 5) != 4)
+            def _():
+                body(place - place // 5)
+
+        def pass_keys(tile):
+            for part in range(2):
+                arrived(k_at, 4 * tile + 2 * part + core, krecv)
+                forward(k_at, 2 * tile + part, kpass, krecv).start()
+
+        def score(tile):
+            for part in range(2):
+                frame = 4 * tile + 2 * part + 1 - core
+                arrived(v_at, frame, vrecv)
+                arrived(k_at, frame, krecv)
+            base = TILE_BLOCKS * tile
+            for part in range(4):
+                blocks = [kv[frame_rows(NB * (base + part) + which, BLK), :] for which in range(NB)]
+                for index, weights in enumerate(is_chosen):
+                    picked = blocks[0] * weights[0].astype(jnp.bfloat16)
+                    for which in range(1, NB):
+                        picked = picked + blocks[which] * weights[which].astype(jnp.bfloat16)
+                    kv[frame_rows(NB * (base + 4 + index) + part, BLK), :] = picked
+            for part in range(TILE_BLOCKS):
+                kt[base + part] = kv[frame_rows(base + part), 0:HD].T
+            for apart in range(TILES):
+                asker = lax.rem(tile + TILES - apart, TILES)
+                found = blocks_between(apart, wrapped(asker, apart))
+                rows = jnp.concatenate([kv[frame_rows(base + blk), :] for _, blk, _ in found], axis=0)
+                both = dot(rows, w[asker], ((1,), (1,)))
+                peak = peaks[asker]
+                for index, (slot, _, kind) in enumerate(found):
+                    part = both[index * TOK : (index + 1) * TOK]
+                    t = part[:, 0:TOK] * SCALE2 + bias[kind]
+                    tbuf[asker, slot] = t
+                    gbuf[asker, slot] = part[:, TOK:]
+                    peak = jnp.maximum(peak, jnp.max(t.reshape(16, 8, TOK), axis=0))
+                peaks[asker] = peak
+
+        at_step(0, pass_keys)
+
+        @pl.loop(0, 9)
         def _(step):
-            frame = lax.rem(me + 2 * step, FRAMES) + 1 - 2 * core
-            arrived(v_at, frame, vrecv)
-            arrived(k_at, frame, krecv)
-            kt[frame] = kv[frame_rows(frame), 0:HD].T
-
-        chosen = [(block + offset_ref[level - 1]) & 3 for level in (2, 3, 4)]
-        is_chosen = [
-            [(1 - jnp.minimum((pick - which) & 3, 1)).astype(jnp.float32) for which in range(NB)]
-            for pick in chosen
-        ]
-
-        @pl.loop(0, FRAMES)
-        def _(frame):
-            blocks = [kv[frame_rows(NB * frame + which, BLK), :] for which in range(NB)]
-            for index, weights in enumerate(is_chosen):
-                picked = blocks[0] * weights[0].astype(jnp.bfloat16)
-                for which in range(1, NB):
-                    picked = picked + blocks[which] * weights[which].astype(jnp.bfloat16)
-                kv[frame_rows(FRAMES * NB + index * FRAMES + frame, BLK), :] = picked
-
-        @pl.loop(FRAMES, 56)
-        def _(blk):
-            kt[blk] = kv[frame_rows(blk), 0:HD].T
+            at_step(step + 1, pass_keys)
+            at_step(step, score)
+
+        at_step(9, score)
 
         @pl.loop(0, TILES)
         def _(tile):
-            found = tile_blocks(tile)
-            at = [frame_rows(blk) for blk, _ in found]
-            groups = [range(i, i + GROUP) for i in range(0, MOST_BLOCKS, GROUP)]
-            peak = jnp.full((8, TOK), NEG, jnp.float32)
-            for group in groups:
-                rows = jnp.concatenate([kv[at[slot], :] for slot in group], axis=0)
-                both = dot(rows, w[tile], ((1,), (1,)))
-                for index, slot in enumerate(group):
-                    part = both[index * TOK : (index + 1) * TOK]
-                    t = part[:, 0:TOK] * SCALE2 + bias[found[slot][1]]
-                    tbuf[slot] = t
-                    gbuf[slot] = part[:, TOK:]
-                    peak = jnp.maximum(peak, jnp.max(t.reshape(16, 8, TOK), axis=0))
-            peak = jnp.max(peak, axis=0, keepdims=True)
+            peak = jnp.max(peaks[tile], axis=0, keepdims=True)
             total = jnp.zeros((8, TOK), jnp.float32)
             weighted = jnp.zeros((8, TOK), jnp.float32)
             for slot in range(MOST_BLOCKS):
-                weight = jnp.exp2(tbuf[slot] - peak)
-                tbuf[slot] = weight
+                weight = jnp.exp2(tbuf[tile, slot] - peak)
+                tbuf[tile, slot] = weight
                 total = total + jnp.sum(weight.reshape(16, 8, TOK), axis=0)
-                weighted = weighted + jnp.sum((weight * gbuf[slot]).reshape(16, 8, TOK), axis=0)
+                weighted = weighted + jnp.sum((weight * gbuf[tile, slot]).reshape(16, 8, TOK), axis=0)
             total = jnp.sum(total, axis=0, keepdims=True)
             inverse = 1.0 / total
             delta = jnp.sum(weighted, axis=0, keepdims=True) * inverse
-            dqt[...] = jnp.zeros((HD, 2 * TOK), jnp.float32)
-            for group in groups:
-                lefts, lows = [], []
-                for slot in group:
-                    probs = tbuf[slot] * inverse
-                    grad = probs * (gbuf[slot] - delta)
-                    high = grad.astype(jnp.bfloat16)
-                    low = (grad - high.astype(jnp.float32)).astype(jnp.bfloat16)
-                    lefts.append(jnp.concatenate([high, probs.astype(jnp.bfloat16)], axis=1))
-                    lows.append(jnp.concatenate([high, low], axis=1))
-                both = dot(jnp.concatenate(lefts, axis=0), w[tile], ((1,), (0,)))
-                for index, slot in enumerate(group):
-                    acc[at[slot], :] += both[index * TOK : (index + 1) * TOK]
-                keyt = jnp.concatenate([kt[found[slot][0]] for slot in group], axis=1)
-                dqt[...] += dot(keyt, jnp.concatenate(lows, axis=0), ((1,), (0,)))
-
-            dq = (dqt[:, 0:TOK] + dqt[:, TOK:]).T.astype(jnp.bfloat16)
+            for slot in range(MOST_BLOCKS):
+                probs = tbuf[tile, slot] * inverse
+                grad = probs * (gbuf[tile, slot] - delta)
+                high = grad.astype(jnp.bfloat16)
+                grads[tile, slot, :, 0:TOK] = high
+                grads[tile, slot, :, TOK:] = probs.astype(jnp.bfloat16)
+                lows[tile, slot] = (grad - high.astype(jnp.float32)).astype(jnp.bfloat16)
+
+        def key_grads(tile):
+            for index in range(3):
+                acc[4 + index] = jnp.zeros((TOK, 2 * HD), jnp.float32)
+            for apart in range(TILES):
+                asker = lax.rem(tile + TILES - apart, TILES)
+                found = blocks_between(apart, wrapped(asker, apart))
+                left = jnp.concatenate([grads[asker, slot] for slot, _, _ in found], axis=0)
+                both = dot(left, w[asker], ((1,), (0,)))
+                for index, (_, blk, _) in enumerate(found):
+                    piece = both[index * TOK : (index + 1) * TOK]
+                    if apart == 0:
+                        acc[blk] = piece
+                    else:
+                        acc[blk] += piece
+            for part in range(4):
+                rows = pl.ds(part * BLK, BLK)
+                for which in range(NB):
+                    piece = acc[part, which * BLK : (which + 1) * BLK]
+                    for index, weights in enumerate(is_chosen):
+                        piece = piece + acc[4 + index, rows] * weights[which]
+                    acc[part, which * BLK : (which + 1) * BLK] = piece
+            for part in range(2):
+                pair = 2 * tile + part
+                given[pair] = acc[2 * part + 1 - core].astype(jnp.bfloat16)
+                give(pair).start()
+                keep[pair] = acc[2 * part + core]
+
+        def query_grads(tile):
+            total = jnp.zeros((HD, 2 * TOK), jnp.float32)
+            for apart in range(TILES):
+                base = TILE_BLOCKS * lax.rem(tile + apart, TILES)
+                found = blocks_between(apart, wrapped(tile, apart))
+                keyt = jnp.concatenate([kt[base + blk] for _, blk, _ in found], axis=1)
+                right = jnp.concatenate(
+                    [
+                        jnp.concatenate([grads[tile, slot, :, 0:TOK], lows[tile, slot]], axis=1)
+                        for slot, _, _ in found
+                    ],
+                    axis=0,
+                )
+                total = total + dot(keyt, right, ((1,), (0,)))
+            dq = (total[:, 0:TOK] + total[:, TOK:]).T.astype(jnp.bfloat16)
             for part in range(4):
                 frame = 4 * tile + part
                 dq_done[frame] = dq[part * BLK : (part + 1) * BLK]
@@ -402,36 +441,33 @@
                 def _():
                     pltpu.make_async_copy(dq_done.at[frame], dq_in.at[unit], dqrecv.at[unit]).start()
 
-        def gathered(frame):
-            pieces = []
-            for which in range(NB):
-                piece = acc[frame_rows(NB * frame + which, BLK), :]
-                for index, weights in enumerate(is_chosen):
-                    far = acc[frame_rows(FRAMES * NB + index * FRAMES + frame, BLK), :]
-                    piece = piece + far * weights[which]
-                pieces.append(piece)
-            return jnp.concatenate(pieces, axis=0)
-
-        @pl.loop(0, FRAMES // 2)
+        def mix(tile):
+            for part in range(2):
+                pair = 2 * tile + part
+                give(pair).wait_recv()
+                mixed[pair] = (keep[pair] + other[pair].astype(jnp.float32)).astype(jnp.bfloat16)
+
+                @pl.when(2 * pair + core != me)
+                def _():
+                    send_dkv(pair).start()
+
+                @pl.when(2 * pair + core == me)
+                def _():
+                    pltpu.make_async_copy(mixed.at[pair], dkv_in.at[slot_id], kvrecv.at[slot_id]).start()
+
+        def turned(step):
+            return lax.rem(step + slot_id, TILES)
+
+        key_grads(turned(0))
+
+        @pl.loop(1, TILES)
         def _(step):
-            pair = order(step)
-            given[pair] = gathered(2 * pair + 1 - core).astype(jnp.bfloat16)
-            give(pair).start()
-
-        @pl.loop(0, FRAMES // 2)
-        def _(step):
-            pair = order(step)
-            mine = gathered(2 * pair + core)
-            give(pair).wait_recv()
-            mixed[pair] = (mine + other[pair].astype(jnp.float32)).astype(jnp.bfloat16)
-
-            @pl.when(2 * pair + core != me)
-            def _():
-                send_dkv(pair).start()
-
-            @pl.when(2 * pair + core == me)
-            def _():
-                pltpu.make_async_copy(mixed.at[pair], dkv_in.at[slot_id], kvrecv.at[slot_id]).start()
+            key_grads(turned(step))
+            mix(turned(step - 1))
+            query_grads(turned(step - 1))
+
+        mix(turned(TILES - 1))
+        query_grads(turned(TILES - 1))
 
     qinner = jnp.zeros((TOK, HD), jnp.float32)
     kinner = jnp.zeros((TOK, HD), jnp.float32)
@@ -460,7 +496,7 @@
 
     @pl.loop(0, 2 * LOCAL_HEADS)
     def _(slot):
-        for parts in (raw_parts(slot), normal_parts(slot)):
+        for parts in (parts_v(slot), parts_g(slot), parts_k(slot), parts_q(slot)):
             for src, place, target, ssem, rsem in parts:
                 @pl.when(me != target)
                 def _():
@@ -529,14 +565,17 @@
             pltpu.VMEM((56 * TOK, 2 * HD), bf16),
             pltpu.VMEM((56, HD, TOK), bf16),
             pltpu.VMEM((TILES, 2 * TOK, 2 * HD), bf16),
-            pltpu.VMEM((56 * TOK, 2 * HD), f32),
+            pltpu.VMEM((TILE_BLOCKS, TOK, 2 * HD), f32),
             pltpu.VMEM((KINDS, TOK, TOK), f32),
-            pltpu.VMEM((MOST_BLOCKS, TOK, TOK), f32),
-            pltpu.VMEM((MOST_BLOCKS, TOK, TOK), f32),
-            pltpu.VMEM((HD, 2 * TOK), f32),
+            pltpu.VMEM((TILES, MOST_BLOCKS, TOK, TOK), f32),
+            pltpu.VMEM((TILES, MOST_BLOCKS, TOK, TOK), f32),
+            pltpu.VMEM((TILES, MOST_BLOCKS, TOK, 2 * TOK), bf16),
+            pltpu.VMEM((TILES, MOST_BLOCKS, TOK, TOK), bf16),
+            pltpu.VMEM((TILES, 8, TOK), f32),
             pltpu.VMEM((FRAMES, BLK, HD), bf16),
             pltpu.VMEM((half, TOK, 2 * HD), bf16),
             pltpu.VMEM((half, TOK, 2 * HD), bf16),
+            pltpu.VMEM((half, TOK, 2 * HD), f32),
             pltpu.VMEM((half, TOK, 2 * HD), bf16),
             pltpu.VMEM((UNITS // 2, TOK, 2 * HD), bf16),
             pltpu.VMEM((UNITS, BLK, HD), bf16),

time: 75.7 us -> 76.4 us (level)
  Pallas kernels: 74.4 us -> 75.2 us
    pallas_call x1, Pallas kernels: 72.1 us -> 72.8 us  [local(): pl.pallas_call(main_kernel, name='band_grads', out_shape=(shape((TOK, LOC...]
where the time goes in v4:
time: 76.4 us; the launch traced here: 75.8 us
  Pallas kernels  75.2 us (98%)
    pallas_call x1, Pallas kernels, local(): pl.pallas_call(main_kernel, name='band_grads', out_shape=(shape((TOK, LOC...  72.8 us
    pallas_call x1, Pallas kernels, local(): pl.pallas_call(finish_kernel, name='norm_grads', out_shape=(shape((TOK, L...  2.35 us

profile of v4, /device:TPU:0, one launch (start us, length us, event | category | flops | bytes accessed | tf_op | source)
XLA Modules:
  0.0 75.8 jit_solution(6916387334583258868)
XLA Ops:
  0.6 72.8 %band_grads.1 = (f32[128,640]{1,0:T(8,128)}, f32[128,640]{1,0:T(8,128)}, bf16[128,640]{1,0:T(8,128)(2,1)}, f32[8,128]{1,0:T(8,128)}, f32[8,128]{1,0:T(8,128)}) custom-call(s32[7]{0:T(128)} %offset_ref.1, bf16[128,640]{1,0:T(8,128)(2,1)} %q_ref.3, bf16[128,640]{1,0:T(8,128)(2,1)} %k_ref.3, bf16[128,640]{1,0:T(8,128)(2,1)} %v_ref.1, bf16[128,640]{1,0:T(8,128)(2,1)} %g_ref.1, ...), custom_call_target="tpu_custom_call" | custom-call | tf_op jit(solution)/shard_map/band_grads/pallas_call | solution.py:546
  73.5 2.4 %norm_grads.1 = (bf16[128,640]{1,0:T(8,128)(2,1)}, bf16[128,640]{1,0:T(8,128)(2,1)}, bf16[128,640]{1,0:T(8,128)(2,1)}) custom-call(bf16[128,640]{1,0:T(8,128)(2,1)} %q_ref.3, bf16[128,640]{1,0:T(8,128)(2,1)} %k_ref.3, f32[128,640]{1,0:T(8,128)} %get-tuple-element.8.qgrad, f32[128,640]{1,0:T(8,128)} %get-tuple-element.9.kgrad, ...), custom_call_target="tpu_custom_call" | custom-call | tf_op jit(solution)/shard_map/norm_grads/pallas_call | solution.py:592

commit v5 on v4

--- a/solution.py
+++ b/solution.py
@@ -34,16 +34,17 @@
     return me, slot < 2 * LOCAL_HEADS, slot // 2, 2 * lax.rem(slot, 2) + lax.rem(me, 2)
 
 
-KIND_FAR = [(-4, 3), (-4, 4), (-2, 2), (-2, 3), (2, 2), (2, 3), (4, 3), (4, 4)]
-OPEN = 12
-SHUT = 13 + len(KIND_FAR)
+KIND_FAR = [(-4, 3), (-4, 4), (-2, 2), (-2, 3), (2, 2), (2, 3), (4, 3), (4, 4), (-1, 2), (1, 2), (-1, 1), (1, 1)]
+OPEN = 6
+SHUT = OPEN + 1 + len(KIND_FAR)
 KINDS = SHUT + 1
-MOST_BLOCKS = 20
-TILE_BLOCKS = 7
+MOST_BLOCKS = 18
+TILE_BLOCKS = 8
+EARLY_VALUES = 10
 
 
 def far_kind(apart, level):
-    return 13 + KIND_FAR.index((apart, level))
+    return OPEN + 1 + KIND_FAR.index((apart, level))
 
 
 def blocks_between(apart, over):
@@ -51,21 +52,28 @@
         return plain + over * (wrapped - plain)
 
     if apart == 0:
-        return [(part, part, 4 + part) for part in range(4)]
-    if apart in (1, 7):
-        first, slot = (8, 4) if apart == 1 else (0, 8)
-        return [(slot, pick(0, 6), pick(first, OPEN))] + [
-            (slot + part, part, pick(first + part, SHUT)) for part in range(1, 4)
+        return [(part, part, 1 + part) for part in range(4)]
+    if apart == 1:
+        return [
+            (4, pick(0, 6), pick(5, OPEN)),
+            (5, 4, pick(far_kind(1, 2), SHUT)),
+            (6, 7, pick(far_kind(1, 1), SHUT)),
+        ]
+    if apart == 7:
+        return [
+            (7, pick(3, 6), pick(0, OPEN)),
+            (8, 4, pick(far_kind(-1, 2), SHUT)),
+            (9, 7, pick(far_kind(-1, 1), SHUT)),
         ]
     if apart == 2:
-        return [(12, pick(4, 6), pick(far_kind(2, 2), OPEN)), (13, 5, pick(far_kind(2, 3), SHUT))]
+        return [(10, pick(4, 6), pick(far_kind(2, 2), OPEN)), (11, 5, pick(far_kind(2, 3), SHUT))]
     if apart == 3:
-        return [(14, pick(5, 6), OPEN)]
+        return [(12, pick(5, 6), OPEN)]
     if apart == 4:
-        return [(13 + level - 1, 2 + level, pick(far_kind(4, level), far_kind(-4, level))) for level in (3, 4)]
+        return [(10 + level, 2 + level, pick(far_kind(4, level), far_kind(-4, level))) for level in (3, 4)]
     if apart == 5:
-        return [(17, pick(6, 5), OPEN)]
-    return [(18, pick(6, 4), pick(OPEN, far_kind(-2, 2))), (19, 5, pick(SHUT, far_kind(-2, 3)))]
+        return [(15, pick(6, 5), OPEN)]
+    return [(16, pick(6, 4), pick(OPEN, far_kind(-2, 2))), (17, 5, pick(SHUT, far_kind(-2, 3)))]
 
 
 def wrapped(tile, apart):
@@ -143,7 +151,7 @@
     offset_ref, q_ref, k_ref, v_ref, g_ref, qgain_ref, kgain_ref,
     qgrad, kgrad, vgrad, total_ref, inner_ref,
     keys, queries, stat, slots, stat2, slots2,
-    kv, kt, w, acc, bias, tbuf, gbuf, grads, lows, peaks,
+    kv, kt, w, acc, bias, tbuf, gbuf, grads, lows, peaks, totals, weighteds,
     dq_done, given, other, keep, mixed, dkv_in, dq_in,
     zsend, zrecv, zsend2, zrecv2, vsend, gsend, ksend, qsend, vrecv, grecv, krecv, qrecv, vpass, kpass,
     give_send, give_recv, kvsend, dqsend, kvrecv, dqrecv,
@@ -220,14 +228,15 @@
 
     turn = me // 4 + me // 16
 
-    def send_all(*kinds):
-        @pl.loop(0, 2 * LOCAL_HEADS)
+    def send_steps(first, last, *kinds):
+        @pl.loop(first, last)
         def _(step):
             for kind in kinds:
                 for part in kind(lax.rem(step + turn, 2 * LOCAL_HEADS)):
                     send(*part)
 
-    send_all(parts_v, parts_g)
+    send_steps(0, 2 * LOCAL_HEADS, parts_g)
+    send_steps(0, EARLY_VALUES, parts_v)
 
     for copy in sums:
         copy.wait()
@@ -242,8 +251,8 @@
         part = q_ref[:, head_slice(head)].astype(jnp.float32)
         queries[head] = (part * qrms * qgain_ref[head_slice(head)].reshape(1, HD)).astype(jnp.bfloat16)
 
-    send_all(parts_q)
-    send_all(parts_k)
+    send_steps(0, 2 * LOCAL_HEADS, parts_k)
+    send_steps(0, 2 * LOCAL_HEADS, parts_q)
 
     def forward(place, step, send_sem, recv_sem):
         frame = 2 * step + core
@@ -275,46 +284,31 @@
 
     @pl.when(is_unit)
     def _():
-        @pl.loop(0, FRAMES // 2)
-        def _(step):
-            pair = lax.rem(me // 2 + step, FRAMES // 2)
-            arrived(v_at, 2 * pair + core, vrecv)
-            forward(v_at, pair, vpass, vrecv).start()
-
         row_frame = lax.broadcasted_iota(jnp.int32, (TOK, TOK), 0) // BLK
         lane_frame = lax.broadcasted_iota(jnp.int32, (TOK, TOK), 1) // BLK
         zero = jnp.zeros((TOK, TOK), jnp.float32)
         hit1 = jnp.where(((row_frame - block - offset_ref[0]) & 3) < 2, 0.0, NEG)
         hit2 = jnp.where(((row_frame - block - offset_ref[1]) & 3) < 1, 0.0, NEG)
 
-        @pl.loop(0, 12)
+        @pl.loop(0, OPEN)
         def _(kind):
-            d = jnp.abs(kind - 4 - lane_frame)
+            d = jnp.abs(kind - 1 - lane_frame)
             bias[kind] = jnp.where(d < 2, 0.0, jnp.where(d < 4, hit1, hit2))
 
         bias[OPEN] = zero
         bias[SHUT] = zero + NEG
         for apart, level in KIND_FAR:
-            d = jnp.abs(4 * apart + row_frame - lane_frame)
-            bias[far_kind(apart, level)] = jnp.where((d >= 2**level) & (d < 2 ** (level + 1)), 0.0, NEG)
+            frame = row_frame // 2 + 1 if level == 1 else row_frame
+            d = jnp.abs(4 * apart + frame - lane_frame)
+            meets = (d >= 2**level) & (d < 2 ** (level + 1))
+            if level == 2 and abs(apart) == 1:
+                meets = meets & (row_frame != (0 if apart == 1 else 3))
+            bias[far_kind(apart, level)] = jnp.where(meets, 0.0, NEG)
 
         @pl.loop(0, TILES)
         def _(tile):
             w[tile, 0:TOK, HD:] = jnp.zeros((TOK, HD), jnp.bfloat16)
             w[tile, TOK:, 0:HD] = jnp.zeros((TOK, HD), jnp.bfloat16)
-            peaks[tile] = jnp.full((8, TOK), NEG, jnp.float32)
-
-        @pl.loop(0, FRAMES)
-        def _(frame):
-            arrived(g_at, frame, grecv)
-            arrived(q_at, frame, qrecv)
-
-        is_chosen = []
-        for level in (2, 3, 4):
-            pick = (block + offset_ref[level - 1]) & 3
-            is_chosen.append(
-                [(1 - jnp.minimum((pick - which) & 3, 1)).astype(jnp.float32) for which in range(NB)]
-            )
 
         def at_step(step, body):
             place = lax.rem(slot_id - step + 20, 10)
@@ -322,6 +316,22 @@
             @pl.when(lax.rem(place, 5) != 4)
             def _():
                 body(place - place // 5)
+
+        def pass_values(tile):
+            for part in range(2):
+                arrived(v_at, 4 * tile + 2 * part + core, vrecv)
+                forward(v_at, 2 * tile + part, vpass, vrecv).start()
+
+        @pl.loop(0, 10)
+        def _(step):
+            at_step(step, pass_values)
+
+        def chosen(level, after):
+            pick = (block + offset_ref[level - 1] + after) & 3
+            return [(1 - jnp.minimum((pick - which) & 3, 1)).astype(jnp.float32) for which in range(NB)]
+
+        moves = [(4 + index, part, part, chosen(2 + index, 0)) for index in range(3) for part in range(4)]
+        moves += [(7, 2 * part + after, 1 + part, chosen(1, after)) for part in range(2) for after in range(2)]
 
         def pass_keys(tile):
             for part in range(2):
@@ -334,13 +344,12 @@
                 arrived(v_at, frame, vrecv)
                 arrived(k_at, frame, krecv)
             base = TILE_BLOCKS * tile
-            for part in range(4):
-                blocks = [kv[frame_rows(NB * (base + part) + which, BLK), :] for which in range(NB)]
-                for index, weights in enumerate(is_chosen):
-                    picked = blocks[0] * weights[0].astype(jnp.bfloat16)
-                    for which in range(1, NB):
-                        picked = picked + blocks[which] * weights[which].astype(jnp.bfloat16)
-                    kv[frame_rows(NB * (base + 4 + index) + part, BLK), :] = picked
+            for to, place, frame, weights in moves:
+                picked = kv[frame_rows(NB * (base + frame), BLK), :] * weights[0].astype(jnp.bfloat16)
+                for which in range(1, NB):
+                    rows = frame_rows(NB * (base + frame) + which, BLK)
+                    picked = picked + kv[rows, :] * weights[which].astype(jnp.bfloat16)
+                kv[frame_rows(NB * (base + to) + place, BLK), :] = picked
             for part in range(TILE_BLOCKS):
                 kt[base + part] = kv[frame_rows(base + part), 0:HD].T
             for apart in range(TILES):
@@ -348,39 +357,42 @@
                 found = blocks_between(apart, wrapped(asker, apart))
                 rows = jnp.concatenate([kv[frame_rows(base + blk), :] for _, blk, _ in found], axis=0)
                 both = dot(rows, w[asker], ((1,), (1,)))
-                peak = peaks[asker]
                 for index, (slot, _, kind) in enumerate(found):
                     part = both[index * TOK : (index + 1) * TOK]
-                    t = part[:, 0:TOK] * SCALE2 + bias[kind]
-                    tbuf[asker, slot] = t
+                    t = (part[:, 0:TOK] * SCALE2 + bias[kind]).reshape(16, 8, TOK)
+                    grad = part[:, TOK:].reshape(16, 8, TOK)
+                    peak = jnp.max(t, axis=0)
+                    weight = jnp.exp2(t - peak)
+                    tbuf[asker, slot] = weight.reshape(TOK, TOK)
                     gbuf[asker, slot] = part[:, TOK:]
-                    peak = jnp.maximum(peak, jnp.max(t.reshape(16, 8, TOK), axis=0))
-                peaks[asker] = peak
-
-        at_step(0, pass_keys)
-
-        @pl.loop(0, 9)
+                    peaks[asker, slot] = peak
+                    totals[asker, slot] = jnp.sum(weight, axis=0)
+                    weighteds[asker, slot] = jnp.sum(weight * grad, axis=0)
+
+        @pl.loop(0, 10)
         def _(step):
-            at_step(step + 1, pass_keys)
+            at_step(step, pass_keys)
+
+        @pl.loop(0, FRAMES)
+        def _(frame):
+            arrived(g_at, frame, grecv)
+            arrived(q_at, frame, qrecv)
+
+        @pl.loop(0, 10)
+        def _(step):
             at_step(step, score)
-
-        at_step(9, score)
 
         @pl.loop(0, TILES)
         def _(tile):
-            peak = jnp.max(peaks[tile], axis=0, keepdims=True)
-            total = jnp.zeros((8, TOK), jnp.float32)
-            weighted = jnp.zeros((8, TOK), jnp.float32)
+            peak = jnp.max(jnp.max(peaks[tile], axis=0), axis=0, keepdims=True)
+            factor = jnp.exp2(peaks[tile] - peak)
+            total = jnp.sum(jnp.sum(totals[tile] * factor, axis=0), axis=0, keepdims=True)
+            weighted = jnp.sum(jnp.sum(weighteds[tile] * factor, axis=0), axis=0, keepdims=True)
+            inverse = 1.0 / total
+            delta = weighted * inverse
+            factor = factor * inverse
             for slot in range(MOST_BLOCKS):
-                weight = jnp.exp2(tbuf[tile, slot] - peak)
-                tbuf[tile, slot] = weight
-                total = total + jnp.sum(weight.reshape(16, 8, TOK), axis=0)
-                weighted = weighted + jnp.sum((weight * gbuf[tile, slot]).reshape(16, 8, TOK), axis=0)
-            total = jnp.sum(total, axis=0, keepdims=True)
-            inverse = 1.0 / total
-            delta = jnp.sum(weighted, axis=0, keepdims=True) * inverse
-            for slot in range(MOST_BLOCKS):
-                probs = tbuf[tile, slot] * inverse
+                probs = (tbuf[tile, slot].reshape(16, 8, TOK) * factor[slot]).reshape(TOK, TOK)
                 grad = probs * (gbuf[tile, slot] - delta)
                 high = grad.astype(jnp.bfloat16)
                 grads[tile, slot, :, 0:TOK] = high
@@ -388,8 +400,8 @@
                 lows[tile, slot] = (grad - high.astype(jnp.float32)).astype(jnp.bfloat16)
 
         def key_grads(tile):
-            for index in range(3):
-                acc[4 + index] = jnp.zeros((TOK, 2 * HD), jnp.float32)
+            for index in range(4, TILE_BLOCKS):
+                acc[index] = jnp.zeros((TOK, 2 * HD), jnp.float32)
             for apart in range(TILES):
                 asker = lax.rem(tile + TILES - apart, TILES)
                 found = blocks_between(apart, wrapped(asker, apart))
@@ -401,13 +413,13 @@
                         acc[blk] = piece
                     else:
                         acc[blk] += piece
-            for part in range(4):
-                rows = pl.ds(part * BLK, BLK)
+            for frame in range(4):
                 for which in range(NB):
-                    piece = acc[part, which * BLK : (which + 1) * BLK]
-                    for index, weights in enumerate(is_chosen):
-                        piece = piece + acc[4 + index, rows] * weights[which]
-                    acc[part, which * BLK : (which + 1) * BLK] = piece
+                    piece = acc[frame, which * BLK : (which + 1) * BLK]
+                    for source, place, target, weights in moves:
+                        if target == frame:
+                            piece = piece + acc[source, place * BLK : (place + 1) * BLK] * weights[which]
+                    acc[frame, which * BLK : (which + 1) * BLK] = piece
             for part in range(2):
                 pair = 2 * tile + part
                 given[pair] = acc[2 * part + 1 - core].astype(jnp.bfloat16)
@@ -456,7 +468,8 @@
                     pltpu.make_async_copy(mixed.at[pair], dkv_in.at[slot_id], kvrecv.at[slot_id]).start()
 
         def turned(step):
-            return lax.rem(step + slot_id, TILES)
+            x = lax.rem(me // 8 + step + 1, 4)
+            return 2 * x + lax.rem(step // 4 + slot_id, 2)
 
         key_grads(turned(0))
 
@@ -562,8 +575,8 @@
             pltpu.VMEM((3, 8, TOK), f32),
             pltpu.VMEM((8, TOK), f32),
             pltpu.VMEM((3, 8, TOK), f32),
-            pltpu.VMEM((56 * TOK, 2 * HD), bf16),
-            pltpu.VMEM((56, HD, TOK), bf16),
+            pltpu.VMEM((TILES * TILE_BLOCKS * TOK, 2 * HD), bf16),
+            pltpu.VMEM((TILES * TILE_BLOCKS, HD, TOK), bf16),
             pltpu.VMEM((TILES, 2 * TOK, 2 * HD), bf16),
             pltpu.VMEM((TILE_BLOCKS, TOK, 2 * HD), f32),
             pltpu.VMEM((KINDS, TOK, TOK), f32),
@@ -571,7 +584,9 @@
             pltpu.VMEM((TILES, MOST_BLOCKS, TOK, TOK), f32),
             pltpu.VMEM((TILES, MOST_BLOCKS, TOK, 2 * TOK), bf16),
             pltpu.VMEM((TILES, MOST_BLOCKS, TOK, TOK), bf16),
-            pltpu.VMEM((TILES, 8, TOK), f32),
+            pltpu.VMEM((TILES, MOST_BLOCKS, 8, TOK), f32),
+            pltpu.VMEM((TILES, MOST_BLOCKS, 8, TOK), f32),
+            pltpu.VMEM((TILES, MOST_BLOCKS, 8, TOK), f32),
             pltpu.VMEM((FRAMES, BLK, HD), bf16),
             pltpu.VMEM((half, TOK, 2 * HD), bf16),
             pltpu.VMEM((half, TOK, 2 * HD), bf16),

time: 76.4 us -> 69.3 us (0.907)
  Pallas kernels: 75.2 us -> 68.2 us
    pallas_call x1, Pallas kernels: 72.8 us -> 65.9 us  [local(): pl.pallas_call(main_kernel, name='band_grads', out_shape=(shape((TOK, LOC...]
where the time goes in v5:
time: 69.3 us; the launch traced here: 68.9 us
  Pallas kernels  68.2 us (98%)
    pallas_call x1, Pallas kernels, local(): pl.pallas_call(main_kernel, name='band_grads', out_shape=(shape((TOK, LOC...  65.9 us
    pallas_call x1, Pallas kernels, local(): pl.pallas_call(finish_kernel, name='norm_grads', out_shape=(shape((TOK, L...  2.35 us

profile of v5, /device:TPU:0, one launch (start us, length us, event | category | flops | bytes accessed | tf_op | source)
XLA Modules:
  0.0 68.9 jit_solution(6746823689280735463)
XLA Ops:
  0.6 65.9 %band_grads.1 = (f32[128,640]{1,0:T(8,128)}, f32[128,640]{1,0:T(8,128)}, bf16[128,640]{1,0:T(8,128)(2,1)}, f32[8,128]{1,0:T(8,128)}, f32[8,128]{1,0:T(8,128)}) custom-call(s32[7]{0:T(128)} %offset_ref.1, bf16[128,640]{1,0:T(8,128)(2,1)} %q_ref.3, bf16[128,640]{1,0:T(8,128)(2,1)} %k_ref.3, bf16[128,640]{1,0:T(8,128)(2,1)} %v_ref.1, bf16[128,640]{1,0:T(8,128)(2,1)} %g_ref.1, ...), custom_call_target="tpu_custom_call" | custom-call | tf_op jit(solution)/shard_map/band_grads/pallas_call | solution.py:559
  66.5 2.4 %norm_grads.1 = (bf16[128,640]{1,0:T(8,128)(2,1)}, bf16[128,640]{1,0:T(8,128)(2,1)}, bf16[128,640]{1,0:T(8,128)(2,1)}) custom-call(bf16[128,640]{1,0:T(8,128)(2,1)} %q_ref.3, bf16[128,640]{1,0:T(8,128)(2,1)} %k_ref.3, f32[128,640]{1,0:T(8,128)} %get-tuple-element.8.qgrad, f32[128,640]{1,0:T(8,128)} %get-tuple-element.9.kgrad, ...), custom_call_target="tpu_custom_call" | custom-call | tf_op jit(solution)/shard_map/norm_grads/pallas_call | solution.py:607

commit v6 on v5

--- a/solution.py
+++ b/solution.py
@@ -151,9 +151,9 @@
     offset_ref, q_ref, k_ref, v_ref, g_ref, qgain_ref, kgain_ref,
     qgrad, kgrad, vgrad, total_ref, inner_ref,
     keys, queries, stat, slots, stat2, slots2,
-    kv, kt, w, acc, bias, tbuf, gbuf, grads, lows, peaks, totals, weighteds,
+    kv, kt, w, acc, bias, tbuf, gbuf, grads, peaks, totals, weighteds,
     dq_done, given, other, keep, mixed, dkv_in, dq_in,
-    zsend, zrecv, zsend2, zrecv2, vsend, gsend, ksend, qsend, vrecv, grecv, krecv, qrecv, vpass, kpass,
+    zsend, zrecv, zsend2, zrecv2, home_send, vrecv, krecv, qrecv, pass_send, pass_recv,
     give_send, give_recv, kvsend, dqsend, kvrecv, dqrecv,
 ):
     me, is_unit, my_head, block = my_unit()
@@ -186,43 +186,43 @@
     def g_at(frame):
         return w.at[frame // 4, frame_rows(4 + lax.rem(frame, 4), BLK), pl.ds(HD, HD)]
 
-    def remote(src, place, target, send_sem, recv_sem):
+    def remote(src, place, target, recv_sem):
         return pltpu.make_async_remote_copy(
-            src_ref=src, dst_ref=place(me), send_sem=send_sem, recv_sem=recv_sem.at[me],
+            src_ref=src, dst_ref=place(me), send_sem=home_send, recv_sem=recv_sem,
             device_id={"frame": target}, device_id_type=MESH,
         )
 
-    def send(src, place, target, send_sem, recv_sem):
+    def send(src, place, target, recv_sem):
         @pl.when(me != target)
         def _():
-            remote(src, place, target, send_sem, recv_sem).start()
+            remote(src, place, target, recv_sem).start()
 
         @pl.when(me == target)
         def _():
-            pltpu.make_async_copy(src, place(me), recv_sem.at[me]).start()
-
-    def key_part(slot, source, place, ssem, rsem):
-        return source(slot // 2), place, 2 * lax.rem(3 * slot, 16) + core, ssem.at[slot], rsem
-
-    def query_part(slot, side, source, place, ssem, rsem):
+            pltpu.make_async_copy(src, place(me), recv_sem).start()
+
+    def key_part(slot, source, place, rsem):
+        return source(slot // 2), place, 2 * lax.rem(3 * slot, 16) + core, rsem.at[me // 2]
+
+    def query_part(slot, side, source, place):
         rows = frame_rows(2 * lax.rem(slot, 2) + side, BLK)
-        return source(slot // 2, rows), place, 2 * lax.rem(3 * slot, 16) + side, ssem.at[2 * slot + side], rsem
+        return source(slot // 2, rows), place, 2 * lax.rem(3 * slot, 16) + side, qrecv
 
     def parts_v(slot):
-        return (key_part(slot, lambda head: v_ref.at[:, lanes(head)], v_at, vsend, vrecv),)
+        return (key_part(slot, lambda head: v_ref.at[:, lanes(head)], v_at, vrecv),)
 
     def parts_g(slot):
         return tuple(
-            query_part(slot, side, lambda head, rows: g_ref.at[rows, lanes(head)], g_at, gsend, grecv)
+            query_part(slot, side, lambda head, rows: g_ref.at[rows, lanes(head)], g_at)
             for side in range(2)
         )
 
     def parts_k(slot):
-        return (key_part(slot, lambda head: keys.at[head], k_at, ksend, krecv),)
+        return (key_part(slot, lambda head: keys.at[head], k_at, krecv),)
 
     def parts_q(slot):
         return tuple(
-            query_part(slot, side, lambda head, rows: queries.at[head, rows], q_at, qsend, qrecv)
+            query_part(slot, side, lambda head, rows: queries.at[head, rows], q_at)
             for side in range(2)
         )
 
@@ -254,32 +254,31 @@
     send_steps(0, 2 * LOCAL_HEADS, parts_k)
     send_steps(0, 2 * LOCAL_HEADS, parts_q)
 
-    def forward(place, step, send_sem, recv_sem):
-        frame = 2 * step + core
+    def forward(place, frame):
         return pltpu.make_async_remote_copy(
-            src_ref=place(frame), dst_ref=place(frame), send_sem=send_sem.at[step],
-            recv_sem=recv_sem.at[frame], device_id={"frame": partner}, device_id_type=MESH,
-        )
-
-    def arrived(place, frame, sem):
-        pltpu.make_async_copy(place(frame), place(frame), sem.at[frame]).wait()
+            src_ref=place(frame), dst_ref=place(frame), send_sem=pass_send, recv_sem=pass_recv,
+            device_id={"frame": partner}, device_id_type=MESH,
+        )
+
+    def await_bytes(ref, sem):
+        pltpu.make_async_copy(ref, ref, sem).wait()
 
     def give(pair):
         return pltpu.make_async_remote_copy(
-            src_ref=given.at[pair], dst_ref=other.at[pair], send_sem=give_send.at[pair],
+            src_ref=given.at[pair], dst_ref=other.at[pair], send_sem=give_send,
             recv_sem=give_recv.at[pair], device_id={"frame": partner}, device_id_type=MESH,
         )
 
     def send_dq(frame):
         return pltpu.make_async_remote_copy(
-            src_ref=dq_done.at[frame], dst_ref=dq_in.at[unit], send_sem=dqsend.at[frame],
-            recv_sem=dqrecv.at[unit], device_id={"frame": frame}, device_id_type=MESH,
+            src_ref=dq_done.at[frame], dst_ref=dq_in.at[unit], send_sem=dqsend,
+            recv_sem=dqrecv.at[my_head], device_id={"frame": frame}, device_id_type=MESH,
         )
 
     def send_dkv(pair):
         return pltpu.make_async_remote_copy(
-            src_ref=mixed.at[pair], dst_ref=dkv_in.at[slot_id], send_sem=kvsend.at[pair],
-            recv_sem=kvrecv.at[slot_id], device_id={"frame": 2 * pair + core}, device_id_type=MESH,
+            src_ref=mixed.at[pair], dst_ref=dkv_in.at[slot_id], send_sem=kvsend,
+            recv_sem=kvrecv.at[my_head], device_id={"frame": 2 * pair + core}, device_id_type=MESH,
         )
 
     @pl.when(is_unit)
@@ -317,14 +316,18 @@
             def _():
                 body(place - place // 5)
 
-        def pass_values(tile):
-            for part in range(2):
-                arrived(v_at, 4 * tile + 2 * part + core, vrecv)
-                forward(v_at, 2 * tile + part, vpass, vrecv).start()
+        def passing(place, sem):
+            def body(tile):
+                for part in range(2):
+                    frame = 4 * tile + 2 * part + core
+                    await_bytes(place(frame), sem.at[frame // 2])
+                    forward(place, frame).start()
+
+            return body
 
         @pl.loop(0, 10)
         def _(step):
-            at_step(step, pass_values)
+            at_step(step, passing(v_at, vrecv))
 
         def chosen(level, after):
             pick = (block + offset_ref[level - 1] + after) & 3
@@ -333,16 +336,7 @@
         moves = [(4 + index, part, part, chosen(2 + index, 0)) for index in range(3) for part in range(4)]
         moves += [(7, 2 * part + after, 1 + part, chosen(1, after)) for part in range(2) for after in range(2)]
 
-        def pass_keys(tile):
-            for part in range(2):
-                arrived(k_at, 4 * tile + 2 * part + core, krecv)
-                forward(k_at, 2 * tile + part, kpass, krecv).start()
-
         def score(tile):
-            for part in range(2):
-                frame = 4 * tile + 2 * part + 1 - core
-                arrived(v_at, frame, vrecv)
-                arrived(k_at, frame, krecv)
             base = TILE_BLOCKS * tile
             for to, place, frame, weights in moves:
                 picked = kv[frame_rows(NB * (base + frame), BLK), :] * weights[0].astype(jnp.bfloat16)
@@ -371,19 +365,22 @@
 
         @pl.loop(0, 10)
         def _(step):
-            at_step(step, pass_keys)
-
-        @pl.loop(0, FRAMES)
-        def _(frame):
-            arrived(g_at, frame, grecv)
-            arrived(q_at, frame, qrecv)
+            at_step(step, passing(k_at, krecv))
+
+        await_bytes(w.at[pl.ds(0, TILES // 2)], qrecv)
+        await_bytes(kv.at[pl.ds(0, FRAMES * TOK // 2)], pass_recv)
 
         @pl.loop(0, 10)
         def _(step):
             at_step(step, score)
 
+        def turned(step):
+            x = lax.rem(me // 8 + step + 1, 4)
+            return 2 * x + lax.rem(step // 4 + slot_id, 2)
+
         @pl.loop(0, TILES)
-        def _(tile):
+        def _(step):
+            tile = turned(step)
             peak = jnp.max(jnp.max(peaks[tile], axis=0), axis=0, keepdims=True)
             factor = jnp.exp2(peaks[tile] - peak)
             total = jnp.sum(jnp.sum(totals[tile] * factor, axis=0), axis=0, keepdims=True)
@@ -391,13 +388,34 @@
             inverse = 1.0 / total
             delta = weighted * inverse
             factor = factor * inverse
-            for slot in range(MOST_BLOCKS):
-                probs = (tbuf[tile, slot].reshape(16, 8, TOK) * factor[slot]).reshape(TOK, TOK)
-                grad = probs * (gbuf[tile, slot] - delta)
-                high = grad.astype(jnp.bfloat16)
-                grads[tile, slot, :, 0:TOK] = high
-                grads[tile, slot, :, TOK:] = probs.astype(jnp.bfloat16)
-                lows[tile, slot] = (grad - high.astype(jnp.float32)).astype(jnp.bfloat16)
+            total = jnp.zeros((HD, 2 * TOK), jnp.float32)
+            for apart in range(TILES):
+                base = TILE_BLOCKS * lax.rem(tile + apart, TILES)
+                found = blocks_between(apart, wrapped(tile, apart))
+                right = []
+                for slot, _, _ in found:
+                    probs = (tbuf[tile, slot].reshape(16, 8, TOK) * factor[slot]).reshape(TOK, TOK)
+                    grad = probs * (gbuf[tile, slot] - delta)
+                    high = grad.astype(jnp.bfloat16)
+                    grads[tile, slot, :, 0:TOK] = high
+                    grads[tile, slot, :, TOK:] = probs.astype(jnp.bfloat16)
+                    low = (grad - high.astype(jnp.float32)).astype(jnp.bfloat16)
+                    right.append(jnp.concatenate([high, low], axis=1))
+                keyt = jnp.concatenate([kt[base + blk] for _, blk, _ in found], axis=1)
+                total = total + dot(keyt, jnp.concatenate(right, axis=0), ((1,), (0,)))
+            dq = (total[:, 0:TOK] + total[:, TOK:]).T.astype(jnp.bfloat16)
+            for part in range(4):
+                dq_done[4 * tile + part] = dq[part * BLK : (part + 1) * BLK]
+            for part in range(4):
+                frame = 4 * tile + part
+
+                @pl.when(frame != me)
+                def _():
+                    send_dq(frame).start()
+
+                @pl.when(frame == me)
+                def _():
+                    pltpu.make_async_copy(dq_done.at[frame], dq_in.at[unit], dqrecv.at[my_head]).start()
 
         def key_grads(tile):
             for index in range(4, TILE_BLOCKS):
@@ -426,33 +444,6 @@
                 give(pair).start()
                 keep[pair] = acc[2 * part + core]
 
-        def query_grads(tile):
-            total = jnp.zeros((HD, 2 * TOK), jnp.float32)
-            for apart in range(TILES):
-                base = TILE_BLOCKS * lax.rem(tile + apart, TILES)
-                found = blocks_between(apart, wrapped(tile, apart))
-                keyt = jnp.concatenate([kt[base + blk] for _, blk, _ in found], axis=1)
-                right = jnp.concatenate(
-                    [
-                        jnp.concatenate([grads[tile, slot, :, 0:TOK], lows[tile, slot]], axis=1)
-                        for slot, _, _ in found
-                    ],
-                    axis=0,
-                )
-                total = total + dot(keyt, right, ((1,), (0,)))
-            dq = (total[:, 0:TOK] + total[:, TOK:]).T.astype(jnp.bfloat16)
-            for part in range(4):
-                frame = 4 * tile + part
-                dq_done[frame] = dq[part * BLK : (part + 1) * BLK]
-
-                @pl.when(frame != me)
-                def _():
-                    send_dq(frame).start()
-
-                @pl.when(frame == me)
-                def _():
-                    pltpu.make_async_copy(dq_done.at[frame], dq_in.at[unit], dqrecv.at[unit]).start()
-
         def mix(tile):
             for part in range(2):
                 pair = 2 * tile + part
@@ -465,11 +456,7 @@
 
                 @pl.when(2 * pair + core == me)
                 def _():
-                    pltpu.make_async_copy(mixed.at[pair], dkv_in.at[slot_id], kvrecv.at[slot_id]).start()
-
-        def turned(step):
-            x = lax.rem(me // 8 + step + 1, 4)
-            return 2 * x + lax.rem(step // 4 + slot_id, 2)
+                    pltpu.make_async_copy(mixed.at[pair], dkv_in.at[slot_id], kvrecv.at[my_head]).start()
 
         key_grads(turned(0))
 
@@ -477,24 +464,19 @@
         def _(step):
             key_grads(turned(step))
             mix(turned(step - 1))
-            query_grads(turned(step - 1))
 
         mix(turned(TILES - 1))
-        query_grads(turned(TILES - 1))
 
     qinner = jnp.zeros((TOK, HD), jnp.float32)
     kinner = jnp.zeros((TOK, HD), jnp.float32)
     for h in range(LOCAL_HEADS):
-        for b in range(NB):
-            u = h * NB + b
-            pltpu.make_async_copy(dq_in.at[u], dq_in.at[u], dqrecv.at[u]).wait()
+        await_bytes(dq_in.at[pl.ds(h * NB, NB)], dqrecv.at[h])
         dq = dq_in[pl.ds(h * NB, NB)].astype(jnp.float32).reshape(TOK, HD)
         gained = qgain_ref[head_slice(h)].reshape(1, HD) * (dq * SCALE)
         qgrad[:, head_slice(h)] = gained
         qinner = qinner + gained * q_ref[:, head_slice(h)].astype(jnp.float32)
     for h in range(LOCAL_HEADS):
-        for u in (2 * h, 2 * h + 1):
-            pltpu.make_async_copy(dkv_in.at[u], dkv_in.at[u], kvrecv.at[u]).wait()
+        await_bytes(dkv_in.at[pl.ds(2 * h, 2)], kvrecv.at[h])
         both = dkv_in[2 * h].astype(jnp.float32) + dkv_in[2 * h + 1].astype(jnp.float32)
         vgrad[:, head_slice(h)] = both[:, HD:].astype(jnp.bfloat16)
         gained = kgain_ref[head_slice(h)].reshape(1, HD) * (both[:, 0:HD] * SCALE)
@@ -507,31 +489,20 @@
         copy.wait()
     inner_ref[...] = stat2[...] + slots2[0] + slots2[1] + slots2[2]
 
-    @pl.loop(0, 2 * LOCAL_HEADS)
-    def _(slot):
-        for parts in (parts_v(slot), parts_g(slot), parts_k(slot), parts_q(slot)):
-            for src, place, target, ssem, rsem in parts:
-                @pl.when(me != target)
-                def _():
-                    remote(src, place, target, ssem, rsem).wait_send()
+    sent = 2 * (2 * LOCAL_HEADS) * TOK + 2 * UNITS * BLK
+    kept = 2 * TOK + 2 * BLK
+
+    @pl.when(jnp.logical_not(is_unit))
+    def _():
+        await_bytes(kv.at[pl.ds(0, sent // 2)], home_send)
 
     @pl.when(is_unit)
     def _():
-        @pl.loop(0, FRAMES)
-        def _(frame):
-            @pl.when(frame != me)
-            def _():
-                send_dq(frame).wait_send()
-
-        @pl.loop(0, FRAMES // 2)
-        def _(pair):
-            forward(v_at, pair, vpass, vrecv).wait_send()
-            forward(k_at, pair, kpass, krecv).wait_send()
-            give(pair).wait_send()
-
-            @pl.when(2 * pair + core != me)
-            def _():
-                send_dkv(pair).wait_send()
+        await_bytes(kv.at[pl.ds(0, (sent - kept) // 2)], home_send)
+        await_bytes(kv.at[pl.ds(0, FRAMES * TOK // 2)], pass_send)
+        await_bytes(dq_done.at[pl.ds(0, FRAMES - 1)], dqsend)
+        await_bytes(given, give_send)
+        await_bytes(mixed.at[pl.ds(0, FRAMES // 2 - 1)], kvsend)
 
 
 def finish_kernel(q_ref, k_ref, qgrad, kgrad, vgrad, total_ref, inner_ref, dq_out, dk_out, dv_out):
@@ -583,7 +554,6 @@
             pltpu.VMEM((TILES, MOST_BLOCKS, TOK, TOK), f32),
             pltpu.VMEM((TILES, MOST_BLOCKS, TOK, TOK), f32),
             pltpu.VMEM((TILES, MOST_BLOCKS, TOK, 2 * TOK), bf16),
-            pltpu.VMEM((TILES, MOST_BLOCKS, TOK, TOK), bf16),
             pltpu.VMEM((TILES, MOST_BLOCKS, 8, TOK), f32),
             pltpu.VMEM((TILES, MOST_BLOCKS, 8, TOK), f32),
             pltpu.VMEM((TILES, MOST_BLOCKS, 8, TOK), f32),
@@ -595,10 +565,9 @@
             pltpu.VMEM((UNITS // 2, TOK, 2 * HD), bf16),
             pltpu.VMEM((UNITS, BLK, HD), bf16),
             dma((3,)), dma((3,)), dma((3,)), dma((3,)),
-            dma((UNITS // 2,)), dma((UNITS,)), dma((UNITS // 2,)), dma((UNITS,)),
-            dma((FRAMES,)), dma((FRAMES,)), dma((FRAMES,)), dma((FRAMES,)),
-            dma((half,)), dma((half,)), dma((half,)), dma((half,)),
-            dma((half,)), dma((FRAMES,)), dma((UNITS // 2,)), dma((UNITS,)),
+            dma, dma((half,)), dma((half,)), dma, dma, dma,
+            dma, dma((half,)),
+            dma, dma, dma((LOCAL_HEADS,)), dma((LOCAL_HEADS,)),
         ],
         compiler_params=pltpu.CompilerParams(
             collective_id=0, has_side_effects=True, vmem_limit_bytes=VMEM_LIMIT

time: 69.3 us -> 65.5 us (0.945)
  Pallas kernels: 68.2 us -> 64.5 us
    pallas_call x1, Pallas kernels: 65.9 us -> 62.2 us  [local(): pl.pallas_call(main_kernel, name='band_grads', out_shape=(shape((TOK, LOC...]
where the time goes in v6:
time: 65.5 us; the launch traced here: 65.2 us
  Pallas kernels  64.5 us (98%)
    pallas_call x1, Pallas kernels, local(): pl.pallas_call(main_kernel, name='band_grads', out_shape=(shape((TOK, LOC...  62.2 us
    pallas_call x1, Pallas kernels, local(): pl.pallas_call(finish_kernel, name='norm_grads', out_shape=(shape((TOK, L...  2.35 us

profile of v6, /device:TPU:0, one launch (start us, length us, event | category | flops | bytes accessed | tf_op | source)
XLA Modules:
  0.0 65.2 jit_solution(17121120427897348100)
XLA Ops:
  0.6 62.2 %band_grads.1 = (f32[128,640]{1,0:T(8,128)}, f32[128,640]{1,0:T(8,128)}, bf16[128,640]{1,0:T(8,128)(2,1)}, f32[8,128]{1,0:T(8,128)}, f32[8,128]{1,0:T(8,128)}) custom-call(s32[7]{0:T(128)} %offset_ref.1, bf16[128,640]{1,0:T(8,128)(2,1)} %q_ref.3, bf16[128,640]{1,0:T(8,128)(2,1)} %k_ref.3, bf16[128,640]{1,0:T(8,128)(2,1)} %v_ref.1, bf16[128,640]{1,0:T(8,128)(2,1)} %g_ref.1, ...), custom_call_target="tpu_custom_call" | custom-call | tf_op jit(solution)/shard_map/band_grads/pallas_call | solution.py:530
  62.8 2.4 %norm_grads.1 = (bf16[128,640]{1,0:T(8,128)(2,1)}, bf16[128,640]{1,0:T(8,128)(2,1)}, bf16[128,640]{1,0:T(8,128)(2,1)}) custom-call(bf16[128,640]{1,0:T(8,128)(2,1)} %q_ref.3, bf16[128,640]{1,0:T(8,128)(2,1)} %k_ref.3, f32[128,640]{1,0:T(8,128)} %get-tuple-element.8.qgrad, f32[128,640]{1,0:T(8,128)} %get-tuple-element.9.kgrad, ...), custom_call_target="tpu_custom_call" | custom-call | tf_op jit(solution)/shard_map/norm_grads/pallas_call | solution.py:576

commit v7 on v6

--- a/solution.py
+++ b/solution.py
@@ -148,10 +148,10 @@
 
 
 def main_kernel(
-    offset_ref, q_ref, k_ref, v_ref, g_ref, qgain_ref, kgain_ref,
+    offset_ref, q_hbm, k_hbm, v_hbm, g_hbm, qgain_ref, kgain_ref,
     qgrad, kgrad, vgrad, total_ref, inner_ref,
-    keys, queries, stat, slots, stat2, slots2,
-    kv, kt, w, acc, bias, tbuf, gbuf, grads, peaks, totals, weighteds,
+    q_ref, k_ref, v_ref, g_ref, load_sem, keys, queries, stat, slots, stat2, slots2,
+    kv, kt, picks, w, acc, bias, tbuf, gbuf, grads, peaks, totals, weighteds,
     dq_done, given, other, keep, mixed, dkv_in, dq_in,
     zsend, zrecv, zsend2, zrecv2, home_send, vrecv, krecv, qrecv, pass_send, pass_recv,
     give_send, give_recv, kvsend, dqsend, kvrecv, dqrecv,
@@ -169,7 +169,15 @@
             sums = sums + part * part
         return jnp.sum(sums, axis=1, keepdims=True)
 
+    loads = [
+        pltpu.make_async_copy(src, dst, load_sem.at[index])
+        for index, (src, dst) in enumerate(((q_hbm, q_ref), (k_hbm, k_ref), (v_hbm, v_ref), (g_hbm, g_ref)))
+    ]
+    for load in loads:
+        load.start()
     greet()
+    for load in loads:
+        load.wait()
     stat[...] = pair_rows(squares(q_ref), squares(k_ref))
     all_here()
     sums = head_sum(stat, slots, zsend, zrecv)
@@ -338,18 +346,34 @@
 
         def score(tile):
             base = TILE_BLOCKS * tile
+            for part in range(4):
+                kt[base + part] = kv[frame_rows(base + part), 0:HD].T
             for to, place, frame, weights in moves:
                 picked = kv[frame_rows(NB * (base + frame), BLK), :] * weights[0].astype(jnp.bfloat16)
                 for which in range(1, NB):
                     rows = frame_rows(NB * (base + frame) + which, BLK)
                     picked = picked + kv[rows, :] * weights[which].astype(jnp.bfloat16)
-                kv[frame_rows(NB * (base + to) + place, BLK), :] = picked
-            for part in range(TILE_BLOCKS):
-                kt[base + part] = kv[frame_rows(base + part), 0:HD].T
+                picks[to - 4, place * BLK : (place + 1) * BLK] = picked
+            picks[4] = kv[frame_rows(base), :]
+            picks[5] = kv[frame_rows(base + 3), :]
+            for part in range(4, TILE_BLOCKS):
+                kt[base + part] = picks[part - 4, :, 0:HD].T
+
+            def operand(apart, over, index, blk):
+                if apart == 0:
+                    return kv[frame_rows(base + blk), :]
+                if apart in (1, 7) and index == 0:
+                    end = 4 if apart == 1 else 5
+                    return picks[end + over * (2 - end)]
+                return picks[blk - 4]
+
             for apart in range(TILES):
                 asker = lax.rem(tile + TILES - apart, TILES)
-                found = blocks_between(apart, wrapped(asker, apart))
-                rows = jnp.concatenate([kv[frame_rows(base + blk), :] for _, blk, _ in found], axis=0)
+                over = wrapped(asker, apart)
+                found = blocks_between(apart, over)
+                rows = jnp.concatenate(
+                    [operand(apart, over, index, blk) for index, (_, blk, _) in enumerate(found)], axis=0
+                )
                 both = dot(rows, w[asker], ((1,), (1,)))
                 for index, (slot, _, kind) in enumerate(found):
                     part = both[index * TOK : (index + 1) * TOK]
@@ -537,9 +561,14 @@
             shape((8, TOK), f32),
             shape((8, TOK), f32),
         ),
-        in_specs=[smem] + [vmem] * 6,
+        in_specs=[smem] + [pl.BlockSpec(memory_space=pl.ANY)] * 4 + [vmem] * 2,
         out_specs=[vmem] * 5,
         scratch_shapes=[
+            pltpu.VMEM((TOK, LOCAL), bf16),
+            pltpu.VMEM((TOK, LOCAL), bf16),
+            pltpu.VMEM((TOK, LOCAL), bf16),
+            pltpu.VMEM((TOK, LOCAL), bf16),
+            dma((4,)),
             pltpu.VMEM((LOCAL_HEADS, TOK, HD), bf16),
             pltpu.VMEM((LOCAL_HEADS, TOK, HD), bf16),
             pltpu.VMEM((8, TOK), f32),
@@ -548,6 +577,7 @@
             pltpu.VMEM((3, 8, TOK), f32),
             pltpu.VMEM((TILES * TILE_BLOCKS * TOK, 2 * HD), bf16),
             pltpu.VMEM((TILES * TILE_BLOCKS, HD, TOK), bf16),
+            pltpu.VMEM((6, TOK, 2 * HD), bf16),
             pltpu.VMEM((TILES, 2 * TOK, 2 * HD), bf16),
             pltpu.VMEM((TILE_BLOCKS, TOK, 2 * HD), f32),
             pltpu.VMEM((KINDS, TOK, TOK), f32),

time: 65.5 us -> 64.6 us (0.986)
  Pallas kernels: 64.5 us -> 63.5 us
    pallas_call x1, Pallas kernels: 62.2 us -> 61.2 us  [local(): pl.pallas_call(main_kernel, name='band_grads', out_shape=(shape((TOK, LOC...]
where the time goes in v7:
time: 64.6 us; the launch traced here: 64.2 us
  Pallas kernels  63.5 us (98%)
    pallas_call x1, Pallas kernels, local(): pl.pallas_call(main_kernel, name='band_grads', out_shape=(shape((TOK, LOC...  61.2 us
    pallas_call x1, Pallas kernels, local(): pl.pallas_call(finish_kernel, name='norm_grads', out_shape=(shape((TOK, L...  2.35 us

profile of v7, /device:TPU:0, one launch (start us, length us, event | category | flops | bytes accessed | tf_op | source)
XLA Modules:
  0.0 64.2 jit_solution(8090913977265465459)
XLA Ops:
  0.6 61.2 %band_grads.1 = (f32[128,640]{1,0:T(8,128)}, f32[128,640]{1,0:T(8,128)}, bf16[128,640]{1,0:T(8,128)(2,1)}, f32[8,128]{1,0:T(8,128)}, f32[8,128]{1,0:T(8,128)}) custom-call(s32[7]{0:T(128)} %offset_ref.1, bf16[128,640]{1,0:T(8,128)(2,1)} %q_ref.1, bf16[128,640]{1,0:T(8,128)(2,1)} %k_ref.1, bf16[128,640]{1,0:T(8,128)(2,1)} %v_hbm.1, bf16[128,640]{1,0:T(8,128)(2,1)} %g_hbm.1, ...), custom_call_target="tpu_custom_call" | custom-call | tf_op jit(solution)/shard_map/band_grads/pallas_call | solution.py:554
  61.8 2.4 %norm_grads.1 = (bf16[128,640]{1,0:T(8,128)(2,1)}, bf16[128,640]{1,0:T(8,128)(2,1)}, bf16[128,640]{1,0:T(8,128)(2,1)}) custom-call(bf16[128,640]{1,0:T(8,128)(2,1)} %q_ref.1, bf16[128,640]{1,0:T(8,128)(2,1)} %k_ref.1, f32[128,640]{1,0:T(8,128)} %get-tuple-element.8.qgrad, f32[128,640]{1,0:T(8,128)} %get-tuple-element.9.kgrad, ...), custom_call_target="tpu_custom_call" | custom-call | tf_op jit(solution)/shard_map/norm_grads/pallas_call | solution.py:606

commit v8 on v7

--- a/solution.py
+++ b/solution.py
@@ -30,7 +30,7 @@
 
 def my_unit():
     me = lax.axis_index("frame")
-    slot = lax.rem(11 * (me // 2), 16)
+    slot = me // 2
     return me, slot < 2 * LOCAL_HEADS, slot // 2, 2 * lax.rem(slot, 2) + lax.rem(me, 2)
 
 
@@ -87,7 +87,7 @@
     row = lax.axis_index("head")
     for step in range(1, FRAMES):
         pl.semaphore_signal(
-            barrier, inc=1, device_id={"frame": lax.rem(me + step, FRAMES)}, device_id_type=MESH
+            barrier, inc=1, device_id={"frame": (me + step) & (FRAMES - 1)}, device_id_type=MESH
         )
     for step in range(1, 4):
         pl.semaphore_signal(
@@ -149,8 +149,8 @@
 
 def main_kernel(
     offset_ref, q_hbm, k_hbm, v_hbm, g_hbm, qgain_ref, kgain_ref,
-    qgrad, kgrad, vgrad, total_ref, inner_ref,
-    q_ref, k_ref, v_ref, g_ref, load_sem, keys, queries, stat, slots, stat2, slots2,
+    qgrad_out, kgrad_out, vgrad_out, total_ref, inner_ref,
+    qgrad, kgrad, vgrad, store_sem, q_ref, k_ref, v_ref, g_ref, load_sem, keys, queries, stat, slots, stat2, slots2,
     kv, kt, picks, w, acc, bias, tbuf, gbuf, grads, peaks, totals, weighteds,
     dq_done, given, other, keep, mixed, dkv_in, dq_in,
     zsend, zrecv, zsend2, zrecv2, home_send, vrecv, krecv, qrecv, pass_send, pass_recv,
@@ -210,11 +210,11 @@
             pltpu.make_async_copy(src, place(me), recv_sem).start()
 
     def key_part(slot, source, place, rsem):
-        return source(slot // 2), place, 2 * lax.rem(3 * slot, 16) + core, rsem.at[me // 2]
+        return source(slot // 2), place, 2 * slot + core, rsem.at[me // 2]
 
     def query_part(slot, side, source, place):
         rows = frame_rows(2 * lax.rem(slot, 2) + side, BLK)
-        return source(slot // 2, rows), place, 2 * lax.rem(3 * slot, 16) + side, qrecv
+        return source(slot // 2, rows), place, 2 * slot + side, qrecv
 
     def parts_v(slot):
         return (key_part(slot, lambda head: v_ref.at[:, lanes(head)], v_at, vrecv),)
@@ -506,12 +506,22 @@
         gained = kgain_ref[head_slice(h)].reshape(1, HD) * (both[:, 0:HD] * SCALE)
         kgrad[:, head_slice(h)] = gained
         kinner = kinner + gained * k_ref[:, head_slice(h)].astype(jnp.float32)
+    stores = [
+        pltpu.make_async_copy(src, dst, store_sem.at[index])
+        for index, (src, dst) in enumerate(((qgrad, qgrad_out), (kgrad, kgrad_out), (vgrad, vgrad_out)))
+    ]
     stat2[...] = pair_rows(
         jnp.sum(qinner, axis=1, keepdims=True), jnp.sum(kinner, axis=1, keepdims=True)
     )
-    for copy in head_sum(stat2, slots2, zsend2, zrecv2):
+    sums = head_sum(stat2, slots2, zsend2, zrecv2)
+    for store in stores:
+        store.start()
+    for copy in sums:
         copy.wait()
     inner_ref[...] = stat2[...] + slots2[0] + slots2[1] + slots2[2]
+
+    for store in stores:
+        store.wait()
 
     sent = 2 * (2 * LOCAL_HEADS) * TOK + 2 * UNITS * BLK
     kept = 2 * TOK + 2 * BLK
@@ -562,8 +572,12 @@
             shape((8, TOK), f32),
         ),
         in_specs=[smem] + [pl.BlockSpec(memory_space=pl.ANY)] * 4 + [vmem] * 2,
-        out_specs=[vmem] * 5,
+        out_specs=[pl.BlockSpec(memory_space=pl.ANY)] * 3 + [vmem] * 2,
         scratch_shapes=[
+            pltpu.VMEM((TOK, LOCAL), f32),
+            pltpu.VMEM((TOK, LOCAL), f32),
+            pltpu.VMEM((TOK, LOCAL), bf16),
+            dma((3,)),
             pltpu.VMEM((TOK, LOCAL), bf16),
             pltpu.VMEM((TOK, LOCAL), bf16),
             pltpu.VMEM((TOK, LOCAL), bf16),

time: 64.6 us -> 64 us (level)
  no operation moved by 1% of the time
where the time goes in v8:
time: 64 us; the launch traced here: 63.8 us
  Pallas kernels  63.2 us (99%)
  between operations  0.64 us (1%)
    pallas_call x1, Pallas kernels, local(): pl.pallas_call(main_kernel, name='band_grads', out_shape=(shape((TOK, LOC...  60.8 us
    pallas_call x1, Pallas kernels, local(): pl.pallas_call(finish_kernel, name='norm_grads', out_shape=(shape((TOK, L...  2.35 us

profile of v8, /device:TPU:0, one launch (start us, length us, event | category | flops | bytes accessed | tf_op | source)
XLA Modules:
  0.0 63.8 jit_solution(9079154068345511445)
XLA Ops:
  0.6 60.8 %band_grads.1 = (f32[128,640]{1,0:T(8,128)}, f32[128,640]{1,0:T(8,128)}, bf16[128,640]{1,0:T(8,128)(2,1)}, f32[8,128]{1,0:T(8,128)}, f32[8,128]{1,0:T(8,128)}) custom-call(s32[7]{0:T(128)} %offset_ref.1, bf16[128,640]{1,0:T(8,128)(2,1)} %q_ref.1, bf16[128,640]{1,0:T(8,128)(2,1)} %k_ref.1, bf16[128,640]{1,0:T(8,128)(2,1)} %v_hbm.1, bf16[128,640]{1,0:T(8,128)(2,1)} %g_hbm.1, ...), custom_call_target="tpu_custom_call" | custom-call | tf_op jit(solution)/shard_map/band_grads/pallas_call | solution.py:564
  61.4 2.4 %norm_grads.1 = (bf16[128,640]{1,0:T(8,128)(2,1)}, bf16[128,640]{1,0:T(8,128)(2,1)}, bf16[128,640]{1,0:T(8,128)(2,1)}) custom-call(bf16[128,640]{1,0:T(8,128)(2,1)} %q_ref.1, bf16[128,640]{1,0:T(8,128)(2,1)} %k_ref.1, f32[128,640]{1,0:T(8,128)} %get-tuple-element.8.qgrad, f32[128,640]{1,0:T(8,128)} %get-tuple-element.9.kgrad, ...), custom_call_target="tpu_custom_call" | custom-call | tf_op jit(solution)/shard_map/norm_grads/pallas_call | solution.py:620

commit v9 on v8

--- a/solution.py
+++ b/solution.py
@@ -176,11 +176,13 @@
     for load in loads:
         load.start()
     greet()
-    for load in loads:
+    for load in loads[:2]:
         load.wait()
     stat[...] = pair_rows(squares(q_ref), squares(k_ref))
     all_here()
     sums = head_sum(stat, slots, zsend, zrecv)
+    for load in loads[2:]:
+        load.wait()
 
     def k_at(frame):
         return kv.at[frame_rows(frame_block(frame)), pl.ds(0, HD)]

time: 64 us -> 64 us (level)
  no operation moved by 1% of the time
where the time goes in v9:
time: 64 us; the launch traced here: 63.8 us
  Pallas kernels  63.2 us (99%)
  between operations  0.64 us (1%)
    pallas_call x1, Pallas kernels, local(): pl.pallas_call(main_kernel, name='band_grads', out_shape=(shape((TOK, LOC...  60.8 us
    pallas_call x1, Pallas kernels, local(): pl.pallas_call(finish_kernel, name='norm_grads', out_shape=(shape((TOK, L...  2.35 us

profile of v9, /device:TPU:0, one launch (start us, length us, event | category | flops | bytes accessed | tf_op | source)
XLA Modules:
  0.0 63.8 jit_solution(308666410895301019)
XLA Ops:
  0.6 60.8 %band_grads.1 = (f32[128,640]{1,0:T(8,128)}, f32[128,640]{1,0:T(8,128)}, bf16[128,640]{1,0:T(8,128)(2,1)}, f32[8,128]{1,0:T(8,128)}, f32[8,128]{1,0:T(8,128)}) custom-call(s32[7]{0:T(128)} %offset_ref.1, bf16[128,640]{1,0:T(8,128)(2,1)} %q_ref.1, bf16[128,640]{1,0:T(8,128)(2,1)} %k_ref.1, bf16[128,640]{1,0:T(8,128)(2,1)} %v_hbm.1, bf16[128,640]{1,0:T(8,128)(2,1)} %g_hbm.1, ...), custom_call_target="tpu_custom_call" | custom-call | tf_op jit(solution)/shard_map/band_grads/pallas_call | solution.py:566
  61.4 2.4 %norm_grads.1 = (bf16[128,640]{1,0:T(8,128)(2,1)}, bf16[128,640]{1,0:T(8,128)(2,1)}, bf16[128,640]{1,0:T(8,128)(2,1)}) custom-call(bf16[128,640]{1,0:T(8,128)(2,1)} %q_ref.1, bf16[128,640]{1,0:T(8,128)(2,1)} %k_ref.1, f32[128,640]{1,0:T(8,128)} %get-tuple-element.8.qgrad, f32[128,640]{1,0:T(8,128)} %get-tuple-element.9.kgrad, ...), custom_call_target="tpu_custom_call" | custom-call | tf_op jit(solution)/shard_map/norm_grads/pallas_call | solution.py:622
